TPU v7x, 512 devices: a whole 4x4x16 slice. The times are simulated.
512 devices in a mesh: ctx: 16 (over x, y), ep: 32 (over z, core).
Axes of the slice: x: 4, y: 4, z: 16, core: 2. Of those that a mesh axis runs over, the one named last changes fastest.
Arguments:
- queries: bfloat16 [32, 2048, 4096], P('ep', 'ctx'), may hold values from -7 to 7
- keys: bfloat16 [32, 2048, 256], P('ep', 'ctx'), may hold values from -4.5 to 4.5
- values: bfloat16 [32, 2048, 256], P('ep', 'ctx'), may hold values from -5 to 5
- hidden: bfloat16 [32, 2048, 2048], P('ep', 'ctx'), may hold values from -130 to 130
- expert_ids: int32 [32, 2048, 2], P('ep', 'ctx'), may hold values from 0 to 31, all different within a row; in each aligned block of 128 rows (0 to 127, 128 to 255, ..., all dimensions but the last counted through in order) at most 12 rows name the same one
- gate_probs: float32 [32, 2048, 2], P('ep', 'ctx'), may hold values from 0.2 to 1
- norm_gain: float32 [2048], replicated, may hold values from 0.1 to 1.9
- w_gate: bfloat16 [32, 768, 2048], P('ep', 'ctx'), may hold values from -0.125 to 0.125
- w_up: bfloat16 [32, 768, 2048], P('ep', 'ctx'), may hold values from -0.125 to 0.125
- w_down: bfloat16 [32, 768, 2048], P('ep', 'ctx'), may hold values from -0.21875 to 0.21875
Outputs:
- attended: bfloat16 [32, 2048, 4096], P('ep', 'ctx')
- expert_mix: bfloat16 [32, 2048, 2048], P('ep', 'ctx')
Inputs may be any that keep to these rules, and one draw needn't show every extreme that they name: `expert_ids`: the 2 experts of one token differ. Among the 128 tokens of one device no expert is named more than 12 times.
All inputs are finite; a program needn't handle non-finite values.
Results may differ from a plain program's by a relative error of at most 0.0071.
Values may be sent and summed in bfloat16 or wider, within the bound.
No kernel may reach another device: no remote copies, remote signals or barrier semaphores. Data moves between devices by JAX's collectives and lax.ppermute only.
A program may use at most 128 MiB of HBM per device.

v0:
```python
import math

import jax
import jax.numpy as jnp
from jax import lax
from jax.sharding import PartitionSpec as P

HQ = 32
KVH = 2
DH = 128


def attend(queries, keys, values):
    row_count = queries.shape[1]
    head_ratio = HQ // KVH
    score_factor = 1.0 / math.sqrt(DH)
    my_index = lax.axis_index("ctx")
    query_heads = queries[0].reshape(row_count, KVH, head_ratio, DH)
    groups = [(query_heads, my_index * row_count + jnp.arange(row_count, dtype=jnp.int32))]
    initial = tuple(
        (
            (
                jnp.full((KVH, head_ratio, group_rows.shape[0]), -1e30, jnp.float32),
                jnp.zeros((KVH, head_ratio, group_rows.shape[0]), jnp.float32),
                jnp.zeros((KVH, head_ratio, group_rows.shape[0], DH), jnp.float32),
            )
            for group_rows, group_pos in groups
        )
    )

    def update(carried, pieces_in, offset):
        key_piece, value_piece = pieces_in
        piece_rows = key_piece.shape[0]
        key_heads = key_piece.reshape(piece_rows, KVH, DH)
        value_heads = value_piece.reshape(piece_rows, KVH, DH)
        key_pos = jnp.arange(piece_rows, dtype=jnp.int32)
        updated = []
        for (group_rows, query_pos), current in zip(groups, carried):

            def compute(present, group_rows=group_rows, query_pos=query_pos):
                maxima, totals, weighted = present
                scores = (
                    jnp.einsum(
                        "rgjd,ngd->gjrn", group_rows, key_heads, preferred_element_type=jnp.float32
                    )
                    * score_factor
                )
                visible = key_pos[None, :] <= query_pos[:, None]
                scores = jnp.where(visible, scores, -jnp.inf)
                new_maxima = jnp.maximum(maxima, jnp.max(scores, axis=-1))
                exponent = jnp.exp(scores - new_maxima[..., None])
                new_totals = jnp.sum(exponent, axis=-1)
                product = jnp.einsum(
                    "gjrn,ngd->gjrd",
                    exponent.astype(jnp.bfloat16),
                    value_heads,
                    preferred_element_type=jnp.float32,
                )
                return (new_maxima, new_totals, product)

            def unchanged(present):
                return present

            updated.append(lax.cond(offset <= jnp.max(query_pos), compute, unchanged, current))
        return tuple(updated)

    finals = update(
        initial,
        (
            lax.all_gather(keys[0], "ctx", axis=0, tiled=True),
            lax.all_gather(values[0], "ctx", axis=0, tiled=True),
        ),
        jnp.int32(0),
    )
    outputs = []
    for (group_rows, query_pos), final_state in zip(groups, finals):
        maxima, totals, weighted = final_state
        result = weighted / totals[..., None]
        result = jnp.transpose(result, (2, 0, 1, 3)).reshape(group_rows.shape[0], HQ * DH)
        outputs.append(result.astype(jnp.bfloat16))
    merged = outputs[0]
    return merged[None]


def experts(hidden, expert_ids, gate_probs, norm_gain, w_gate, w_up, w_down):
    tokens = hidden[0].astype(jnp.float32)
    row_count = tokens.shape[0]
    route_count = expert_ids.shape[2]
    expert_count = lax.axis_size("ep")
    capacity = 3 * row_count * route_count // (2 * expert_count)
    mean_square = jnp.mean(tokens * tokens, axis=-1, keepdims=True)
    normed = (tokens * lax.rsqrt(mean_square + 1e-06) * norm_gain).astype(jnp.bfloat16)
    flat_ids = expert_ids[0].reshape(row_count * route_count)
    onehot = (flat_ids[:, None] == jnp.arange(expert_count, dtype=jnp.int32)[None, :]).astype(
        jnp.int32
    )
    before = jnp.cumsum(onehot, axis=0) - onehot
    slot_index = jnp.sum(before * onehot, axis=1)
    target = (flat_ids * capacity + slot_index).reshape(row_count, route_count)
    slot_rows = jnp.arange(expert_count * capacity, dtype=jnp.int32)
    placement = jnp.any(target[None, :, :] == slot_rows[:, None, None], axis=-1).astype(
        jnp.bfloat16
    )
    outgoing = jnp.dot(placement, normed, preferred_element_type=jnp.float32).astype(jnp.bfloat16)
    outgoing = outgoing.reshape(expert_count, capacity, normed.shape[1])
    received = lax.all_to_all(outgoing, "ep", split_axis=0, concat_axis=0, tiled=True)
    flat_rows = received.reshape(expert_count * capacity, normed.shape[1])
    gate_rows = lax.all_gather(w_gate[0], "ctx", axis=0, tiled=True)
    up_rows = lax.all_gather(w_up[0], "ctx", axis=0, tiled=True)
    down_rows = lax.all_gather(w_down[0], "ctx", axis=0, tiled=True)
    contract = (((1,), (1,)), ((), ()))
    gate_pre = lax.dot_general(flat_rows, gate_rows, contract, preferred_element_type=jnp.float32)
    up_pre = lax.dot_general(flat_rows, up_rows, contract, preferred_element_type=jnp.float32)
    activated = (jax.nn.silu(gate_pre) * up_pre).astype(jnp.bfloat16)
    produced = jnp.dot(activated, down_rows, preferred_element_type=jnp.float32)
    produced = produced.astype(jnp.bfloat16).reshape(expert_count, capacity, normed.shape[1])
    returned = lax.all_to_all(produced, "ep", split_axis=0, concat_axis=0, tiled=True)
    returned_rows = returned.reshape(expert_count * capacity, normed.shape[1])
    picked = returned_rows[target]
    route_weight = gate_probs[0]
    mixture = jnp.zeros((row_count, normed.shape[1]), jnp.float32)
    for route in range(route_count):
        mixture = mixture + route_weight[:, route : route + 1] * picked[:, route].astype(
            jnp.float32
        )
    return mixture.astype(jnp.bfloat16)[None]


def per_device(
    queries, keys, values, hidden, expert_ids, gate_probs, norm_gain, w_gate, w_up, w_down
):
    attended = attend(queries, keys, values)
    expert_mix = experts(hidden, expert_ids, gate_probs, norm_gain, w_gate, w_up, w_down)
    return (attended, expert_mix)


def solution(mesh):
    placed = (
        P("ep", "ctx", None),
        P("ep", "ctx", None),
        P("ep", "ctx", None),
        P("ep", "ctx", None),
        P("ep", "ctx", None),
        P("ep", "ctx", None),
        P(),
        P("ep", "ctx", None),
        P("ep", "ctx", None),
        P("ep", "ctx", None),
    )
    return jax.shard_map(
        per_device,
        mesh=mesh,
        in_specs=placed,
        out_specs=(P("ep", "ctx", None), P("ep", "ctx", None)),
        check_vma=False,
    )
```

profile of v0, /device:TPU:1, one launch (start us, length us, event | category | flops | bytes accessed | tf_op | source)
XLA Modules:
  0.0 414.1 jit_solution(6666725445391555825)
XLA Ops:
  7.2 0.7 all-gather.15.cloned.1.call-update
  7.9 0.7 all-gather.19.cloned.1.call-update
  8.6 0.8 copy.37
  11.0 1.2 fusion.27
  12.2 1.7 convolution_convert_fusion
  13.9 1.5 reshape.198
  15.4 16.7 %all-to-all-start = ((bf16[32,12,2048]{2,1,0:T(8,128)(2,1)}), bf16[32,12,2048]{2,1,0:T(8,128)(2,1)S(1)}, u32[]{:S(2)}, u32[]{:S(2)}) async-start(bf16[32,12,2048]{2,1,0:T(8,128)(2,1)} %reshape.198), calls=%async_computation | async-start | bytes 4194304 | tf_op jit(solution)/shard_map/all_to_all | solution.py:106
  32.2 0.7 all-gather.17.cloned.1.call-update
  32.9 97.9 %all-to-all-done = bf16[32,12,2048]{2,1,0:T(8,128)(2,1)S(1)} async-done(((bf16[32,12,2048]{2,1,0:T(8,128)(2,1)}), bf16[32,12,2048]{2,1,0:T(8,128)(2,1)S(1)}, u32[]{:S(2)}, u32[]{:S(2)}) %all-to-all-start) | async-done | bytes 1572896 | tf_op jit(solution)/shard_map/all_to_all | solution.py:106
  130.8 1.4 reshape.199
  132.1 5.0 %fusion.16 = f32[384,768]{1,0:T(8,128)} fusion(bf16[384,2048]{1,0:T(8,128)(2,1)} %reshape.199, bf16[1,768,2048]{2,1,0:T(8,128)(2,1)} %all-gather.15.cloned.1.call-done), kind=kOutput, calls=%fused_computation.20 | convolution fusion | flops 1207959552 | bytes 5898240 | tf_op jit(solution)/shard_map/dot_general | solution.py:112
  137.2 7.5 %all-gather.19.cloned.1.call-done = bf16[1,768,2048]{2,1,0:T(8,128)(2,1)} async-done(((bf16[1,48,2048]{2,1,0:T(8,128)(2,1)}), bf16[1,768,2048]{2,1,0:T(8,128)(2,1)}) %all-gather.19.cloned.1.call-update) | async-done | bytes 3145744 | tf_op jit(solution)/shard_map/all_gather | solution.py:110
  144.7 65.4 %all-gather.17.cloned.1.call-done = bf16[1,768,2048]{2,1,0:T(8,128)(2,1)} async-done(((bf16[1,48,2048]{2,1,0:T(8,128)(2,1)}), bf16[1,768,2048]{2,1,0:T(8,128)(2,1)}) %all-gather.17.cloned.1.call-update) | async-done | bytes 3145744 | tf_op jit(solution)/shard_map/all_gather | solution.py:109
  210.1 6.3 %fusion.18 = bf16[384,2048]{1,0:T(8,128)(2,1)S(1)} fusion(bf16[1,768,2048]{2,1,0:T(8,128)(2,1)} %all-gather.19.cloned.1.call-done, bf16[384,2048]{1,0:T(8,128)(2,1)S(1)} %copy-done, bf16[1,768,2048]{2,1,0:T(8,128)(2,1)} %all-gather.17.cloned.1.call-done, f32[384,768]{1,0:T(8,128)} %fusion.16), kind=kOutput, calls=%fused_computation.22 | convolution fusion | flops 2418475008 | bytes 10616832 | tf_op jit(solution)/shard_map/dot_general | solution.py:115
  216.4 1.6 reshape.200
  217.9 13.5 %all-to-all-start.1 = ((bf16[32,12,2048]{2,1,0:T(8,128)(2,1)}), bf16[32,12,2048]{2,1,0:T(8,128)(2,1)}, u32[]{:S(2)}, u32[]{:S(2)}) async-start(bf16[32,12,2048]{2,1,0:T(8,128)(2,1)} %reshape.200), calls=%async_computation.1 | async-start | bytes 4194304 | tf_op jit(solution)/shard_map/all_to_all | solution.py:117
  234.3 55.6 %all-gather.11.cloned.1.call-done = bf16[1,2048,256]{2,1,0:T(8,128)(2,1)} async-done(((bf16[1,128,256]{2,1,0:T(8,128)(2,1)}), bf16[1,2048,256]{2,1,0:T(8,128)(2,1)}) %all-gather.11.cloned.1.call-update) | async-done | bytes 1048592 | tf_op jit(solution)/shard_map/all_gather | solution.py:70
  289.9 60.2 %all-gather.13.cloned.1.call-done = bf16[1,2048,256]{2,1,0:T(8,128)(2,1)} async-done(((bf16[1,128,256]{2,1,0:T(8,128)(2,1)}), bf16[1,2048,256]{2,1,0:T(8,128)(2,1)}) %all-gather.13.cloned.1.call-update) | async-done | bytes 1048592 | tf_op jit(solution)/shard_map/all_gather | solution.py:71
  350.1 46.9 %conditional.1 = (f32[2,16,128]{2,1,0:T(8,128)S(1)}, f32[2,16,128,128]{3,2,1,0:T(8,128)S(1)}) conditional(s32[]{:T(128)} %convert_element_type.84, () %tuple.16, (s32[2048]{0:T(1024)S(1)}, s32[128]{0:T(128)S(1)}, bf16[2048,256]{1,0:T(8,128)(2,1)}, bf16[1,128,4096]{2,1,0:T(8,128)(2,1)S(1)}, bf16[2048,256]{1,0:T(8,128)(2,1)}) %tuple.36), branch_computations={%region_1.0_spmd, %region_2.5_spmd} | conditional | flops 4387500032 | bytes 117547560 | solution.py:64
  350.7 1.3 reshape.190
  352.0 13.2 %fusion.2 = (f32[2,16,128]{2,1,0:T(8,128)S(1)}, f32[2,2048,128,16]{2,1,3,0:T(8,128)}) fusion(pred[128,2048]{0,1:T(8,128)(4,1)S(1)} %broadcast_compare_fusion, bf16[128,2,16,128]{3,2,1,0:T(8,128)(2,1)S(1)} %bitcast.90, bf16[2048,2,128,1]{2,1,0,3:T(2,128)(2,1)S(1)} %bitcast.91), kind=kOutput, calls=%fused_computation.5 | convolution fusion | flops 2172645376 | bytes 35930112 | tf_op jit(solution)/shard_map/cond/branch_1_fun/rgjd,ngd->gjrn/dot_general | solution.py:43
  365.3 14.4 %fusion.1 = f32[2,16,128]{2,1,0:T(8,128)S(1)} fusion(f32[2,2048,128,16]{2,1,3,0:T(8,128)} %get-tuple-element.27, f32[2,16,128]{2,1,0:T(8,128)S(1)} %broadcast_maximum_fusion, pred[128,2048]{0,1:T(8,128)(4,1)S(1)} %broadcast_compare_fusion), kind=kLoop, calls=%fused_computation.4 | loop fusion | flops 33550336 | bytes 33849344 | tf_op jit(solution)/shard_map/cond/branch_1_fun/reduce_sum | solution.py:52
  379.7 1.1 reshape.191
  380.8 15.9 %fusion.3 = f32[2,16,128,128]{3,2,1,0:T(8,128)S(1)} fusion(f32[2,2048,128,16]{2,1,3,0:T(8,128)} %get-tuple-element.27, f32[2,16,128]{2,1,0:T(8,128)S(1)} %broadcast_maximum_fusion, pred[128,2048]{0,1:T(8,128)(4,1)S(1)} %broadcast_compare_fusion, bf16[2048,2,128,1]{2,1,0,3:T(2,128)(2,1)} %bitcast.95), kind=kOutput, calls=%fused_computation.6 | convolution fusion | flops 2181038080 | bytes 36978688 | tf_op jit(solution)/shard_map/cond/branch_1_fun/gjrn,ngd->gjrd/dot_general | solution.py:53
  396.9 0.7 fusion.32
  397.7 0.7 copy.36
  398.4 1.3 convert_element_type.87
  399.6 2.5 reshape.201
  402.1 1.4 gather_fusion
  403.5 0.7 reshape.206
  404.2 1.5 fusion.47
  405.7 1.8 fusion.31
  (41 shorter events, 4.3 us)
Async XLA Ops:
  7.2 125.0 %all-gather.15.cloned.1.call-start = ((), (), s32[]{:S(2)}) async-start(), calls=%async_computation.4 | async-start | bytes 3342336 | tf_op jit(solution)/shard_map/all_gather | solution.py:108
  7.9 136.8 %all-gather.19.cloned.1.call-start = ((), (), s32[]{:S(2)}) async-start(), calls=%async_computation.6 | async-start | bytes 3342336 | tf_op jit(solution)/shard_map/all_gather | solution.py:110
  15.4 115.4 %all-to-all-start = ((bf16[32,12,2048]{2,1,0:T(8,128)(2,1)}), bf16[32,12,2048]{2,1,0:T(8,128)(2,1)S(1)}, u32[]{:S(2)}, u32[]{:S(2)}) async-start(bf16[32,12,2048]{2,1,0:T(8,128)(2,1)} %reshape.198), calls=%async_computation | async-start | bytes 4194304 | tf_op jit(solution)/shard_map/all_to_all | solution.py:106
  32.2 177.9 %all-gather.17.cloned.1.call-start = ((), (), s32[]{:S(2)}) async-start(), calls=%async_computation.5 | async-start | bytes 3342336 | tf_op jit(solution)/shard_map/all_gather | solution.py:109
  132.1 78.0 %copy-start = (bf16[384,2048]{1,0:T(8,128)(2,1)S(1)}, bf16[384,2048]{1,0:T(8,128)(2,1)}, u32[]{:S(2)}) copy-start(bf16[384,2048]{1,0:T(8,128)(2,1)} %reshape.199) | copy-start | bytes 4718596
  217.9 16.3 %copy-start.3 = (f32[1,128,2]{1,2,0:T(2,128)S(1)}, f32[1,128,2]{1,2,0:T(2,128)}, u32[]{:S(2)}) copy-start(f32[1,128,2]{1,2,0:T(2,128)} %param.17) | copy-start | bytes 3076
  217.9 132.1 %copy-start.1 = (bf16[1,128,4096]{2,1,0:T(8,128)(2,1)S(1)}, bf16[1,128,4096]{2,1,0:T(8,128)(2,1)}, u32[]{:S(2)}) copy-start(bf16[1,128,4096]{2,1,0:T(8,128)(2,1)} %param.12) | copy-start | bytes 3145732
  217.9 181.7 %all-to-all-start.1 = ((bf16[32,12,2048]{2,1,0:T(8,128)(2,1)}), bf16[32,12,2048]{2,1,0:T(8,128)(2,1)}, u32[]{:S(2)}, u32[]{:S(2)}) async-start(bf16[32,12,2048]{2,1,0:T(8,128)(2,1)} %reshape.200), calls=%async_computation.1 | async-start | bytes 4194304 | tf_op jit(solution)/shard_map/all_to_all | solution.py:117
  231.5 58.5 %all-gather.11.cloned.1.call-start = ((), (), s32[]{:S(2)}) async-start(), calls=%async_computation.2 | async-start | bytes 1114112 | tf_op jit(solution)/shard_map/all_gather | solution.py:70
  232.0 118.0 %all-gather.13.cloned.1.call-start = ((), (), s32[]{:S(2)}) async-start(), calls=%async_computation.3 | async-start | bytes 1114112 | tf_op jit(solution)/shard_map/all_gather | solution.py:71
  365.3 14.4 %copy-start.2 = (bf16[2048,256]{1,0:T(8,128)(2,1)S(1)}, bf16[2048,256]{1,0:T(8,128)(2,1)}, u32[]{:S(2)}) copy-start(bf16[2048,256]{1,0:T(8,128)(2,1)} %get-tuple-element.17) | copy-start | bytes 3145732 | tf_op jit(solution)/shard_map/cond
Sparse Core Ops, SparseCore 0:
  11.1 68.2 all-gather.14
  82.4 62.2 all-gather.18
  147.8 62.2 all-gather.16
  235.0 54.8 all-gather.10
  292.8 57.2 all-gather.12
where the time goes:
time: 415 us; the launch traced here: 414 us
  waiting for transfers between devices  290 us (70%)
  matrix products  42.2 us (10%)
  starting transfers between devices  30.4 us (7%)
  other arithmetic  20 us (5%)
  local copies, waits for them, and re-layouts  16.9 us (4%)
  between operations  14.6 us (4%)
    all_to_all x1, waiting for transfers between devices, experts(): lax.all_to_all(outgoing, 'ep', split_axis=0, concat_axis=0, tiled=True)  97.9 us
    all_gather x1, waiting for transfers between devices, experts(): up_rows = lax.all_gather(w_up[0], 'ctx', axis=0, tiled=True)  65.4 us
    all_gather x1, waiting for transfers between devices, attend(): lax.all_gather(values[0], 'ctx', axis=0, tiled=True)  60.2 us
    all_gather x1, waiting for transfers between devices, attend(): lax.all_gather(keys[0], 'ctx', axis=0, tiled=True)  55.6 us
    all_to_all x1, starting transfers between devices, experts(): lax.all_to_all(outgoing, 'ep', split_axis=0, concat_axis=0, tiled=True)  16.7 us
    dot_general x1, matrix products, compute(): jnp.einsum('gjrn,ngd->gjrd', exponent.astype(jnp.bfloat16), value_heads,...  15.9 us
    reduce_sum x1, other arithmetic, compute(): new_totals = jnp.sum(exponent, axis=-1)  14.4 us
    all_to_all x1, starting transfers between devices, experts(): lax.all_to_all(produced, 'ep', split_axis=0, concat_axis=0, tiled=True)  13.5 us
  transfers between devices with their start and end apart: 7, of which 5 were waited for; matrix products, arithmetic and copies ran while one was open for 15% of the time, Pallas kernels for 0%

commit v1 on v0

v1 whole, which is shorter than its diff:
```python
import functools
import math

import jax
import jax.numpy as jnp
from jax import lax
from jax.experimental import pallas as pl
from jax.experimental.pallas import tpu as pltpu
from jax.sharding import PartitionSpec as P

HQ = 32
KVH = 2
DH = 128
CAP = 12
WHOLE = 8
CHUNK = 512
PAIRS = 4
VMEM = 40 << 20
BF16 = jnp.bfloat16
F32 = jnp.float32


def dot(a, b):
    return jnp.dot(a, b, preferred_element_type=F32)


def dot_nt(a, b):
    return lax.dot_general(a, b, (((1,), (1,)), ((), ())), preferred_element_type=F32)


def dispatch_kernel(hidden_ref, ids_ref, gain_ref, out_ref, place_ref):
    rows, width = hidden_ref.shape
    half = width // 2
    experts = out_ref.shape[0] // WHOLE
    tokens = hidden_ref[...].astype(F32)
    mean_square = jnp.mean(tokens * tokens, axis=-1, keepdims=True)
    normed = (tokens * lax.rsqrt(mean_square + 1e-06) * gain_ref[...]).astype(BF16)

    ids = ids_ref[...]
    first, second = ids[0:1, :], ids[1:2, :]
    expert_iota = lax.broadcasted_iota(jnp.int32, (experts, rows), 0)
    hot = [(expert_iota == ids_row).astype(F32) for ids_row in (first, second)]
    earlier = (
        lax.broadcasted_iota(jnp.int32, (rows, rows), 0)
        < lax.broadcasted_iota(jnp.int32, (rows, rows), 1)
    ).astype(BF16)
    before = [dot(h.astype(BF16), earlier) for h in hot]
    before[1] = before[1] + jnp.sum(hot[0], axis=1, keepdims=True)
    slots = [
        jnp.sum(h * b, axis=0, keepdims=True).astype(jnp.int32) for h, b in zip(hot, before)
    ]
    whole = [
        jnp.where(s < WHOLE, e * WHOLE + s, -1) for e, s in zip((first, second), slots)
    ]
    halves = [
        jnp.where(s < WHOLE, -2, e * WHOLE + 2 * (s - WHOLE))
        for e, s in zip((first, second), slots)
    ]
    slot_iota = lax.broadcasted_iota(jnp.int32, (experts * WHOLE, rows), 0)

    def onehot(targets):
        return ((slot_iota == targets[0]) | (slot_iota == targets[1])).astype(F32).astype(BF16)

    out_ref[:, :width] = dot(onehot(whole), normed).astype(BF16)
    out_ref[:, width:] = (
        dot(onehot(halves), normed[:, :half])
        + dot(onehot([h + 1 for h in halves]), normed[:, half:])
    ).astype(BF16)
    place_ref[...] = jnp.concatenate(whole + halves + whole + halves, axis=0)


def dispatch(hidden, ids, gain, experts):
    rows, width = hidden.shape
    return pl.pallas_call(
        dispatch_kernel,
        out_shape=(
            jax.ShapeDtypeStruct((experts * WHOLE, width + width // 2), BF16),
            jax.ShapeDtypeStruct((8, rows), jnp.int32),
        ),
        compiler_params=pltpu.CompilerParams(vmem_limit_bytes=VMEM),
        name="dispatch",
    )(hidden, ids, gain)


def expert_kernel(rows_ref, weights_ref, out_ref, x_ref, y_ref, act_ref, w_ref, sems):
    count = rows_ref.shape[0]
    width = x_ref.shape[1]
    half = width // 2
    hidden = w_ref.shape[1]
    steps = 3
    span = hidden // steps
    copies = {}
    for step in range(steps):
        for part in range(2):
            copies[part, step] = pltpu.make_async_copy(
                weights_ref.at[pl.ds(step * span, span), pl.ds(part * width, width)],
                w_ref.at[part, pl.ds(step * span, span), :],
                sems.at[2 * step + part],
            )
    copies[2, 0] = pltpu.make_async_copy(
        weights_ref.at[:, pl.ds(2 * width, width)], w_ref.at[2], sems.at[2 * steps]
    )
    for copy in copies.values():
        copy.start()

    extra = count // 2
    pick_row = lax.broadcasted_iota(jnp.int32, (extra, count), 0)
    pick_col = lax.broadcasted_iota(jnp.int32, (extra, count), 1)
    x_ref[pl.ds(0, count), :] = rows_ref[:, :width]
    tail = rows_ref[:, width:]
    for part in range(2):
        pick = (pick_col == 2 * pick_row + part).astype(F32).astype(BF16)
        x_ref[pl.ds(count, extra), pl.ds(part * half, half)] = dot(pick, tail).astype(BF16)

    for step in range(steps):
        for part in range(2):
            copies[part, step].wait()
        x = x_ref[...]
        gate_pre = dot_nt(x, w_ref[0, pl.ds(step * span, span), :])
        up_pre = dot_nt(x, w_ref[1, pl.ds(step * span, span), :])
        act_ref[:, pl.ds(step * span, span)] = (
            gate_pre / (1.0 + jnp.exp(-gate_pre)) * up_pre
        ).astype(BF16)
    copies[2, 0].wait()
    act = act_ref[...]
    piece = width // 4
    for step in range(4):
        lanes = pl.ds(step * piece, piece)
        y = dot(act, w_ref[2, :, lanes]).astype(BF16)
        out_ref[:, lanes] = y[:count]
        y_ref[:, lanes] = y[count:]
    put_row = lax.broadcasted_iota(jnp.int32, (count, extra), 0)
    put_col = lax.broadcasted_iota(jnp.int32, (count, extra), 1)
    total = 0.0
    for part in range(2):
        put = (put_row == 2 * put_col + part).astype(F32).astype(BF16)
        total = total + dot(put, y_ref[:, pl.ds(part * half, half)])
    out_ref[:, width:] = total.astype(BF16)


def expert(rows, weights):
    count = rows.shape[0]
    hidden, width = weights.shape[0], weights.shape[1] // 3
    total = count // WHOLE * CAP
    return pl.pallas_call(
        expert_kernel,
        out_shape=jax.ShapeDtypeStruct(rows.shape, BF16),
        in_specs=[
            pl.BlockSpec(memory_space=pltpu.VMEM),
            pl.BlockSpec(memory_space=pltpu.HBM),
        ],
        out_specs=pl.BlockSpec(memory_space=pltpu.VMEM),
        scratch_shapes=[
            pltpu.VMEM((total, width), BF16),
            pltpu.VMEM((total - count, width), BF16),
            pltpu.VMEM((total, hidden), BF16),
            pltpu.VMEM((3, hidden, width), BF16),
            pltpu.SemaphoreType.DMA((7,)),
        ],
        compiler_params=pltpu.CompilerParams(vmem_limit_bytes=56 << 20),
        cost_estimate=pl.CostEstimate(
            flops=6 * total * hidden * width,
            bytes_accessed=2 * weights.size + 4 * rows.size,
            transcendentals=total * hidden,
        ),
        name="expert",
    )(rows, weights)


def combine_kernel(returned_ref, place_ref, prob_ref, out_ref):
    count = returned_ref.shape[0]
    rows, width = out_ref.shape
    half = width // 2
    place = place_ref[...].astype(F32).T.astype(jnp.int32)
    prob = prob_ref[...].T
    slot_iota = lax.broadcasted_iota(jnp.int32, (rows, count), 1)

    def onehot(column):
        return (slot_iota == column).astype(F32).astype(BF16)

    whole = [onehot(place[:, route : route + 1]) for route in range(2)]
    for part in range(2):
        lanes = pl.ds(part * half, half)
        mixture = 0.0
        for route in range(2):
            picked = dot(whole[route], returned_ref[:, lanes]) + dot(
                onehot(place[:, 2 + route : 3 + route] + part), returned_ref[:, width:]
            )
            mixture = mixture + prob[:, route : route + 1] * picked
        out_ref[:, lanes] = mixture.astype(BF16)


def combine(returned, place, prob):
    rows, width = place.shape[1], returned.shape[1] // 3 * 2
    return pl.pallas_call(
        combine_kernel,
        out_shape=jax.ShapeDtypeStruct((rows, width), BF16),
        compiler_params=pltpu.CompilerParams(vmem_limit_bytes=VMEM),
        name="combine",
    )(returned, place, prob)


def attention_kernel(block_ref, query_ref, key_ref, value_ref, out_ref, vt_ref, *score_refs):
    block = block_ref[0]
    rows = query_ref.shape[0]
    seq = key_ref.shape[0]
    width = 2 * rows
    factor = math.log2(math.e) / math.sqrt(DH)

    @pl.when(pl.program_id(1) == 0)
    def _():
        vt_ref[...] = value_ref[...].T

    row_less_key = (
        block * rows
        + lax.rem(lax.broadcasted_iota(jnp.int32, (CHUNK, width), 1), jnp.int32(rows))
        - lax.broadcasted_iota(jnp.int32, (CHUNK, width), 0)
    )

    def scores(pair, chunks):
        first = query_ref[:, 2 * pair * DH : (2 * pair + 1) * DH]
        second = query_ref[:, (2 * pair + 1) * DH : (2 * pair + 2) * DH]
        query_t = jnp.concatenate([first.T, second.T], axis=1)
        tops = []
        for chunk in range(chunks):
            at = slice(chunk * CHUNK, (chunk + 1) * CHUNK)
            raw = dot(key_ref[at, :], query_t)
            if chunk == chunks - 1:
                raw = jnp.where(row_less_key >= chunk * CHUNK, raw, -jnp.inf)
            score_refs[pair][at, :] = raw
            tops.append(jnp.max(raw, axis=0, keepdims=True))
        return functools.reduce(jnp.maximum, tops)

    def weigh(pair, chunks, top):
        total, weighted = 0.0, 0.0
        for chunk in range(chunks):
            at = slice(chunk * CHUNK, (chunk + 1) * CHUNK)
            prob = jnp.exp2((score_refs[pair][at, :] - top) * factor)
            weighted = weighted + dot(vt_ref[:, at], prob.astype(BF16))
            total = total + jnp.sum(prob, axis=0, keepdims=True)
        result = weighted / total
        for head in range(2):
            out_ref[:, (2 * pair + head) * DH : (2 * pair + head + 1) * DH] = (
                result[:, head * rows : (head + 1) * rows].T.astype(BF16)
            )

    for chunks in range(1, seq // CHUNK + 1):

        @pl.when(block * rows // CHUNK + 1 == chunks)
        def _():
            top = scores(0, chunks)
            for pair in range(1, PAIRS):
                next_top = scores(pair, chunks)
                weigh(pair - 1, chunks, top)
                top = next_top
            weigh(PAIRS - 1, chunks, top)


def attention(block, queries, keys_values):
    rows = queries.shape[0]
    seq = keys_values.shape[0]
    steps = HQ // KVH // 2 // PAIRS
    span = 2 * PAIRS * DH
    return pl.pallas_call(
        attention_kernel,
        out_shape=jax.ShapeDtypeStruct(queries.shape, BF16),
        grid_spec=pltpu.PrefetchScalarGridSpec(
            num_scalar_prefetch=1,
            grid=(KVH, steps),
            in_specs=[
                pl.BlockSpec((rows, span), lambda g, p, b: (0, g * steps + p)),
                pl.BlockSpec((seq, DH), lambda g, p, b: (0, g)),
                pl.BlockSpec((seq, DH), lambda g, p, b: (0, KVH + g)),
            ],
            out_specs=pl.BlockSpec((rows, span), lambda g, p, b: (0, g * steps + p)),
            scratch_shapes=[pltpu.VMEM((DH, seq), BF16)]
            + [pltpu.VMEM((seq, 2 * rows), F32)] * PAIRS,
        ),
        compiler_params=pltpu.CompilerParams(
            dimension_semantics=("arbitrary", "arbitrary"), vmem_limit_bytes=VMEM
        ),
        cost_estimate=pl.CostEstimate(
            flops=4 * rows * seq * HQ * DH,
            bytes_accessed=4 * queries.size + 2 * keys_values.size,
            transcendentals=rows * seq * HQ,
        ),
        name="attention",
    )(block, queries, keys_values, keys_values)


def per_device(
    queries, keys, values, hidden, expert_ids, gate_probs, norm_gain, w_gate, w_up, w_down
):
    experts = lax.axis_size("ep")
    width = hidden.shape[2]
    shards = jnp.concatenate([w_gate[0], w_up[0], w_down[0]], axis=1)
    weights = lax.all_gather(shards, "ctx", axis=0, tiled=True)

    outgoing, place = dispatch(hidden[0], expert_ids[0].T, norm_gain[None], experts)
    keys_values = jnp.concatenate([keys[0], values[0]], axis=1)
    outgoing, keys_values = lax.optimization_barrier((outgoing, keys_values))
    keys_values = lax.all_gather(keys_values, "ctx", axis=0, tiled=True)

    def exchange(rows):
        moved = lax.all_to_all(
            rows.reshape(experts, WHOLE, rows.shape[1]), "ep", split_axis=0, concat_axis=0, tiled=True
        )
        return moved.reshape(rows.shape)

    produced = expert(exchange(outgoing), weights)
    produced, queries = lax.optimization_barrier((produced, queries))
    returned = exchange(produced)
    block = lax.axis_index("ctx").astype(jnp.int32)[None]
    attended = attention(block, queries[0], keys_values)
    mixed = combine(returned, place, gate_probs[0].T)
    return (attended[None], mixed[None])


def solution(mesh):
    split = P("ep", "ctx", None)
    return jax.shard_map(
        per_device,
        mesh=mesh,
        in_specs=(split,) * 6 + (P(),) + (split,) * 3,
        out_specs=(split, split),
        check_vma=False,
    )
```

time: 415 us -> 217 us (0.52)
  waiting for transfers between devices: 290 us -> 71.3 us
  blocking collectives: 0 us -> 95.2 us
  matrix products: 42.2 us -> 0 us
  Pallas kernels: 0 us -> 18.2 us
  other arithmetic: 20 us -> 2.68 us
  starting transfers between devices: 30.4 us -> 13.4 us
  local copies, waits for them, and re-layouts: 16.9 us -> 1.62 us
    all_gather x5 -> x2, waiting for transfers between devices: 189 us -> 64 us  [the longest x1 62.1 us: per_device(): keys_values = lax.all_gather(keys_values, 'ctx', axis=0, tiled=True)]
    all_to_all x0 -> x1, blocking collectives: none -> 95.2 us  [exchange(): lax.all_to_all(rows.reshape(experts, WHOLE, rows.shape[1]), 'ep', split_a...]
    all_to_all x2 -> x1, waiting for transfers between devices: 97.9 us -> 6.82 us  [exchange(): lax.all_to_all(rows.reshape(experts, WHOLE, rows.shape[1]), 'ep', split_a...]
    dot_general x5 -> x0, matrix products: 42.2 us -> none  [the longest x1 15.9 us: compute(): jnp.einsum('gjrn,ngd->gjrd', exponent.astype(jnp.bfloat16), value_heads,...]
    pallas_call x0 -> x4, Pallas kernels: none -> 18.2 us  [the longest x1 8.99 us: expert(): pl.pallas_call(expert_kernel, out_shape=jax.ShapeDtypeStruct(rows.shape,...]
    all_to_all x2 -> x1, starting transfers between devices: 30.2 us -> 13.2 us  [exchange(): lax.all_to_all(rows.reshape(experts, WHOLE, rows.shape[1]), 'ep', split_a...]
    reduce_sum x3 -> x0, other arithmetic: 15.7 us -> none  [the longest x1 14.4 us: compute(): new_totals = jnp.sum(exponent, axis=-1)]
    reshape x6 -> x0, local copies, waits for them, and re-layouts: 9.38 us -> none  [the longest x1 2.49 us: experts(): returned_rows = returned.reshape(expert_count * capacity, normed.shape[1])]
  transfers between devices with their start and end apart: 7 -> 3, of which waited for: 5 -> 3; matrix products, arithmetic and copies ran while one was open for 15% -> 0% of each run, Pallas kernels for 0% -> 3%
where the time goes in v1:
time: 217 us
  blocking collectives  95.2 us (44%)
  waiting for transfers between devices  71.3 us (33%)
  Pallas kernels  18.2 us (8%)
  between operations  14.2 us (7%)
  starting transfers between devices  13.4 us (6%)
  other arithmetic  2.68 us (1%)
    all_to_all x1, blocking collectives, exchange(): lax.all_to_all(rows.reshape(experts, WHOLE, rows.shape[1]), 'ep', split_a...  95.2 us
    all_gather x1, waiting for transfers between devices, per_device(): keys_values = lax.all_gather(keys_values, 'ctx', axis=0, tiled=True)  62.1 us
    all_to_all x1, starting transfers between devices, exchange(): lax.all_to_all(rows.reshape(experts, WHOLE, rows.shape[1]), 'ep', split_a...  13.2 us
    pallas_call x1, Pallas kernels, expert(): pl.pallas_call(expert_kernel, out_shape=jax.ShapeDtypeStruct(rows.shape,...  8.99 us
    all_to_all x1, waiting for transfers between devices, exchange(): lax.all_to_all(rows.reshape(experts, WHOLE, rows.shape[1]), 'ep', split_a...  6.82 us
    pallas_call x1, Pallas kernels, attention(): pl.pallas_call(attention_kernel, out_shape=jax.ShapeDtypeStruct(queries.s...  6.58 us
  transfers between devices with their start and end apart: 3, of which 3 were waited for; matrix products, arithmetic and copies ran while one was open for 0% of the time, Pallas kernels for 3%

profile of v1, /device:TPU:1, one launch (start us, length us, event | category | flops | bytes accessed | tf_op | source)
XLA Modules:
  0.0 216.6 jit_solution(14815573514239771979)
XLA Ops:
  7.2 0.0 copy-start
  7.2 0.0 copy-start.2
  7.2 0.0 copy-start.1
  7.2 0.0 copy-start.7
  7.2 0.0 copy-start.6
  7.2 0.0 all-gather.3.cloned.1.call-start
  7.3 2.0 pad_maximum_fusion
  9.3 0.0 all-gather.3.cloned.1.call-update
  9.3 0.0 copy-done
  9.3 0.0 copy-done.2
  9.3 0.0 copy-done.1
  9.3 0.9 dispatch.1
  10.3 0.0 copy-done.7
  10.3 0.0 copy-done.6
  10.3 0.7 pad_maximum_fusion.1
  11.0 95.2 %all_to_all.10 = bf16[32,8,3072]{2,1,0:T(8,128)(2,1)} all-to-all(bf16[32,8,3072]{2,1,0:T(8,128)(2,1)S(1)} %bitcast.22), channel_id=1, replica_groups=mesh['ctx'=16,'ep'=32] {'ep'}, dimensions={0} | all-to-all | bytes 3145728 | tf_op jit(solution)/shard_map/all_to_all | solution.py:305
  106.1 1.9 all-gather.3.cloned.1.call-done.weights_ref
  108.0 9.0 %expert.1 = bf16[256,3072]{1,0:T(8,128)(2,1)} custom-call(bf16[256,3072]{1,0:T(8,128)(2,1)} %bitcast.29, bf16[768,6144]{1,0:T(8,128)(2,1)} %all-gather.3.cloned.1.call-done.weights_ref), custom_call_target="tpu_custom_call" | custom-call | flops 3623878656 | bytes 12582912 | tf_op jit(solution)/shard_map/expert/pallas_call | solution.py:145
  117.0 0.0 copy-start.5
  117.1 13.2 %all-to-all-start.1 = ((bf16[32,8,3072]{2,1,0:T(8,128)(2,1)}), bf16[32,8,3072]{2,1,0:T(8,128)(2,1)S(1)}, u32[]{:S(2)}, u32[]{:S(2)}) async-start(bf16[32,8,3072]{2,1,0:T(8,128)(2,1)} %bitcast.28), calls=%async_computation.1 | async-start | bytes 3145728 | tf_op jit(solution)/shard_map/all_to_all | solution.py:305
  130.2 0.2 all-gather.5.cloned.1.call-start
  130.4 0.5 all-gather.5.cloned.1.call-update
  131.0 62.1 %all-gather.5.cloned.1.call-done.key_ref.value_ref = bf16[2048,512]{1,0:T(8,128)(2,1)} async-done(((bf16[128,512]{1,0:T(8,128)(2,1)}), bf16[2048,512]{1,0:T(8,128)(2,1)}) %all-gather.5.cloned.1.call-update) | async-done | bytes 2097168 | tf_op jit(solution)/shard_map/all_gather | solution.py:302
  193.0 0.0 copy-done.5
  193.0 0.0 copy-start.4
  193.0 1.6 copy-done.4
  194.6 0.0 copy-start.3
  194.6 6.6 %attention.1 = bf16[128,4096]{1,0:T(8,128)(2,1)} custom-call(s32[1]{0:T(128)} %bitcast.block_ref, bf16[128,4096]{1,0:T(8,128)(2,1)S(1)} %bitcast.27, bf16[2048,512]{1,0:T(8,128)(2,1)S(1)} %copy-done.4, bf16[2048,512]{1,0:T(8,128)(2,1)S(1)} %copy-done.4), custom_call_target="tpu_custom_call" | custom-call | flops 4294967296 | bytes 4194304 | tf_op jit(solution)/shard_map/attention/pallas_call | solution.py:264
  201.2 6.8 %all-to-all-done.1 = bf16[32,8,3072]{2,1,0:T(8,128)(2,1)S(1)} async-done(((bf16[32,8,3072]{2,1,0:T(8,128)(2,1)}), bf16[32,8,3072]{2,1,0:T(8,128)(2,1)S(1)}, u32[]{:S(2)}, u32[]{:S(2)}) %all-to-all-start.1) | async-done | bytes 1572896 | tf_op jit(solution)/shard_map/all_to_all | solution.py:305
  208.0 0.0 copy-done.3
  208.0 1.7 combine.1
Async XLA Ops:
  7.2 2.1 copy-start
  7.2 2.1 copy-start.2
  7.2 2.1 copy-start.1
  7.2 3.1 %copy-start.7 = (bf16[1,128,256]{2,1,0:T(8,128)(2,1)S(1)}, bf16[1,128,256]{2,1,0:T(8,128)(2,1)}, u32[]{:S(2)}) copy-start(bf16[1,128,256]{2,1,0:T(8,128)(2,1)} %param.11) | copy-start | bytes 196612
  7.2 3.1 %copy-start.6 = (bf16[1,128,256]{2,1,0:T(8,128)(2,1)S(1)}, bf16[1,128,256]{2,1,0:T(8,128)(2,1)}, u32[]{:S(2)}) copy-start(bf16[1,128,256]{2,1,0:T(8,128)(2,1)} %param.12) | copy-start | bytes 196612
  7.2 100.8 %all-gather.3.cloned.1.call-start = ((), (), s32[]{:S(2)}) async-start(), calls=%async_computation.2 | async-start | bytes 10027008 | tf_op jit(solution)/shard_map/all_gather | solution.py:297
  117.0 76.0 %copy-start.5 = (bf16[1,128,4096]{2,1,0:T(8,128)(2,1)S(1)}, bf16[1,128,4096]{2,1,0:T(8,128)(2,1)}, u32[]{:S(2)}) copy-start(bf16[1,128,4096]{2,1,0:T(8,128)(2,1)} %param.10) | copy-start | bytes 3145732
  117.1 91.0 %all-to-all-start.1 = ((bf16[32,8,3072]{2,1,0:T(8,128)(2,1)}), bf16[32,8,3072]{2,1,0:T(8,128)(2,1)S(1)}, u32[]{:S(2)}, u32[]{:S(2)}) async-start(bf16[32,8,3072]{2,1,0:T(8,128)(2,1)} %bitcast.28), calls=%async_computation.1 | async-start | bytes 3145728 | tf_op jit(solution)/shard_map/all_to_all | solution.py:305
  130.2 62.8 %all-gather.5.cloned.1.call-start = ((), (), s32[]{:S(2)}) async-start(), calls=%async_computation.3 | async-start | bytes 2228224 | tf_op jit(solution)/shard_map/all_gather | solution.py:302
  193.0 1.6 copy-start.4
  194.6 13.4 %copy-start.3 = (f32[1,128,2]{1,2,0:T(2,128)S(1)}, f32[1,128,2]{1,2,0:T(2,128)}, u32[]{:S(2)}) copy-start(f32[1,128,2]{1,2,0:T(2,128)} %param.15) | copy-start | bytes 3076
Sparse Core Ops, SparseCore 0:
  11.7 96.3 all-gather.2
  134.6 58.3 all-gather.4

commit v2 on v1

--- a/solution.py
+++ b/solution.py
@@ -14,8 +14,10 @@
 CAP = 12
 WHOLE = 8
 CHUNK = 512
+RING = 4
+HIDDEN_STEP = 256
 PAIRS = 4
-VMEM = 40 << 20
+VMEM = 16 << 20
 BF16 = jnp.bfloat16
 F32 = jnp.float32
 
@@ -82,25 +84,18 @@
     )(hidden, ids, gain)
 
 
-def expert_kernel(rows_ref, weights_ref, out_ref, x_ref, y_ref, act_ref, w_ref, sems):
+def expert_kernel(rows_ref, *refs):
+    *piece_refs, out_ref, x_ref, y_ref, act_ref, w_ref, sems = refs
     count = rows_ref.shape[0]
     width = x_ref.shape[1]
     half = width // 2
-    hidden = w_ref.shape[1]
-    steps = 3
-    span = hidden // steps
-    copies = {}
-    for step in range(steps):
-        for part in range(2):
-            copies[part, step] = pltpu.make_async_copy(
-                weights_ref.at[pl.ds(step * span, span), pl.ds(part * width, width)],
-                w_ref.at[part, pl.ds(step * span, span), :],
-                sems.at[2 * step + part],
-            )
-    copies[2, 0] = pltpu.make_async_copy(
-        weights_ref.at[:, pl.ds(2 * width, width)], w_ref.at[2], sems.at[2 * steps]
-    )
-    for copy in copies.values():
+    hidden = act_ref.shape[1]
+    copies, base = [], 0
+    for index, ref in enumerate(piece_refs):
+        place = w_ref.at[pl.ds(base, ref.shape[0]), :]
+        copies.append((base, pltpu.make_async_copy(ref, place, sems.at[index])))
+        base += ref.shape[0]
+    for _, copy in copies:
         copy.start()
 
     extra = count // 2
@@ -112,21 +107,19 @@
         pick = (pick_col == 2 * pick_row + part).astype(F32).astype(BF16)
         x_ref[pl.ds(count, extra), pl.ds(part * half, half)] = dot(pick, tail).astype(BF16)
 
-    for step in range(steps):
-        for part in range(2):
-            copies[part, step].wait()
+    for start in range(0, hidden, HIDDEN_STEP):
+        stop = start + HIDDEN_STEP
+        while copies and copies[0][0] < stop:
+            copies.pop(0)[1].wait()
         x = x_ref[...]
-        gate_pre = dot_nt(x, w_ref[0, pl.ds(step * span, span), :])
-        up_pre = dot_nt(x, w_ref[1, pl.ds(step * span, span), :])
-        act_ref[:, pl.ds(step * span, span)] = (
-            gate_pre / (1.0 + jnp.exp(-gate_pre)) * up_pre
-        ).astype(BF16)
-    copies[2, 0].wait()
+        gate_pre = dot_nt(x, w_ref[start:stop, :width])
+        up_pre = dot_nt(x, w_ref[start:stop, width : 2 * width])
+        act_ref[:, start:stop] = (gate_pre / (1.0 + jnp.exp(-gate_pre)) * up_pre).astype(BF16)
     act = act_ref[...]
     piece = width // 4
     for step in range(4):
-        lanes = pl.ds(step * piece, piece)
-        y = dot(act, w_ref[2, :, lanes]).astype(BF16)
+        lanes = slice(step * piece, (step + 1) * piece)
+        y = dot(act, w_ref[:, 2 * width + lanes.start : 2 * width + lanes.stop]).astype(BF16)
         out_ref[:, lanes] = y[:count]
         y_ref[:, lanes] = y[count:]
     put_row = lax.broadcasted_iota(jnp.int32, (count, extra), 0)
@@ -138,33 +131,31 @@
     out_ref[:, width:] = total.astype(BF16)
 
 
-def expert(rows, weights):
+def expert(rows, pieces):
     count = rows.shape[0]
-    hidden, width = weights.shape[0], weights.shape[1] // 3
+    hidden, width = sum(p.shape[0] for p in pieces), pieces[0].shape[1] // 3
     total = count // WHOLE * CAP
     return pl.pallas_call(
         expert_kernel,
         out_shape=jax.ShapeDtypeStruct(rows.shape, BF16),
-        in_specs=[
-            pl.BlockSpec(memory_space=pltpu.VMEM),
-            pl.BlockSpec(memory_space=pltpu.HBM),
-        ],
+        in_specs=[pl.BlockSpec(memory_space=pltpu.VMEM)]
+        + [pl.BlockSpec(memory_space=pl.ANY)] * len(pieces),
         out_specs=pl.BlockSpec(memory_space=pltpu.VMEM),
         scratch_shapes=[
             pltpu.VMEM((total, width), BF16),
             pltpu.VMEM((total - count, width), BF16),
             pltpu.VMEM((total, hidden), BF16),
-            pltpu.VMEM((3, hidden, width), BF16),
-            pltpu.SemaphoreType.DMA((7,)),
+            pltpu.VMEM((hidden, 3 * width), BF16),
+            pltpu.SemaphoreType.DMA((len(pieces),)),
         ],
         compiler_params=pltpu.CompilerParams(vmem_limit_bytes=56 << 20),
         cost_estimate=pl.CostEstimate(
             flops=6 * total * hidden * width,
-            bytes_accessed=2 * weights.size + 4 * rows.size,
+            bytes_accessed=6 * hidden * width + 4 * rows.size,
             transcendentals=total * hidden,
         ),
         name="expert",
-    )(rows, weights)
+    )(rows, *pieces)
 
 
 def combine_kernel(returned_ref, place_ref, prob_ref, out_ref):
@@ -200,7 +191,13 @@
     )(returned, place, prob)
 
 
-def attention_kernel(block_ref, query_ref, key_ref, value_ref, out_ref, vt_ref, *score_refs):
+OFFSETS = (0, -1, 1, 2)
+SOURCES = [(dx, dy) for dx in (0, -1, 1) for dy in OFFSETS]
+SOURCES += [(2, dy) for dy in OFFSETS]
+
+
+def attention_kernel(block_ref, query_ref, *refs):
+    piece_refs, (out_ref, key_ref, vt_ref), score_refs = refs[:10], refs[10:13], refs[13:]
     block = block_ref[0]
     rows = query_ref.shape[0]
     seq = key_ref.shape[0]
@@ -209,31 +206,42 @@
 
     @pl.when(pl.program_id(1) == 0)
     def _():
-        vt_ref[...] = value_ref[...].T
-
-    row_less_key = (
-        block * rows
-        + lax.rem(lax.broadcasted_iota(jnp.int32, (CHUNK, width), 1), jnp.int32(rows))
-        - lax.broadcasted_iota(jnp.int32, (CHUNK, width), 0)
-    )
-
-    def scores(pair, chunks):
+        start = 0
+        for keys, values in zip(piece_refs[:5], piece_refs[5:]):
+            stop = start + keys.shape[0]
+            key_ref[start:stop, :] = keys[...]
+            vt_ref[:, start:stop] = values[...].T
+            start = stop
+
+    row_less_key = lax.rem(
+        lax.broadcasted_iota(jnp.int32, (rows, width), 1), jnp.int32(rows)
+    ) - lax.broadcasted_iota(jnp.int32, (rows, width), 0)
+    place_x, place_y = block // RING, lax.rem(block, RING)
+    least = []
+    for dx, dy in SOURCES:
+        source_x = lax.rem(place_x + (dx + RING), RING)
+        source_y = lax.rem(place_y + (dy + RING), RING)
+        least.append((source_x * RING + source_y - block) * rows)
+
+    def scores(pair):
         first = query_ref[:, 2 * pair * DH : (2 * pair + 1) * DH]
         second = query_ref[:, (2 * pair + 1) * DH : (2 * pair + 2) * DH]
         query_t = jnp.concatenate([first.T, second.T], axis=1)
         tops = []
-        for chunk in range(chunks):
-            at = slice(chunk * CHUNK, (chunk + 1) * CHUNK)
-            raw = dot(key_ref[at, :], query_t)
-            if chunk == chunks - 1:
-                raw = jnp.where(row_less_key >= chunk * CHUNK, raw, -jnp.inf)
-            score_refs[pair][at, :] = raw
-            tops.append(jnp.max(raw, axis=0, keepdims=True))
+        for chunk in range(seq // CHUNK):
+            raw = dot(key_ref[chunk * CHUNK : (chunk + 1) * CHUNK, :], query_t)
+            for sub in range(CHUNK // rows):
+                at = chunk * CHUNK + sub * rows
+                seen = jnp.where(
+                    row_less_key >= least[at // rows], raw[sub * rows : (sub + 1) * rows], -jnp.inf
+                )
+                score_refs[pair][at : at + rows, :] = seen
+                tops.append(jnp.max(seen, axis=0, keepdims=True))
         return functools.reduce(jnp.maximum, tops)
 
-    def weigh(pair, chunks, top):
+    def weigh(pair, top):
         total, weighted = 0.0, 0.0
-        for chunk in range(chunks):
+        for chunk in range(seq // CHUNK):
             at = slice(chunk * CHUNK, (chunk + 1) * CHUNK)
             prob = jnp.exp2((score_refs[pair][at, :] - top) * factor)
             weighted = weighted + dot(vt_ref[:, at], prob.astype(BF16))
@@ -244,21 +252,17 @@
                 result[:, head * rows : (head + 1) * rows].T.astype(BF16)
             )
 
-    for chunks in range(1, seq // CHUNK + 1):
-
-        @pl.when(block * rows // CHUNK + 1 == chunks)
-        def _():
-            top = scores(0, chunks)
-            for pair in range(1, PAIRS):
-                next_top = scores(pair, chunks)
-                weigh(pair - 1, chunks, top)
-                top = next_top
-            weigh(PAIRS - 1, chunks, top)
-
-
-def attention(block, queries, keys_values):
+    top = scores(0)
+    for pair in range(1, PAIRS):
+        next_top = scores(pair)
+        weigh(pair - 1, top)
+        top = next_top
+    weigh(PAIRS - 1, top)
+
+
+def attention(block, queries, pieces):
     rows = queries.shape[0]
-    seq = keys_values.shape[0]
+    seq = sum(p.shape[0] for p in pieces)
     steps = HQ // KVH // 2 // PAIRS
     span = 2 * PAIRS * DH
     return pl.pallas_call(
@@ -267,39 +271,53 @@
         grid_spec=pltpu.PrefetchScalarGridSpec(
             num_scalar_prefetch=1,
             grid=(KVH, steps),
-            in_specs=[
-                pl.BlockSpec((rows, span), lambda g, p, b: (0, g * steps + p)),
-                pl.BlockSpec((seq, DH), lambda g, p, b: (0, g)),
-                pl.BlockSpec((seq, DH), lambda g, p, b: (0, KVH + g)),
-            ],
+            in_specs=[pl.BlockSpec((rows, span), lambda g, p, b: (0, g * steps + p))]
+            + [pl.BlockSpec((x.shape[0], DH), lambda g, p, b: (0, g)) for x in pieces]
+            + [pl.BlockSpec((x.shape[0], DH), lambda g, p, b: (0, KVH + g)) for x in pieces],
             out_specs=pl.BlockSpec((rows, span), lambda g, p, b: (0, g * steps + p)),
-            scratch_shapes=[pltpu.VMEM((DH, seq), BF16)]
+            scratch_shapes=[pltpu.VMEM((seq, DH), BF16), pltpu.VMEM((DH, seq), BF16)]
             + [pltpu.VMEM((seq, 2 * rows), F32)] * PAIRS,
         ),
         compiler_params=pltpu.CompilerParams(
-            dimension_semantics=("arbitrary", "arbitrary"), vmem_limit_bytes=VMEM
+            dimension_semantics=("arbitrary", "arbitrary"), vmem_limit_bytes=24 << 20
         ),
         cost_estimate=pl.CostEstimate(
             flops=4 * rows * seq * HQ * DH,
-            bytes_accessed=4 * queries.size + 2 * keys_values.size,
+            bytes_accessed=4 * queries.size + 4 * seq * KVH * DH,
             transcendentals=rows * seq * HQ,
         ),
         name="attention",
-    )(block, queries, keys_values, keys_values)
+    )(block, queries, *pieces, *pieces)
+
+
+def shift_x(rows, step):
+    pairs = [
+        (x * RING + y, (x + step) % RING * RING + y) for x in range(RING) for y in range(RING)
+    ]
+    return lax.ppermute(rows, "ctx", pairs)
+
+
+def shift_y(rows, step):
+    pairs = [
+        (x * RING + y, x * RING + (y + step) % RING) for x in range(RING) for y in range(RING)
+    ]
+    return lax.ppermute(rows, "ctx", pairs)
+
+
+def gather_far(rows, shift):
+    half = rows.shape[0] // 2
+    before, after = shift(rows, 1), shift(rows, -1)
+    return [rows, before, after, shift(before[:half], 1), shift(after[half:], -1)]
+
+
+def gather_near(rows, shift):
+    return jnp.concatenate([rows, shift(rows, 1), shift(rows, -1), shift(rows, 2)], axis=0)
 
 
 def per_device(
     queries, keys, values, hidden, expert_ids, gate_probs, norm_gain, w_gate, w_up, w_down
 ):
     experts = lax.axis_size("ep")
-    width = hidden.shape[2]
-    shards = jnp.concatenate([w_gate[0], w_up[0], w_down[0]], axis=1)
-    weights = lax.all_gather(shards, "ctx", axis=0, tiled=True)
-
-    outgoing, place = dispatch(hidden[0], expert_ids[0].T, norm_gain[None], experts)
-    keys_values = jnp.concatenate([keys[0], values[0]], axis=1)
-    outgoing, keys_values = lax.optimization_barrier((outgoing, keys_values))
-    keys_values = lax.all_gather(keys_values, "ctx", axis=0, tiled=True)
 
     def exchange(rows):
         moved = lax.all_to_all(
@@ -307,11 +325,21 @@
         )
         return moved.reshape(rows.shape)
 
-    produced = expert(exchange(outgoing), weights)
-    produced, queries = lax.optimization_barrier((produced, queries))
+    outgoing, place = dispatch(hidden[0], expert_ids[0].T, norm_gain[None], experts)
+    outgoing, *shards = lax.optimization_barrier((outgoing, w_gate, w_up, w_down))
+    received = exchange(outgoing)
+    shards = jnp.concatenate([shard[0] for shard in shards], axis=1)
+    half = shards.shape[0] // 2
+    pieces = gather_far(gather_near(shards[:half], shift_y), shift_x)
+    pieces += gather_far(gather_near(shards[half:], shift_x), shift_y)
+    produced = expert(received, pieces)
+
+    produced, keys, values = lax.optimization_barrier((produced, keys, values))
     returned = exchange(produced)
+    keys_values = jnp.concatenate([keys[0], values[0]], axis=1)
+    pieces = gather_far(gather_near(keys_values, shift_y), shift_x)
     block = lax.axis_index("ctx").astype(jnp.int32)[None]
-    attended = attention(block, queries[0], keys_values)
+    attended = attention(block, queries[0], pieces)
     mixed = combine(returned, place, gate_probs[0].T)
     return (attended[None], mixed[None])
 

time: 217 us -> 209 us (0.963)
  blocking collectives: 95.2 us -> 0 us
  starting transfers between devices: 13.4 us -> 96.7 us
  between operations: 14.2 us -> 1.14 us
  Pallas kernels: 18.2 us -> 29.2 us
  local copies, waits for them, and re-layouts: 1.62 us -> 6.48 us
  waiting for transfers between devices: 71.3 us -> 74 us
  other arithmetic: 2.68 us -> 0.24 us
    all_to_all x1 -> x0, blocking collectives: 95.2 us -> none  [exchange(): lax.all_to_all(rows.reshape(experts, WHOLE, rows.shape[1]), 'ep', split_a...]
    ppermute x0 -> x21, starting transfers between devices: none -> 65.9 us  [the longest x11 37 us: shift_x(): return lax.ppermute(rows, 'ctx', pairs)]
    all_gather x2 -> x0, waiting for transfers between devices: 64 us -> none  [the longest x1 62.1 us: per_device(): keys_values = lax.all_gather(keys_values, 'ctx', axis=0, tiled=True)]
    ppermute x0 -> x21, waiting for transfers between devices: none -> 55.5 us  [the longest x11 44.7 us: shift_x(): return lax.ppermute(rows, 'ctx', pairs)]
    all_to_all x1 -> x2, starting transfers between devices: 13.2 us -> 30.8 us  [exchange(): lax.all_to_all(rows.reshape(experts, WHOLE, rows.shape[1]), 'ep', split_a...]
    all_to_all x1 -> x2, waiting for transfers between devices: 6.82 us -> 18.5 us  [exchange(): lax.all_to_all(rows.reshape(experts, WHOLE, rows.shape[1]), 'ep', split_a...]
    pallas_call x1, Pallas kernels: 6.58 us -> 16 us  [attention(): pl.pallas_call(attention_kernel, out_shape=jax.ShapeDtypeStruct(queries.s...]
    unnamed x16 -> x40, local copies, waits for them, and re-layouts: 1.62 us -> 4.84 us
  transfers between devices with their start and end apart: 3 -> 23, of which waited for: 3 -> 13; matrix products, arithmetic and copies ran while one was open for 0% -> 1% of each run, Pallas kernels for 3% -> 8%
where the time goes in v2:
time: 209 us; the launch traced here: 208 us
  starting transfers between devices  96.7 us (46%)
  waiting for transfers between devices  74 us (35%)
  Pallas kernels  29.2 us (14%)
  local copies, waits for them, and re-layouts  6.48 us (3%)
    ppermute x11, waiting for transfers between devices, shift_x(): return lax.ppermute(rows, 'ctx', pairs)  44.7 us
    ppermute x11, starting transfers between devices, shift_x(): return lax.ppermute(rows, 'ctx', pairs)  37 us
    all_to_all x2, starting transfers between devices, exchange(): lax.all_to_all(rows.reshape(experts, WHOLE, rows.shape[1]), 'ep', split_a...  30.8 us
    ppermute x10, starting transfers between devices, shift_y(): return lax.ppermute(rows, 'ctx', pairs)  28.9 us
    all_to_all x2, waiting for transfers between devices, exchange(): lax.all_to_all(rows.reshape(experts, WHOLE, rows.shape[1]), 'ep', split_a...  18.5 us
    pallas_call x1, Pallas kernels, attention(): pl.pallas_call(attention_kernel, out_shape=jax.ShapeDtypeStruct(queries.s...  16 us
    ppermute x10, waiting for transfers between devices, shift_y(): return lax.ppermute(rows, 'ctx', pairs)  10.8 us
    pallas_call x1, Pallas kernels, expert(): pl.pallas_call(expert_kernel, out_shape=jax.ShapeDtypeStruct(rows.shape,...  9.33 us
  transfers between devices with their start and end apart: 23, of which 13 were waited for; matrix products, arithmetic and copies ran while one was open for 1% of the time, Pallas kernels for 8%

profile of v2, /device:TPU:1, one launch (start us, length us, event | category | flops | bytes accessed | tf_op | source)
XLA Modules:
  0.0 207.8 jit_solution(3319467642702739620)
XLA Ops:
  3.0 2.1 %dispatch.1 = (bf16[256,3072]{1,0:T(8,128)(2,1)}, s32[8,128]{1,0:T(8,128)S(1)}) custom-call(bf16[128,2048]{1,0:T(8,128)(2,1)S(1)} %bitcast.22, s32[2,128]{1,0:T(2,128)S(1)} %bitcast.24, f32[1,2048]{1,0:T(1,128)S(1)} %bitcast.23), custom_call_target="tpu_custom_call" | custom-call | tf_op jit(solution)/shard_map/dispatch/pallas_call | solution.py:76
  5.1 16.9 %all-to-all-start = ((bf16[32,8,3072]{2,1,0:T(8,128)(2,1)}), bf16[32,8,3072]{2,1,0:T(8,128)(2,1)S(1)}, u32[]{:S(2)}, u32[]{:S(2)}) async-start(bf16[32,8,3072]{2,1,0:T(8,128)(2,1)} %bitcast.6), calls=%async_computation | async-start | bytes 3145728 | tf_op jit(solution)/shard_map/all_to_all | solution.py:323
  22.2 4.8 %collective-permute-start.2 = (bf16[24,6144]{1,0:T(8,128)(2,1)S(1)}, bf16[24,6144]{1,0:T(8,128)(2,1)S(1)}, u32[]{:S(2)}, u32[]{:S(2)}) collective-permute-start(bf16[24,6144]{1,0:T(8,128)(2,1)S(1)} %get-tuple-element.21), channel_id=1, source_target_pairs={{0,64},{32,96},{64,0},{96,32},{128,192},{160,224},{192,128},{224,1... | collective-permute-start | bytes 884744 | tf_op jit(solution)/shard_map/ppermute | solution.py:304
  27.0 2.7 %collective-permute-start.1 = (bf16[24,6144]{1,0:T(8,128)(2,1)S(1)}, bf16[24,6144]{1,0:T(8,128)(2,1)S(1)}, u32[]{:S(2)}, u32[]{:S(2)}) collective-permute-start(bf16[24,6144]{1,0:T(8,128)(2,1)S(1)} %get-tuple-element.21), channel_id=1, source_target_pairs={{0,96},{32,0},{64,32},{96,64},{128,224},{160,128},{192,160},{224,1... | collective-permute-start | bytes 884744 | tf_op jit(solution)/shard_map/ppermute | solution.py:304
  29.7 2.6 %collective-permute-start = (bf16[24,6144]{1,0:T(8,128)(2,1)S(1)}, bf16[24,6144]{1,0:T(8,128)(2,1)S(1)}, u32[]{:S(2)}, u32[]{:S(2)}) collective-permute-start(bf16[24,6144]{1,0:T(8,128)(2,1)S(1)} %get-tuple-element.21), channel_id=1, source_target_pairs={{0,32},{32,64},{64,96},{96,0},{128,160},{160,192},{192,224},{224,1... | collective-permute-start | bytes 884744 | tf_op jit(solution)/shard_map/ppermute | solution.py:304
  32.3 4.7 %collective-permute-start.9 = (bf16[24,6144]{1,0:T(8,128)(2,1)S(1)}, bf16[24,6144]{1,0:T(8,128)(2,1)S(1)}, u32[]{:S(2)}, u32[]{:S(2)}) collective-permute-start(bf16[24,6144]{1,0:T(8,128)(2,1)S(1)} %get-tuple-element.20), channel_id=1, source_target_pairs={{0,256},{32,288},{64,320},{96,352},{128,384},{160,416},{192,448},{... | collective-permute-start | bytes 884744 | tf_op jit(solution)/shard_map/ppermute | solution.py:297
  37.0 2.8 %collective-permute-start.8 = (bf16[24,6144]{1,0:T(8,128)(2,1)S(1)}, bf16[24,6144]{1,0:T(8,128)(2,1)S(1)}, u32[]{:S(2)}, u32[]{:S(2)}) collective-permute-start(bf16[24,6144]{1,0:T(8,128)(2,1)S(1)} %get-tuple-element.20), channel_id=1, source_target_pairs={{0,384},{32,416},{64,448},{96,480},{128,0},{160,32},{192,64},{224,... | collective-permute-start | bytes 884744 | tf_op jit(solution)/shard_map/ppermute | solution.py:297
  39.7 2.5 %collective-permute-start.7 = (bf16[24,6144]{1,0:T(8,128)(2,1)S(1)}, bf16[24,6144]{1,0:T(8,128)(2,1)S(1)}, u32[]{:S(2)}, u32[]{:S(2)}) collective-permute-start(bf16[24,6144]{1,0:T(8,128)(2,1)S(1)} %get-tuple-element.20), channel_id=1, source_target_pairs={{0,128},{32,160},{64,192},{96,224},{128,256},{160,288},{192,320},{... | collective-permute-start | bytes 884744 | tf_op jit(solution)/shard_map/ppermute | solution.py:297
  42.4 4.0 %collective-permute-start.4 = (bf16[96,6144]{1,0:T(8,128)(2,1)S(1)}, bf16[96,6144]{1,0:T(8,128)(2,1)S(1)}, u32[]{:S(2)}, u32[]{:S(2)}) collective-permute-start(bf16[96,6144]{1,0:T(8,128)(2,1)S(1)} %pad_maximum_fusion.refs_0_), channel_id=1, source_target_pairs={{0,384},{32,416},{64,448},{96,480},{128,0},{160,32},{192,64},{224,... | collective-permute-start | bytes 3538952 | tf_op jit(solution)/shard_map/ppermute | solution.py:297
  46.4 1.9 collective-permute-start.3
  50.1 3.9 %collective-permute-start.11 = (bf16[96,6144]{1,0:T(8,128)(2,1)S(1)}, bf16[96,6144]{1,0:T(8,128)(2,1)S(1)}, u32[]{:S(2)}, u32[]{:S(2)}) collective-permute-start(bf16[96,6144]{1,0:T(8,128)(2,1)S(1)} %pad_maximum_fusion.1.refs_5_), channel_id=1, source_target_pairs={{0,96},{32,0},{64,32},{96,64},{128,224},{160,128},{192,160},{224,1... | collective-permute-start | bytes 3538952 | tf_op jit(solution)/shard_map/ppermute | solution.py:304
  54.0 1.9 collective-permute-start.10
  55.9 19.4 %collective-permute-done.4.refs_2_ = bf16[96,6144]{1,0:T(8,128)(2,1)S(1)} collective-permute-done((bf16[96,6144]{1,0:T(8,128)(2,1)S(1)}, bf16[96,6144]{1,0:T(8,128)(2,1)S(1)}, u32[]{:S(2)}, u32[]{:S(2)}) %collective-permute-start.4) | collective-permute-done | bytes 1179680 | tf_op jit(solution)/shard_map/ppermute | solution.py:297
  75.3 5.3 %collective-permute-start.6 = (bf16[48,6144]{1,0:T(8,128)(2,1)S(1)}, bf16[48,6144]{1,0:T(8,128)(2,1)S(1)}, u32[]{:S(2)}, u32[]{:S(2)}) collective-permute-start(bf16[48,6144]{1,0:T(8,128)(2,1)S(1)} %slice.34), channel_id=1, source_target_pairs={{0,384},{32,416},{64,448},{96,480},{128,0},{160,32},{192,64},{224,... | collective-permute-start | bytes 1769480 | tf_op jit(solution)/shard_map/ppermute | solution.py:297
  82.8 3.9 %collective-permute-start.13 = (bf16[48,6144]{1,0:T(8,128)(2,1)S(1)}, bf16[48,6144]{1,0:T(8,128)(2,1)S(1)}, u32[]{:S(2)}, u32[]{:S(2)}) collective-permute-start(bf16[48,6144]{1,0:T(8,128)(2,1)S(1)} %slice.37), channel_id=1, source_target_pairs={{0,96},{32,0},{64,32},{96,64},{128,224},{160,128},{192,160},{224,1... | collective-permute-start | bytes 1769480 | tf_op jit(solution)/shard_map/ppermute | solution.py:304
  86.7 1.9 collective-permute-start.12
  88.7 4.2 %collective-permute-done.6.refs_4_ = bf16[48,6144]{1,0:T(8,128)(2,1)S(1)} collective-permute-done((bf16[48,6144]{1,0:T(8,128)(2,1)S(1)}, bf16[48,6144]{1,0:T(8,128)(2,1)S(1)}, u32[]{:S(2)}, u32[]{:S(2)}) %collective-permute-start.6) | collective-permute-done | bytes 589856 | tf_op jit(solution)/shard_map/ppermute | solution.py:297
  92.9 5.2 %collective-permute-done.5.refs_3_ = bf16[48,6144]{1,0:T(8,128)(2,1)S(1)} collective-permute-done((bf16[48,6144]{1,0:T(8,128)(2,1)S(1)}, bf16[48,6144]{1,0:T(8,128)(2,1)S(1)}, u32[]{:S(2)}, u32[]{:S(2)}) %collective-permute-start.5) | collective-permute-done | bytes 589856 | tf_op jit(solution)/shard_map/ppermute | solution.py:297
  98.8 4.9 %collective-permute-done.12.refs_8_ = bf16[48,6144]{1,0:T(8,128)(2,1)} collective-permute-done((bf16[48,6144]{1,0:T(8,128)(2,1)S(1)}, bf16[48,6144]{1,0:T(8,128)(2,1)}, u32[]{:S(2)}, u32[]{:S(2)}) %collective-permute-start.12) | collective-permute-done | bytes 589856 | tf_op jit(solution)/shard_map/ppermute | solution.py:304
  104.9 9.3 %expert.1 = bf16[256,3072]{1,0:T(8,128)(2,1)} custom-call(bf16[256,3072]{1,0:T(8,128)(2,1)} %bitcast.27, bf16[96,6144]{1,0:T(8,128)(2,1)} %copy-done.6, bf16[96,6144]{1,0:T(8,128)(2,1)} %copy-done.9, bf16[96,6144]{1,0:T(8,128)(2,1)} %copy-done.8, bf16[48,6144]{1,0:T(8,128)(2,1)} %copy-done.18, bf16[48,6144]{1,0:T(8,128)(2,1)} %copy-done.17, ...), custom_call_target="tpu_custom_call" | custom-call | flops 3623878656 | bytes 12582912 | tf_op jit(solution)/shard_map/expert/pallas_call | solution.py:138
  114.3 13.9 %all-to-all-start.1 = ((bf16[32,8,3072]{2,1,0:T(8,128)(2,1)}), bf16[32,8,3072]{2,1,0:T(8,128)(2,1)S(1)}, u32[]{:S(2)}, u32[]{:S(2)}) async-start(bf16[32,8,3072]{2,1,0:T(8,128)(2,1)} %bitcast.28), calls=%async_computation.1 | async-start | bytes 3145728 | tf_op jit(solution)/shard_map/all_to_all | solution.py:323
  130.2 3.1 %collective-permute-start.15 = (bf16[128,512]{1,0:T(8,128)(2,1)S(1)}, bf16[128,512]{1,0:T(8,128)(2,1)S(1)}, u32[]{:S(2)}, u32[]{:S(2)}) collective-permute-start(bf16[128,512]{1,0:T(8,128)(2,1)S(1)} %pad_maximum_fusion.4), channel_id=1, source_target_pairs={{0,96},{32,0},{64,32},{96,64},{128,224},{160,128},{192,160},{224,1... | collective-permute-start | bytes 393224 | tf_op jit(solution)/shard_map/ppermute | solution.py:304
  133.3 2.2 %collective-permute-start.14 = (bf16[128,512]{1,0:T(8,128)(2,1)S(1)}, bf16[128,512]{1,0:T(8,128)(2,1)S(1)}, u32[]{:S(2)}, u32[]{:S(2)}) collective-permute-start(bf16[128,512]{1,0:T(8,128)(2,1)S(1)} %pad_maximum_fusion.4), channel_id=1, source_target_pairs={{0,32},{32,64},{64,96},{96,0},{128,160},{160,192},{192,224},{224,1... | collective-permute-start | bytes 393224 | tf_op jit(solution)/shard_map/ppermute | solution.py:304
  136.9 3.7 %collective-permute-done.14 = bf16[128,512]{1,0:T(8,128)(2,1)S(1)} collective-permute-done((bf16[128,512]{1,0:T(8,128)(2,1)S(1)}, bf16[128,512]{1,0:T(8,128)(2,1)S(1)}, u32[]{:S(2)}, u32[]{:S(2)}) %collective-permute-start.14) | collective-permute-done | bytes 131104 | tf_op jit(solution)/shard_map/ppermute | solution.py:304
  140.6 4.6 %collective-permute-start.18 = (bf16[512,512]{1,0:T(8,128)(2,1)S(1)}, bf16[512,512]{1,0:T(8,128)(2,1)S(1)}, u32[]{:S(2)}, u32[]{:S(2)}) collective-permute-start(bf16[512,512]{1,0:T(8,128)(2,1)S(1)} %pad_maximum_fusion.3.refs_0_.refs_5_), channel_id=1, source_target_pairs={{0,384},{32,416},{64,448},{96,480},{128,0},{160,32},{192,64},{224,... | collective-permute-start | bytes 1572872 | tf_op jit(solution)/shard_map/ppermute | solution.py:297
  145.2 1.9 collective-permute-start.17
  147.1 7.6 %collective-permute-done.18.refs_2_.refs_7_ = bf16[512,512]{1,0:T(8,128)(2,1)S(1)} collective-permute-done((bf16[512,512]{1,0:T(8,128)(2,1)S(1)}, bf16[512,512]{1,0:T(8,128)(2,1)S(1)}, u32[]{:S(2)}, u32[]{:S(2)}) %collective-permute-start.18) | collective-permute-done | bytes 524320 | tf_op jit(solution)/shard_map/ppermute | solution.py:297
  155.4 5.3 %collective-permute-start.20 = (bf16[256,512]{1,0:T(8,128)(2,1)}, bf16[256,512]{1,0:T(8,128)(2,1)S(1)}, u32[]{:S(2)}, u32[]{:S(2)}) collective-permute-start(bf16[256,512]{1,0:T(8,128)(2,1)} %slice.39), channel_id=1, source_target_pairs={{0,384},{32,416},{64,448},{96,480},{128,0},{160,32},{192,64},{224,... | collective-permute-start | bytes 786440 | tf_op jit(solution)/shard_map/ppermute | solution.py:297
  161.5 2.1 %collective-permute-start.19 = (bf16[256,512]{1,0:T(8,128)(2,1)}, bf16[256,512]{1,0:T(8,128)(2,1)}, u32[]{:S(2)}, u32[]{:S(2)}) collective-permute-start(bf16[256,512]{1,0:T(8,128)(2,1)} %slice.38), channel_id=1, source_target_pairs={{0,128},{32,160},{64,192},{96,224},{128,256},{160,288},{192,320},{... | collective-permute-start | bytes 786440 | tf_op jit(solution)/shard_map/ppermute | solution.py:297
  164.4 5.9 %collective-permute-done.19.refs_3_.refs_8_ = bf16[256,512]{1,0:T(8,128)(2,1)} collective-permute-done((bf16[256,512]{1,0:T(8,128)(2,1)}, bf16[256,512]{1,0:T(8,128)(2,1)}, u32[]{:S(2)}, u32[]{:S(2)}) %collective-permute-start.19) | collective-permute-done | bytes 262176 | tf_op jit(solution)/shard_map/ppermute | solution.py:297
  171.5 16.0 %attention.1 = bf16[128,4096]{1,0:T(8,128)(2,1)} custom-call(s32[1]{0:T(128)} %bitcast.block_ref, bf16[128,4096]{1,0:T(8,128)(2,1)S(1)} %bitcast.26, bf16[512,512]{1,0:T(8,128)(2,1)S(1)} %pad_maximum_fusion.3.refs_0_.refs_5_, bf16[512,512]{1,0:T(8,128)(2,1)S(1)} %collective-permute-done.17.refs_1_.refs_6_, ...), custom_call_target="tpu_custom_call" | custom-call | flops 4294967296 | bytes 4194304 | tf_op jit(solution)/shard_map/attention/pallas_call | solution.py:268
  187.6 18.5 %all-to-all-done.1 = bf16[32,8,3072]{2,1,0:T(8,128)(2,1)S(1)} async-done(((bf16[32,8,3072]{2,1,0:T(8,128)(2,1)}), bf16[32,8,3072]{2,1,0:T(8,128)(2,1)S(1)}, u32[]{:S(2)}, u32[]{:S(2)}) %all-to-all-start.1) | async-done | bytes 1572896 | tf_op jit(solution)/shard_map/all_to_all | solution.py:323
  (70 shorter events, 17.1 us)
Async XLA Ops:
  5.1 16.9 %copy-start.14 = (bf16[1,48,2048]{2,1,0:T(8,128)(2,1)S(1)}, bf16[1,48,2048]{2,1,0:T(8,128)(2,1)}, u32[]{:S(2)}) copy-start(bf16[1,48,2048]{2,1,0:T(8,128)(2,1)} %param.19) | copy-start | bytes 589828
  5.1 16.9 %copy-start.15 = (bf16[1,48,2048]{2,1,0:T(8,128)(2,1)S(1)}, bf16[1,48,2048]{2,1,0:T(8,128)(2,1)}, u32[]{:S(2)}) copy-start(bf16[1,48,2048]{2,1,0:T(8,128)(2,1)} %param.18) | copy-start | bytes 589828
  5.1 16.9 %copy-start.16 = (bf16[1,48,2048]{2,1,0:T(8,128)(2,1)S(1)}, bf16[1,48,2048]{2,1,0:T(8,128)(2,1)}, u32[]{:S(2)}) copy-start(bf16[1,48,2048]{2,1,0:T(8,128)(2,1)} %param.17) | copy-start | bytes 589828
  5.1 98.6 %all-to-all-start = ((bf16[32,8,3072]{2,1,0:T(8,128)(2,1)}), bf16[32,8,3072]{2,1,0:T(8,128)(2,1)S(1)}, u32[]{:S(2)}, u32[]{:S(2)}) async-start(bf16[32,8,3072]{2,1,0:T(8,128)(2,1)} %bitcast.6), calls=%async_computation | async-start | bytes 3145728 | tf_op jit(solution)/shard_map/all_to_all | solution.py:323
  22.2 17.6 %collective-permute-start.2 = (bf16[24,6144]{1,0:T(8,128)(2,1)S(1)}, bf16[24,6144]{1,0:T(8,128)(2,1)S(1)}, u32[]{:S(2)}, u32[]{:S(2)}) collective-permute-start(bf16[24,6144]{1,0:T(8,128)(2,1)S(1)} %get-tuple-element.21), channel_id=1, source_target_pairs={{0,64},{32,96},{64,0},{96,32},{128,192},{160,224},{192,128},{224,1... | collective-permute-start | bytes 884744 | tf_op jit(solution)/shard_map/ppermute | solution.py:304
  27.0 15.3 %collective-permute-start.1 = (bf16[24,6144]{1,0:T(8,128)(2,1)S(1)}, bf16[24,6144]{1,0:T(8,128)(2,1)S(1)}, u32[]{:S(2)}, u32[]{:S(2)}) collective-permute-start(bf16[24,6144]{1,0:T(8,128)(2,1)S(1)} %get-tuple-element.21), channel_id=1, source_target_pairs={{0,96},{32,0},{64,32},{96,64},{128,224},{160,128},{192,160},{224,1... | collective-permute-start | bytes 884744 | tf_op jit(solution)/shard_map/ppermute | solution.py:304
  29.7 12.6 %collective-permute-start = (bf16[24,6144]{1,0:T(8,128)(2,1)S(1)}, bf16[24,6144]{1,0:T(8,128)(2,1)S(1)}, u32[]{:S(2)}, u32[]{:S(2)}) collective-permute-start(bf16[24,6144]{1,0:T(8,128)(2,1)S(1)} %get-tuple-element.21), channel_id=1, source_target_pairs={{0,32},{32,64},{64,96},{96,0},{128,160},{160,192},{192,224},{224,1... | collective-permute-start | bytes 884744 | tf_op jit(solution)/shard_map/ppermute | solution.py:304
  32.3 16.0 %collective-permute-start.9 = (bf16[24,6144]{1,0:T(8,128)(2,1)S(1)}, bf16[24,6144]{1,0:T(8,128)(2,1)S(1)}, u32[]{:S(2)}, u32[]{:S(2)}) collective-permute-start(bf16[24,6144]{1,0:T(8,128)(2,1)S(1)} %get-tuple-element.20), channel_id=1, source_target_pairs={{0,256},{32,288},{64,320},{96,352},{128,384},{160,416},{192,448},{... | collective-permute-start | bytes 884744 | tf_op jit(solution)/shard_map/ppermute | solution.py:297
  37.0 13.1 %collective-permute-start.8 = (bf16[24,6144]{1,0:T(8,128)(2,1)S(1)}, bf16[24,6144]{1,0:T(8,128)(2,1)S(1)}, u32[]{:S(2)}, u32[]{:S(2)}) collective-permute-start(bf16[24,6144]{1,0:T(8,128)(2,1)S(1)} %get-tuple-element.20), channel_id=1, source_target_pairs={{0,384},{32,416},{64,448},{96,480},{128,0},{160,32},{192,64},{224,... | collective-permute-start | bytes 884744 | tf_op jit(solution)/shard_map/ppermute | solution.py:297
  39.7 10.3 %collective-permute-start.7 = (bf16[24,6144]{1,0:T(8,128)(2,1)S(1)}, bf16[24,6144]{1,0:T(8,128)(2,1)S(1)}, u32[]{:S(2)}, u32[]{:S(2)}) collective-permute-start(bf16[24,6144]{1,0:T(8,128)(2,1)S(1)} %get-tuple-element.20), channel_id=1, source_target_pairs={{0,128},{32,160},{64,192},{96,224},{128,256},{160,288},{192,320},{... | collective-permute-start | bytes 884744 | tf_op jit(solution)/shard_map/ppermute | solution.py:297
  42.4 33.0 %copy-start.6 = (bf16[96,6144]{1,0:T(8,128)(2,1)}, bf16[96,6144]{1,0:T(8,128)(2,1)S(1)}, u32[]{:S(2)}) copy-start(bf16[96,6144]{1,0:T(8,128)(2,1)S(1)} %pad_maximum_fusion.refs_0_) | copy-start | bytes 3538948
  42.4 32.9 %collective-permute-start.4 = (bf16[96,6144]{1,0:T(8,128)(2,1)S(1)}, bf16[96,6144]{1,0:T(8,128)(2,1)S(1)}, u32[]{:S(2)}, u32[]{:S(2)}) collective-permute-start(bf16[96,6144]{1,0:T(8,128)(2,1)S(1)} %pad_maximum_fusion.refs_0_), channel_id=1, source_target_pairs={{0,384},{32,416},{64,448},{96,480},{128,0},{160,32},{192,64},{224,... | collective-permute-start | bytes 3538952 | tf_op jit(solution)/shard_map/ppermute | solution.py:297
  46.4 34.3 %collective-permute-start.3 = (bf16[96,6144]{1,0:T(8,128)(2,1)S(1)}, bf16[96,6144]{1,0:T(8,128)(2,1)S(1)}, u32[]{:S(2)}, u32[]{:S(2)}) collective-permute-start(bf16[96,6144]{1,0:T(8,128)(2,1)S(1)} %pad_maximum_fusion.refs_0_), channel_id=1, source_target_pairs={{0,128},{32,160},{64,192},{96,224},{128,256},{160,288},{192,320},{... | collective-permute-start | bytes 3538952 | tf_op jit(solution)/shard_map/ppermute | solution.py:297
  50.1 30.6 %copy-start.7 = (bf16[96,6144]{1,0:T(8,128)(2,1)}, bf16[96,6144]{1,0:T(8,128)(2,1)S(1)}, u32[]{:S(2)}) copy-start(bf16[96,6144]{1,0:T(8,128)(2,1)S(1)} %pad_maximum_fusion.1.refs_5_) | copy-start | bytes 3538948
  50.1 32.6 %collective-permute-start.11 = (bf16[96,6144]{1,0:T(8,128)(2,1)S(1)}, bf16[96,6144]{1,0:T(8,128)(2,1)S(1)}, u32[]{:S(2)}, u32[]{:S(2)}) collective-permute-start(bf16[96,6144]{1,0:T(8,128)(2,1)S(1)} %pad_maximum_fusion.1.refs_5_), channel_id=1, source_target_pairs={{0,96},{32,0},{64,32},{96,64},{128,224},{160,128},{192,160},{224,1... | collective-permute-start | bytes 3538952 | tf_op jit(solution)/shard_map/ppermute | solution.py:304
  54.0 32.7 %collective-permute-start.10 = (bf16[96,6144]{1,0:T(8,128)(2,1)S(1)}, bf16[96,6144]{1,0:T(8,128)(2,1)S(1)}, u32[]{:S(2)}, u32[]{:S(2)}) collective-permute-start(bf16[96,6144]{1,0:T(8,128)(2,1)S(1)} %pad_maximum_fusion.1.refs_5_), channel_id=1, source_target_pairs={{0,32},{32,64},{64,96},{96,0},{128,160},{160,192},{192,224},{224,1... | collective-permute-start | bytes 3538952 | tf_op jit(solution)/shard_map/ppermute | solution.py:304
  75.3 17.5 %collective-permute-start.6 = (bf16[48,6144]{1,0:T(8,128)(2,1)S(1)}, bf16[48,6144]{1,0:T(8,128)(2,1)S(1)}, u32[]{:S(2)}, u32[]{:S(2)}) collective-permute-start(bf16[48,6144]{1,0:T(8,128)(2,1)S(1)} %slice.34), channel_id=1, source_target_pairs={{0,384},{32,416},{64,448},{96,480},{128,0},{160,32},{192,64},{224,... | collective-permute-start | bytes 1769480 | tf_op jit(solution)/shard_map/ppermute | solution.py:297
  80.8 17.3 %collective-permute-start.5 = (bf16[48,6144]{1,0:T(8,128)(2,1)S(1)}, bf16[48,6144]{1,0:T(8,128)(2,1)S(1)}, u32[]{:S(2)}, u32[]{:S(2)}) collective-permute-start(bf16[48,6144]{1,0:T(8,128)(2,1)S(1)} %slice.33), channel_id=1, source_target_pairs={{0,128},{32,160},{64,192},{96,224},{128,256},{160,288},{192,320},{... | collective-permute-start | bytes 1769480 | tf_op jit(solution)/shard_map/ppermute | solution.py:297
  82.8 16.1 %collective-permute-start.13 = (bf16[48,6144]{1,0:T(8,128)(2,1)S(1)}, bf16[48,6144]{1,0:T(8,128)(2,1)S(1)}, u32[]{:S(2)}, u32[]{:S(2)}) collective-permute-start(bf16[48,6144]{1,0:T(8,128)(2,1)S(1)} %slice.37), channel_id=1, source_target_pairs={{0,96},{32,0},{64,32},{96,64},{128,224},{160,128},{192,160},{224,1... | collective-permute-start | bytes 1769480 | tf_op jit(solution)/shard_map/ppermute | solution.py:304
  86.7 12.2 %copy-start.11 = (bf16[96,6144]{1,0:T(8,128)(2,1)}, bf16[96,6144]{1,0:T(8,128)(2,1)S(1)}, u32[]{:S(2)}) copy-start(bf16[96,6144]{1,0:T(8,128)(2,1)S(1)} %collective-permute-done.10.refs_6_) | copy-start | bytes 3538948
  86.7 17.0 %collective-permute-start.12 = (bf16[48,6144]{1,0:T(8,128)(2,1)S(1)}, bf16[48,6144]{1,0:T(8,128)(2,1)}, u32[]{:S(2)}, u32[]{:S(2)}) collective-permute-start(bf16[48,6144]{1,0:T(8,128)(2,1)S(1)} %slice.36), channel_id=1, source_target_pairs={{0,32},{32,64},{64,96},{96,0},{128,160},{160,192},{192,224},{224,1... | collective-permute-start | bytes 1769480 | tf_op jit(solution)/shard_map/ppermute | solution.py:304
  114.2 14.0 %copy-start.12 = (bf16[1,128,256]{2,1,0:T(8,128)(2,1)S(1)}, bf16[1,128,256]{2,1,0:T(8,128)(2,1)}, u32[]{:S(2)}) copy-start(bf16[1,128,256]{2,1,0:T(8,128)(2,1)} %param.12) | copy-start | bytes 196612
  114.3 14.0 %copy-start.13 = (bf16[1,128,256]{2,1,0:T(8,128)(2,1)S(1)}, bf16[1,128,256]{2,1,0:T(8,128)(2,1)}, u32[]{:S(2)}) copy-start(bf16[1,128,256]{2,1,0:T(8,128)(2,1)} %param.11) | copy-start | bytes 196612
  114.3 91.8 %all-to-all-start.1 = ((bf16[32,8,3072]{2,1,0:T(8,128)(2,1)}), bf16[32,8,3072]{2,1,0:T(8,128)(2,1)S(1)}, u32[]{:S(2)}, u32[]{:S(2)}) async-start(bf16[32,8,3072]{2,1,0:T(8,128)(2,1)} %bitcast.28), calls=%async_computation.1 | async-start | bytes 3145728 | tf_op jit(solution)/shard_map/all_to_all | solution.py:323
  128.2 8.3 %collective-permute-start.16 = (bf16[128,512]{1,0:T(8,128)(2,1)S(1)}, bf16[128,512]{1,0:T(8,128)(2,1)S(1)}, u32[]{:S(2)}, u32[]{:S(2)}) collective-permute-start(bf16[128,512]{1,0:T(8,128)(2,1)S(1)} %pad_maximum_fusion.4), channel_id=1, source_target_pairs={{0,64},{32,96},{64,0},{96,32},{128,192},{160,224},{192,128},{224,1... | collective-permute-start | bytes 393224 | tf_op jit(solution)/shard_map/ppermute | solution.py:304
  130.2 6.8 %collective-permute-start.15 = (bf16[128,512]{1,0:T(8,128)(2,1)S(1)}, bf16[128,512]{1,0:T(8,128)(2,1)S(1)}, u32[]{:S(2)}, u32[]{:S(2)}) collective-permute-start(bf16[128,512]{1,0:T(8,128)(2,1)S(1)} %pad_maximum_fusion.4), channel_id=1, source_target_pairs={{0,96},{32,0},{64,32},{96,64},{128,224},{160,128},{192,160},{224,1... | collective-permute-start | bytes 393224 | tf_op jit(solution)/shard_map/ppermute | solution.py:304
  133.3 7.3 %collective-permute-start.14 = (bf16[128,512]{1,0:T(8,128)(2,1)S(1)}, bf16[128,512]{1,0:T(8,128)(2,1)S(1)}, u32[]{:S(2)}, u32[]{:S(2)}) collective-permute-start(bf16[128,512]{1,0:T(8,128)(2,1)S(1)} %pad_maximum_fusion.4), channel_id=1, source_target_pairs={{0,32},{32,64},{64,96},{96,0},{128,160},{160,192},{192,224},{224,1... | collective-permute-start | bytes 393224 | tf_op jit(solution)/shard_map/ppermute | solution.py:304
  140.6 14.1 %collective-permute-start.18 = (bf16[512,512]{1,0:T(8,128)(2,1)S(1)}, bf16[512,512]{1,0:T(8,128)(2,1)S(1)}, u32[]{:S(2)}, u32[]{:S(2)}) collective-permute-start(bf16[512,512]{1,0:T(8,128)(2,1)S(1)} %pad_maximum_fusion.3.refs_0_.refs_5_), channel_id=1, source_target_pairs={{0,384},{32,416},{64,448},{96,480},{128,0},{160,32},{192,64},{224,... | collective-permute-start | bytes 1572872 | tf_op jit(solution)/shard_map/ppermute | solution.py:297
  145.2 15.5 %collective-permute-start.17 = (bf16[512,512]{1,0:T(8,128)(2,1)S(1)}, bf16[512,512]{1,0:T(8,128)(2,1)S(1)}, u32[]{:S(2)}, u32[]{:S(2)}) collective-permute-start(bf16[512,512]{1,0:T(8,128)(2,1)S(1)} %pad_maximum_fusion.3.refs_0_.refs_5_), channel_id=1, source_target_pairs={{0,128},{32,160},{64,192},{96,224},{128,256},{160,288},{192,320},{... | collective-permute-start | bytes 1572872 | tf_op jit(solution)/shard_map/ppermute | solution.py:297
  155.4 8.9 %collective-permute-start.20 = (bf16[256,512]{1,0:T(8,128)(2,1)}, bf16[256,512]{1,0:T(8,128)(2,1)S(1)}, u32[]{:S(2)}, u32[]{:S(2)}) collective-permute-start(bf16[256,512]{1,0:T(8,128)(2,1)} %slice.39), channel_id=1, source_target_pairs={{0,384},{32,416},{64,448},{96,480},{128,0},{160,32},{192,64},{224,... | collective-permute-start | bytes 786440 | tf_op jit(solution)/shard_map/ppermute | solution.py:297
  161.5 8.8 %collective-permute-start.19 = (bf16[256,512]{1,0:T(8,128)(2,1)}, bf16[256,512]{1,0:T(8,128)(2,1)}, u32[]{:S(2)}, u32[]{:S(2)}) collective-permute-start(bf16[256,512]{1,0:T(8,128)(2,1)} %slice.38), channel_id=1, source_target_pairs={{0,128},{32,160},{64,192},{96,224},{128,256},{160,288},{192,320},{... | collective-permute-start | bytes 786440 | tf_op jit(solution)/shard_map/ppermute | solution.py:297
  171.5 34.5 %copy-start.3 = (f32[1,128,2]{1,2,0:T(2,128)S(1)}, f32[1,128,2]{1,2,0:T(2,128)}, u32[]{:S(2)}) copy-start(f32[1,128,2]{1,2,0:T(2,128)} %param.15) | copy-start | bytes 3076
  (11 other events, 41.8 us)

commit v3 on v2

--- a/solution.py
+++ b/solution.py
@@ -18,6 +18,7 @@
 HIDDEN_STEP = 256
 PAIRS = 4
 VMEM = 16 << 20
+EXPERT_VMEM = 24
 BF16 = jnp.bfloat16
 F32 = jnp.float32
 
@@ -30,14 +31,21 @@
     return lax.dot_general(a, b, (((1,), (1,)), ((), ())), preferred_element_type=F32)
 
 
-def dispatch_kernel(hidden_ref, ids_ref, gain_ref, out_ref, place_ref):
+def dispatch_kernel(hidden_hbm, ids_hbm, gain_hbm, out_ref, place_ref, *scratch):
+    hidden_ref, ids_ref, gain_ref, sems = scratch
+    copies = [
+        pltpu.make_async_copy(source, place, sems.at[index])
+        for index, (source, place) in enumerate(
+            ((ids_hbm, ids_ref), (hidden_hbm, hidden_ref), (gain_hbm, gain_ref))
+        )
+    ]
+    for copy in copies:
+        copy.start()
     rows, width = hidden_ref.shape
     half = width // 2
     experts = out_ref.shape[0] // WHOLE
-    tokens = hidden_ref[...].astype(F32)
-    mean_square = jnp.mean(tokens * tokens, axis=-1, keepdims=True)
-    normed = (tokens * lax.rsqrt(mean_square + 1e-06) * gain_ref[...]).astype(BF16)
-
+
+    copies[0].wait()
     ids = ids_ref[...]
     first, second = ids[0:1, :], ids[1:2, :]
     expert_iota = lax.broadcasted_iota(jnp.int32, (experts, rows), 0)
@@ -63,6 +71,11 @@
     def onehot(targets):
         return ((slot_iota == targets[0]) | (slot_iota == targets[1])).astype(F32).astype(BF16)
 
+    copies[1].wait()
+    copies[2].wait()
+    tokens = hidden_ref[...].astype(F32)
+    mean_square = jnp.mean(tokens * tokens, axis=-1, keepdims=True)
+    normed = (tokens * lax.rsqrt(mean_square + 1e-06) * gain_ref[...]).astype(BF16)
     out_ref[:, :width] = dot(onehot(whole), normed).astype(BF16)
     out_ref[:, width:] = (
         dot(onehot(halves), normed[:, :half])
@@ -79,9 +92,16 @@
             jax.ShapeDtypeStruct((experts * WHOLE, width + width // 2), BF16),
             jax.ShapeDtypeStruct((8, rows), jnp.int32),
         ),
+        in_specs=[pl.BlockSpec(memory_space=pltpu.HBM)] * 3,
+        scratch_shapes=[
+            pltpu.VMEM(hidden.shape, BF16),
+            pltpu.VMEM(ids.shape, jnp.int32),
+            pltpu.VMEM(gain.shape, F32),
+            pltpu.SemaphoreType.DMA((3,)),
+        ],
         compiler_params=pltpu.CompilerParams(vmem_limit_bytes=VMEM),
         name="dispatch",
-    )(hidden, ids, gain)
+    )(*[pltpu.with_memory_space_constraint(x, pltpu.HBM) for x in (hidden, ids, gain)])
 
 
 def expert_kernel(rows_ref, *refs):
@@ -90,14 +110,32 @@
     width = x_ref.shape[1]
     half = width // 2
     hidden = act_ref.shape[1]
-    copies, base = [], 0
-    for index, ref in enumerate(piece_refs):
-        place = w_ref.at[pl.ds(base, ref.shape[0]), :]
-        copies.append((base, pltpu.make_async_copy(ref, place, sems.at[index])))
-        base += ref.shape[0]
-    for _, copy in copies:
-        copy.start()
-
+    steps = range(0, hidden, HIDDEN_STEP)
+
+    waves = [[] for _ in range(len(steps) + 1)]
+    base, used = 0, 0
+    for ref in piece_refs:
+        size = ref.shape[0]
+        spans = [(max(s, base), min(s + HIDDEN_STEP, base + size), 0, 2 * width) for s in steps]
+        spans.append((base, base + size, 2 * width, width))
+        for wave, (low, high, lane, lanes) in zip(waves, spans):
+            if low < high:
+                source = ref.at[pl.ds(low - base, high - low), pl.ds(lane, lanes)]
+                place = w_ref.at[pl.ds(low, high - low), pl.ds(lane, lanes)]
+                wave.append(pltpu.make_async_copy(source, place, sems.at[used]))
+                used += 1
+        base += size
+
+    def start(wave):
+        for copy in waves[wave]:
+            copy.start()
+
+    def finish(wave):
+        for copy in waves[wave]:
+            copy.wait()
+
+    start(0)
+    start(1)
     extra = count // 2
     pick_row = lax.broadcasted_iota(jnp.int32, (extra, count), 0)
     pick_col = lax.broadcasted_iota(jnp.int32, (extra, count), 1)
@@ -107,14 +145,16 @@
         pick = (pick_col == 2 * pick_row + part).astype(F32).astype(BF16)
         x_ref[pl.ds(count, extra), pl.ds(part * half, half)] = dot(pick, tail).astype(BF16)
 
-    for start in range(0, hidden, HIDDEN_STEP):
-        stop = start + HIDDEN_STEP
-        while copies and copies[0][0] < stop:
-            copies.pop(0)[1].wait()
+    for wave, low in enumerate(steps):
+        finish(wave)
+        if wave + 2 <= len(steps):
+            start(wave + 2)
+        at = slice(low, low + HIDDEN_STEP)
         x = x_ref[...]
-        gate_pre = dot_nt(x, w_ref[start:stop, :width])
-        up_pre = dot_nt(x, w_ref[start:stop, width : 2 * width])
-        act_ref[:, start:stop] = (gate_pre / (1.0 + jnp.exp(-gate_pre)) * up_pre).astype(BF16)
+        gate_pre = dot_nt(x, w_ref[at, :width])
+        up_pre = dot_nt(x, w_ref[at, width : 2 * width])
+        act_ref[:, at] = (gate_pre / (1.0 + jnp.exp(-gate_pre)) * up_pre).astype(BF16)
+    finish(len(steps))
     act = act_ref[...]
     piece = width // 4
     for step in range(4):
@@ -139,23 +179,23 @@
         expert_kernel,
         out_shape=jax.ShapeDtypeStruct(rows.shape, BF16),
         in_specs=[pl.BlockSpec(memory_space=pltpu.VMEM)]
-        + [pl.BlockSpec(memory_space=pl.ANY)] * len(pieces),
+        + [pl.BlockSpec(memory_space=pltpu.HBM)] * len(pieces),
         out_specs=pl.BlockSpec(memory_space=pltpu.VMEM),
         scratch_shapes=[
             pltpu.VMEM((total, width), BF16),
             pltpu.VMEM((total - count, width), BF16),
             pltpu.VMEM((total, hidden), BF16),
             pltpu.VMEM((hidden, 3 * width), BF16),
-            pltpu.SemaphoreType.DMA((len(pieces),)),
+            pltpu.SemaphoreType.DMA((4 * len(pieces),)),
         ],
-        compiler_params=pltpu.CompilerParams(vmem_limit_bytes=56 << 20),
+        compiler_params=pltpu.CompilerParams(vmem_limit_bytes=EXPERT_VMEM << 20),
         cost_estimate=pl.CostEstimate(
             flops=6 * total * hidden * width,
             bytes_accessed=6 * hidden * width + 4 * rows.size,
             transcendentals=total * hidden,
         ),
         name="expert",
-    )(rows, *pieces)
+    )(rows, *[pltpu.with_memory_space_constraint(piece, pltpu.HBM) for piece in pieces])
 
 
 def combine_kernel(returned_ref, place_ref, prob_ref, out_ref):
@@ -314,6 +354,29 @@
     return jnp.concatenate([rows, shift(rows, 1), shift(rows, -1), shift(rows, 2)], axis=0)
 
 
+def shift_split(rows, phase, step):
+    cores = lax.axis_size("ep")
+    pairs = []
+    for x in range(RING):
+        for y in range(RING):
+            for ep in range(cores):
+                along_y = (phase + ep) % 2 == 0
+                to_x = x if along_y else (x + step) % RING
+                to_y = (y + step) % RING if along_y else y
+                pairs.append(((x * RING + y) * cores + ep, (to_x * RING + to_y) * cores + ep))
+    return lax.ppermute(rows, ("ctx", "ep"), pairs)
+
+
+def gather_split(rows):
+    before, after = shift_split(rows, 0, 1), shift_split(rows, 0, -1)
+    top = jnp.concatenate([rows, before], axis=0)
+    bottom = jnp.concatenate([after, shift_split(before, 0, 1)], axis=0)
+    top_before, bottom_after = shift_split(top, 1, 1), shift_split(bottom, 1, -1)
+    top_after, bottom_before = shift_split(top, 1, -1), shift_split(bottom, 1, 1)
+    top_far, bottom_far = shift_split(top_before, 1, 1), shift_split(bottom_after, 1, -1)
+    return [top, bottom, top_before, top_after, bottom_before, bottom_after, top_far, bottom_far]
+
+
 def per_device(
     queries, keys, values, hidden, expert_ids, gate_probs, norm_gain, w_gate, w_up, w_down
 ):
@@ -329,10 +392,7 @@
     outgoing, *shards = lax.optimization_barrier((outgoing, w_gate, w_up, w_down))
     received = exchange(outgoing)
     shards = jnp.concatenate([shard[0] for shard in shards], axis=1)
-    half = shards.shape[0] // 2
-    pieces = gather_far(gather_near(shards[:half], shift_y), shift_x)
-    pieces += gather_far(gather_near(shards[half:], shift_x), shift_y)
-    produced = expert(received, pieces)
+    produced = expert(received, gather_split(shards))
 
     produced, keys, values = lax.optimization_barrier((produced, keys, values))
     returned = exchange(produced)

time: 209 us -> 201 us (0.962)
  starting transfers between devices: 96.7 us -> 79.2 us
  waiting for transfers between devices: 74 us -> 87.1 us
  local copies, waits for them, and re-layouts: 6.48 us -> 3.81 us
    ppermute x0 -> x9, waiting for transfers between devices: none -> 48.5 us  [shift_split(): return lax.ppermute(rows, ('ctx', 'ep'), pairs)]
    ppermute x11 -> x4, waiting for transfers between devices: 44.7 us -> 14.3 us  [shift_x(): return lax.ppermute(rows, 'ctx', pairs)]
    ppermute x0 -> x9, starting transfers between devices: none -> 26.7 us  [shift_split(): return lax.ppermute(rows, ('ctx', 'ep'), pairs)]
    ppermute x11 -> x4, starting transfers between devices: 37 us -> 13.9 us  [shift_x(): return lax.ppermute(rows, 'ctx', pairs)]
    ppermute x10 -> x3, starting transfers between devices: 28.9 us -> 7.68 us  [shift_y(): return lax.ppermute(rows, 'ctx', pairs)]
    ppermute x10 -> x3, waiting for transfers between devices: 10.8 us -> 4.74 us  [shift_y(): return lax.ppermute(rows, 'ctx', pairs)]
    unnamed x40 -> x29, local copies, waits for them, and re-layouts: 4.84 us -> 2.33 us
  transfers between devices with their start and end apart: 23 -> 18, of which waited for: 13 -> 14; matrix products, arithmetic and copies ran while one was open for 1% -> 1% of each run, Pallas kernels for 8% -> 8%
where the time goes in v3:
time: 201 us; the launch traced here: 200 us
  waiting for transfers between devices  87.1 us (43%)
  starting transfers between devices  79.2 us (39%)
  Pallas kernels  28.9 us (14%)
  local copies, waits for them, and re-layouts  3.81 us (2%)
    ppermute x9, waiting for transfers between devices, shift_split(): return lax.ppermute(rows, ('ctx', 'ep'), pairs)  48.5 us
    all_to_all x2, starting transfers between devices, exchange(): lax.all_to_all(rows.reshape(experts, WHOLE, rows.shape[1]), 'ep', split_a...  30.9 us
    ppermute x9, starting transfers between devices, shift_split(): return lax.ppermute(rows, ('ctx', 'ep'), pairs)  26.7 us
    all_to_all x2, waiting for transfers between devices, exchange(): lax.all_to_all(rows.reshape(experts, WHOLE, rows.shape[1]), 'ep', split_a...  19.5 us
    pallas_call x1, Pallas kernels, attention(): pl.pallas_call(attention_kernel, out_shape=jax.ShapeDtypeStruct(queries.s...  16 us
    ppermute x4, waiting for transfers between devices, shift_x(): return lax.ppermute(rows, 'ctx', pairs)  14.3 us
    ppermute x4, starting transfers between devices, shift_x(): return lax.ppermute(rows, 'ctx', pairs)  13.9 us
    pallas_call x1, Pallas kernels, expert(): pl.pallas_call(expert_kernel, out_shape=jax.ShapeDtypeStruct(rows.shape,...  7.98 us
  transfers between devices with their start and end apart: 18, of which 14 were waited for; matrix products, arithmetic and copies ran while one was open for 1% of the time, Pallas kernels for 8%

profile of v3, /device:TPU:1, one launch (start us, length us, event | category | flops | bytes accessed | tf_op | source)
XLA Modules:
  0.0 200.1 jit_solution(3871435190315659880)
XLA Ops:
  0.6 3.2 %dispatch.1 = (bf16[256,3072]{1,0:T(8,128)(2,1)}, s32[8,128]{1,0:T(8,128)S(1)}) custom-call(bf16[128,2048]{1,0:T(8,128)(2,1)} %bitcast.31, s32[2,128]{1,0:T(2,128)} %bitcast.38, f32[1,2048]{1,0:T(1,128)} %bitcast.37), custom_call_target="tpu_custom_call" | custom-call | tf_op jit(solution)/shard_map/dispatch/pallas_call | solution.py:89
  3.8 16.9 %all-to-all-start = ((bf16[32,8,3072]{2,1,0:T(8,128)(2,1)}), bf16[32,8,3072]{2,1,0:T(8,128)(2,1)S(1)}, u32[]{:S(2)}, u32[]{:S(2)}) async-start(bf16[32,8,3072]{2,1,0:T(8,128)(2,1)} %bitcast.6), calls=%async_computation | async-start | bytes 3145728 | tf_op jit(solution)/shard_map/all_to_all | solution.py:386
  20.8 3.1 %collective-permute-start = (bf16[48,6144]{1,0:T(8,128)(2,1)S(1)}, bf16[48,6144]{1,0:T(8,128)(2,1)S(1)}, u32[]{:S(2)}, u32[]{:S(2)}) collective-permute-start(bf16[48,6144]{1,0:T(8,128)(2,1)S(1)} %pad_maximum_fusion.1), channel_id=1, source_target_pairs={{0,32},{1,129},{2,34},{3,131},{4,36},{5,133},{6,38},{7,135},{8,40}... | collective-permute-start | bytes 1769480 | tf_op jit(solution)/shard_map/ppermute | solution.py:367
  23.9 3.4 %collective-permute-start.1 = (bf16[48,6144]{1,0:T(8,128)(2,1)S(1)}, bf16[48,6144]{1,0:T(8,128)(2,1)S(1)}, u32[]{:S(2)}, u32[]{:S(2)}) collective-permute-start(bf16[48,6144]{1,0:T(8,128)(2,1)S(1)} %pad_maximum_fusion.1), channel_id=1, source_target_pairs={{0,96},{1,385},{2,98},{3,387},{4,100},{5,389},{6,102},{7,391},{8,1... | collective-permute-start | bytes 1769480 | tf_op jit(solution)/shard_map/ppermute | solution.py:367
  27.3 5.6 %collective-permute-done = bf16[48,6144]{1,0:T(8,128)(2,1)S(1)} collective-permute-done((bf16[48,6144]{1,0:T(8,128)(2,1)S(1)}, bf16[48,6144]{1,0:T(8,128)(2,1)S(1)}, u32[]{:S(2)}, u32[]{:S(2)}) %collective-permute-start) | collective-permute-done | bytes 589856 | tf_op jit(solution)/shard_map/ppermute | solution.py:367
  33.0 3.2 %collective-permute-start.3 = (bf16[96,6144]{1,0:T(8,128)(2,1)S(1)}, bf16[96,6144]{1,0:T(8,128)(2,1)S(1)}, u32[]{:S(2)}, u32[]{:S(2)}) collective-permute-start(bf16[96,6144]{1,0:T(8,128)(2,1)S(1)} %pad_maximum_fusion.refs_0_), channel_id=1, source_target_pairs={{0,128},{1,33},{2,130},{3,35},{4,132},{5,37},{6,134},{7,39},{8,136... | collective-permute-start | bytes 3538952 | tf_op jit(solution)/shard_map/ppermute | solution.py:367
  36.2 1.9 collective-permute-start.2
  38.2 16.5 %collective-permute-done.2 = bf16[48,6144]{1,0:T(8,128)(2,1)S(1)} collective-permute-done((bf16[48,6144]{1,0:T(8,128)(2,1)S(1)}, bf16[48,6144]{1,0:T(8,128)(2,1)S(1)}, u32[]{:S(2)}, u32[]{:S(2)}) %collective-permute-start.2) | collective-permute-done | bytes 589856 | tf_op jit(solution)/shard_map/ppermute | solution.py:367
  54.8 3.4 %collective-permute-start.6 = (bf16[96,6144]{1,0:T(8,128)(2,1)S(1)}, bf16[96,6144]{1,0:T(8,128)(2,1)S(1)}, u32[]{:S(2)}, u32[]{:S(2)}) collective-permute-start(bf16[96,6144]{1,0:T(8,128)(2,1)S(1)} %constant_dynamic-update-slice_fusion.refs_1_), channel_id=1, source_target_pairs={{0,384},{1,97},{2,386},{3,99},{4,388},{5,101},{6,390},{7,103},{8,3... | collective-permute-start | bytes 3538952 | tf_op jit(solution)/shard_map/ppermute | solution.py:367
  58.2 3.4 %collective-permute-start.4 = (bf16[96,6144]{1,0:T(8,128)(2,1)S(1)}, bf16[96,6144]{1,0:T(8,128)(2,1)S(1)}, u32[]{:S(2)}, u32[]{:S(2)}) collective-permute-start(bf16[96,6144]{1,0:T(8,128)(2,1)S(1)} %pad_maximum_fusion.refs_0_), channel_id=1, source_target_pairs={{0,384},{1,97},{2,386},{3,99},{4,388},{5,101},{6,390},{7,103},{8,3... | collective-permute-start | bytes 3538952 | tf_op jit(solution)/shard_map/ppermute | solution.py:367
  61.6 1.9 collective-permute-start.5
  63.5 1.9 collective-permute-start.7
  65.4 6.6 %collective-permute-done.6.refs_5_ = bf16[96,6144]{1,0:T(8,128)(2,1)S(1)} collective-permute-done((bf16[96,6144]{1,0:T(8,128)(2,1)S(1)}, bf16[96,6144]{1,0:T(8,128)(2,1)S(1)}, u32[]{:S(2)}, u32[]{:S(2)}) %collective-permute-start.6) | collective-permute-done | bytes 1179680 | tf_op jit(solution)/shard_map/ppermute | solution.py:367
  72.1 4.6 %collective-permute-start.8 = (bf16[96,6144]{1,0:T(8,128)(2,1)S(1)}, bf16[96,6144]{1,0:T(8,128)(2,1)}, u32[]{:S(2)}, u32[]{:S(2)}) collective-permute-start(bf16[96,6144]{1,0:T(8,128)(2,1)S(1)} %collective-permute-done.6.refs_5_), channel_id=1, source_target_pairs={{0,384},{1,97},{2,386},{3,99},{4,388},{5,101},{6,390},{7,103},{8,3... | collective-permute-start | bytes 3538952 | tf_op jit(solution)/shard_map/ppermute | solution.py:367
  76.6 8.1 %collective-permute-done.4.refs_3_ = bf16[96,6144]{1,0:T(8,128)(2,1)S(1)} collective-permute-done((bf16[96,6144]{1,0:T(8,128)(2,1)S(1)}, bf16[96,6144]{1,0:T(8,128)(2,1)S(1)}, u32[]{:S(2)}, u32[]{:S(2)}) %collective-permute-start.4) | collective-permute-done | bytes 1179680 | tf_op jit(solution)/shard_map/ppermute | solution.py:367
  84.7 7.9 %collective-permute-done.7.refs_6_ = bf16[96,6144]{1,0:T(8,128)(2,1)S(1)} collective-permute-done((bf16[96,6144]{1,0:T(8,128)(2,1)S(1)}, bf16[96,6144]{1,0:T(8,128)(2,1)S(1)}, u32[]{:S(2)}, u32[]{:S(2)}) %collective-permute-start.7) | collective-permute-done | bytes 1179680 | tf_op jit(solution)/shard_map/ppermute | solution.py:367
  93.7 3.7 %collective-permute-done.8.refs_7_ = bf16[96,6144]{1,0:T(8,128)(2,1)} collective-permute-done((bf16[96,6144]{1,0:T(8,128)(2,1)S(1)}, bf16[96,6144]{1,0:T(8,128)(2,1)}, u32[]{:S(2)}, u32[]{:S(2)}) %collective-permute-start.8) | collective-permute-done | bytes 1179680 | tf_op jit(solution)/shard_map/ppermute | solution.py:367
  98.5 8.0 %expert.1 = bf16[256,3072]{1,0:T(8,128)(2,1)} custom-call(bf16[256,3072]{1,0:T(8,128)(2,1)S(1)} %bitcast.22, bf16[96,6144]{1,0:T(8,128)(2,1)} %copy-done.2, bf16[96,6144]{1,0:T(8,128)(2,1)} %copy-done.6, bf16[96,6144]{1,0:T(8,128)(2,1)} %copy-done.9, bf16[96,6144]{1,0:T(8,128)(2,1)} %copy-done.11, bf16[96,6144]{1,0:T(8,128)(2,1)} %copy-done.12, ...), custom_call_target="tpu_custom_call" | custom-call | flops 3623878656 | bytes 12582912 | tf_op jit(solution)/shard_map/expert/pallas_call | solution.py:178
  106.6 14.0 %all-to-all-start.1 = ((bf16[32,8,3072]{2,1,0:T(8,128)(2,1)}), bf16[32,8,3072]{2,1,0:T(8,128)(2,1)S(1)}, u32[]{:S(2)}, u32[]{:S(2)}) async-start(bf16[32,8,3072]{2,1,0:T(8,128)(2,1)} %bitcast.14), calls=%async_computation.1 | async-start | bytes 3145728 | tf_op jit(solution)/shard_map/all_to_all | solution.py:386
  120.6 2.4 %collective-permute-start.11 = (bf16[128,512]{1,0:T(8,128)(2,1)S(1)}, bf16[128,512]{1,0:T(8,128)(2,1)S(1)}, u32[]{:S(2)}, u32[]{:S(2)}) collective-permute-start(bf16[128,512]{1,0:T(8,128)(2,1)S(1)} %pad_maximum_fusion.3), channel_id=1, source_target_pairs={{0,64},{32,96},{64,0},{96,32},{128,192},{160,224},{192,128},{224,1... | collective-permute-start | bytes 393224 | tf_op jit(solution)/shard_map/ppermute | solution.py:344
  123.0 2.7 %collective-permute-start.10 = (bf16[128,512]{1,0:T(8,128)(2,1)S(1)}, bf16[128,512]{1,0:T(8,128)(2,1)S(1)}, u32[]{:S(2)}, u32[]{:S(2)}) collective-permute-start(bf16[128,512]{1,0:T(8,128)(2,1)S(1)} %pad_maximum_fusion.3), channel_id=1, source_target_pairs={{0,96},{32,0},{64,32},{96,64},{128,224},{160,128},{192,160},{224,1... | collective-permute-start | bytes 393224 | tf_op jit(solution)/shard_map/ppermute | solution.py:344
  125.7 2.6 %collective-permute-start.9 = (bf16[128,512]{1,0:T(8,128)(2,1)S(1)}, bf16[128,512]{1,0:T(8,128)(2,1)S(1)}, u32[]{:S(2)}, u32[]{:S(2)}) collective-permute-start(bf16[128,512]{1,0:T(8,128)(2,1)S(1)} %pad_maximum_fusion.3), channel_id=1, source_target_pairs={{0,32},{32,64},{64,96},{96,0},{128,160},{160,192},{192,224},{224,1... | collective-permute-start | bytes 393224 | tf_op jit(solution)/shard_map/ppermute | solution.py:344
  129.4 3.6 %collective-permute-done.9 = bf16[128,512]{1,0:T(8,128)(2,1)S(1)} collective-permute-done((bf16[128,512]{1,0:T(8,128)(2,1)S(1)}, bf16[128,512]{1,0:T(8,128)(2,1)S(1)}, u32[]{:S(2)}, u32[]{:S(2)}) %collective-permute-start.9) | collective-permute-done | bytes 131104 | tf_op jit(solution)/shard_map/ppermute | solution.py:344
  133.1 4.6 %collective-permute-start.13 = (bf16[512,512]{1,0:T(8,128)(2,1)S(1)}, bf16[512,512]{1,0:T(8,128)(2,1)S(1)}, u32[]{:S(2)}, u32[]{:S(2)}) collective-permute-start(bf16[512,512]{1,0:T(8,128)(2,1)S(1)} %pad_maximum_fusion.2.refs_0_.refs_5_), channel_id=1, source_target_pairs={{0,384},{32,416},{64,448},{96,480},{128,0},{160,32},{192,64},{224,... | collective-permute-start | bytes 1572872 | tf_op jit(solution)/shard_map/ppermute | solution.py:337
  137.6 1.9 collective-permute-start.12
  139.6 7.6 %collective-permute-done.13.refs_2_.refs_7_ = bf16[512,512]{1,0:T(8,128)(2,1)S(1)} collective-permute-done((bf16[512,512]{1,0:T(8,128)(2,1)S(1)}, bf16[512,512]{1,0:T(8,128)(2,1)S(1)}, u32[]{:S(2)}, u32[]{:S(2)}) %collective-permute-start.13) | collective-permute-done | bytes 524320 | tf_op jit(solution)/shard_map/ppermute | solution.py:337
  147.9 5.3 %collective-permute-start.15 = (bf16[256,512]{1,0:T(8,128)(2,1)}, bf16[256,512]{1,0:T(8,128)(2,1)S(1)}, u32[]{:S(2)}, u32[]{:S(2)}) collective-permute-start(bf16[256,512]{1,0:T(8,128)(2,1)} %slice.9), channel_id=1, source_target_pairs={{0,384},{32,416},{64,448},{96,480},{128,0},{160,32},{192,64},{224,... | collective-permute-start | bytes 786440 | tf_op jit(solution)/shard_map/ppermute | solution.py:337
  153.9 2.1 %collective-permute-start.14 = (bf16[256,512]{1,0:T(8,128)(2,1)}, bf16[256,512]{1,0:T(8,128)(2,1)}, u32[]{:S(2)}, u32[]{:S(2)}) collective-permute-start(bf16[256,512]{1,0:T(8,128)(2,1)} %slice.8), channel_id=1, source_target_pairs={{0,128},{32,160},{64,192},{96,224},{128,256},{160,288},{192,320},{... | collective-permute-start | bytes 786440 | tf_op jit(solution)/shard_map/ppermute | solution.py:337
  156.8 5.9 %collective-permute-done.14.refs_3_.refs_8_ = bf16[256,512]{1,0:T(8,128)(2,1)} collective-permute-done((bf16[256,512]{1,0:T(8,128)(2,1)}, bf16[256,512]{1,0:T(8,128)(2,1)}, u32[]{:S(2)}, u32[]{:S(2)}) %collective-permute-start.14) | collective-permute-done | bytes 262176 | tf_op jit(solution)/shard_map/ppermute | solution.py:337
  164.0 16.0 %attention.1 = bf16[128,4096]{1,0:T(8,128)(2,1)} custom-call(s32[1]{0:T(128)} %bitcast.block_ref, bf16[128,4096]{1,0:T(8,128)(2,1)S(1)} %bitcast.24, bf16[512,512]{1,0:T(8,128)(2,1)S(1)} %pad_maximum_fusion.2.refs_0_.refs_5_, bf16[512,512]{1,0:T(8,128)(2,1)S(1)} %collective-permute-done.12.refs_1_.refs_6_, ...), custom_call_target="tpu_custom_call" | custom-call | flops 4294967296 | bytes 4194304 | tf_op jit(solution)/shard_map/attention/pallas_call | solution.py:308
  180.0 18.4 %all-to-all-done.1 = bf16[32,8,3072]{2,1,0:T(8,128)(2,1)S(1)} async-done(((bf16[32,8,3072]{2,1,0:T(8,128)(2,1)}), bf16[32,8,3072]{2,1,0:T(8,128)(2,1)S(1)}, u32[]{:S(2)}, u32[]{:S(2)}) %all-to-all-start.1) | async-done | bytes 1572896 | tf_op jit(solution)/shard_map/all_to_all | solution.py:386
  198.4 1.7 combine.1
  (44 shorter events, 7.0 us)
Async XLA Ops:
  3.8 16.9 %copy-start.3 = (bf16[1,48,2048]{2,1,0:T(8,128)(2,1)S(1)}, bf16[1,48,2048]{2,1,0:T(8,128)(2,1)}, u32[]{:S(2)}) copy-start(bf16[1,48,2048]{2,1,0:T(8,128)(2,1)} %param.19) | copy-start | bytes 589828
  3.8 16.9 %copy-start.4 = (bf16[1,48,2048]{2,1,0:T(8,128)(2,1)S(1)}, bf16[1,48,2048]{2,1,0:T(8,128)(2,1)}, u32[]{:S(2)}) copy-start(bf16[1,48,2048]{2,1,0:T(8,128)(2,1)} %param.18) | copy-start | bytes 589828
  3.8 16.9 %copy-start.5 = (bf16[1,48,2048]{2,1,0:T(8,128)(2,1)S(1)}, bf16[1,48,2048]{2,1,0:T(8,128)(2,1)}, u32[]{:S(2)}) copy-start(bf16[1,48,2048]{2,1,0:T(8,128)(2,1)} %param.17) | copy-start | bytes 589828
  3.8 94.7 %all-to-all-start = ((bf16[32,8,3072]{2,1,0:T(8,128)(2,1)}), bf16[32,8,3072]{2,1,0:T(8,128)(2,1)S(1)}, u32[]{:S(2)}, u32[]{:S(2)}) async-start(bf16[32,8,3072]{2,1,0:T(8,128)(2,1)} %bitcast.6), calls=%async_computation | async-start | bytes 3145728 | tf_op jit(solution)/shard_map/all_to_all | solution.py:386
  20.8 12.1 %collective-permute-start = (bf16[48,6144]{1,0:T(8,128)(2,1)S(1)}, bf16[48,6144]{1,0:T(8,128)(2,1)S(1)}, u32[]{:S(2)}, u32[]{:S(2)}) collective-permute-start(bf16[48,6144]{1,0:T(8,128)(2,1)S(1)} %pad_maximum_fusion.1), channel_id=1, source_target_pairs={{0,32},{1,129},{2,34},{3,131},{4,36},{5,133},{6,38},{7,135},{8,40}... | collective-permute-start | bytes 1769480 | tf_op jit(solution)/shard_map/ppermute | solution.py:367
  23.9 14.3 %collective-permute-start.1 = (bf16[48,6144]{1,0:T(8,128)(2,1)S(1)}, bf16[48,6144]{1,0:T(8,128)(2,1)S(1)}, u32[]{:S(2)}, u32[]{:S(2)}) collective-permute-start(bf16[48,6144]{1,0:T(8,128)(2,1)S(1)} %pad_maximum_fusion.1), channel_id=1, source_target_pairs={{0,96},{1,385},{2,98},{3,387},{4,100},{5,389},{6,102},{7,391},{8,1... | collective-permute-start | bytes 1769480 | tf_op jit(solution)/shard_map/ppermute | solution.py:367
  33.0 25.2 %copy-start.2 = (bf16[96,6144]{1,0:T(8,128)(2,1)}, bf16[96,6144]{1,0:T(8,128)(2,1)S(1)}, u32[]{:S(2)}) copy-start(bf16[96,6144]{1,0:T(8,128)(2,1)S(1)} %pad_maximum_fusion.refs_0_) | copy-start | bytes 3538948
  33.0 30.5 %collective-permute-start.3 = (bf16[96,6144]{1,0:T(8,128)(2,1)S(1)}, bf16[96,6144]{1,0:T(8,128)(2,1)S(1)}, u32[]{:S(2)}, u32[]{:S(2)}) collective-permute-start(bf16[96,6144]{1,0:T(8,128)(2,1)S(1)} %pad_maximum_fusion.refs_0_), channel_id=1, source_target_pairs={{0,128},{1,33},{2,130},{3,35},{4,132},{5,37},{6,134},{7,39},{8,136... | collective-permute-start | bytes 3538952 | tf_op jit(solution)/shard_map/ppermute | solution.py:367
  36.2 18.5 %collective-permute-start.2 = (bf16[48,6144]{1,0:T(8,128)(2,1)S(1)}, bf16[48,6144]{1,0:T(8,128)(2,1)S(1)}, u32[]{:S(2)}, u32[]{:S(2)}) collective-permute-start(bf16[48,6144]{1,0:T(8,128)(2,1)S(1)} %collective-permute-done), channel_id=1, source_target_pairs={{0,32},{1,129},{2,34},{3,131},{4,36},{5,133},{6,38},{7,135},{8,40}... | collective-permute-start | bytes 1769480 | tf_op jit(solution)/shard_map/ppermute | solution.py:367
  54.8 37.8 %copy-start.6 = (bf16[96,6144]{1,0:T(8,128)(2,1)}, bf16[96,6144]{1,0:T(8,128)(2,1)S(1)}, u32[]{:S(2)}) copy-start(bf16[96,6144]{1,0:T(8,128)(2,1)S(1)} %constant_dynamic-update-slice_fusion.refs_1_) | copy-start | bytes 3538948
  54.8 17.2 %collective-permute-start.6 = (bf16[96,6144]{1,0:T(8,128)(2,1)S(1)}, bf16[96,6144]{1,0:T(8,128)(2,1)S(1)}, u32[]{:S(2)}, u32[]{:S(2)}) collective-permute-start(bf16[96,6144]{1,0:T(8,128)(2,1)S(1)} %constant_dynamic-update-slice_fusion.refs_1_), channel_id=1, source_target_pairs={{0,384},{1,97},{2,386},{3,99},{4,388},{5,101},{6,390},{7,103},{8,3... | collective-permute-start | bytes 3538952 | tf_op jit(solution)/shard_map/ppermute | solution.py:367
  58.2 26.5 %collective-permute-start.4 = (bf16[96,6144]{1,0:T(8,128)(2,1)S(1)}, bf16[96,6144]{1,0:T(8,128)(2,1)S(1)}, u32[]{:S(2)}, u32[]{:S(2)}) collective-permute-start(bf16[96,6144]{1,0:T(8,128)(2,1)S(1)} %pad_maximum_fusion.refs_0_), channel_id=1, source_target_pairs={{0,384},{1,97},{2,386},{3,99},{4,388},{5,101},{6,390},{7,103},{8,3... | collective-permute-start | bytes 3538952 | tf_op jit(solution)/shard_map/ppermute | solution.py:367
  61.6 23.1 %collective-permute-start.5 = (bf16[96,6144]{1,0:T(8,128)(2,1)S(1)}, bf16[96,6144]{1,0:T(8,128)(2,1)S(1)}, u32[]{:S(2)}, u32[]{:S(2)}) collective-permute-start(bf16[96,6144]{1,0:T(8,128)(2,1)S(1)} %constant_dynamic-update-slice_fusion.refs_1_), channel_id=1, source_target_pairs={{0,128},{1,33},{2,130},{3,35},{4,132},{5,37},{6,134},{7,39},{8,136... | collective-permute-start | bytes 3538952 | tf_op jit(solution)/shard_map/ppermute | solution.py:367
  63.5 29.2 %copy-start.9 = (bf16[96,6144]{1,0:T(8,128)(2,1)}, bf16[96,6144]{1,0:T(8,128)(2,1)S(1)}, u32[]{:S(2)}) copy-start(bf16[96,6144]{1,0:T(8,128)(2,1)S(1)} %collective-permute-done.3.refs_2_) | copy-start | bytes 3538948
  63.5 29.1 %collective-permute-start.7 = (bf16[96,6144]{1,0:T(8,128)(2,1)S(1)}, bf16[96,6144]{1,0:T(8,128)(2,1)S(1)}, u32[]{:S(2)}, u32[]{:S(2)}) collective-permute-start(bf16[96,6144]{1,0:T(8,128)(2,1)S(1)} %collective-permute-done.3.refs_2_), channel_id=1, source_target_pairs={{0,128},{1,33},{2,130},{3,35},{4,132},{5,37},{6,134},{7,39},{8,136... | collective-permute-start | bytes 3538952 | tf_op jit(solution)/shard_map/ppermute | solution.py:367
  72.1 20.6 %copy-start.10 = (bf16[96,6144]{1,0:T(8,128)(2,1)}, bf16[96,6144]{1,0:T(8,128)(2,1)S(1)}, u32[]{:S(2)}) copy-start(bf16[96,6144]{1,0:T(8,128)(2,1)S(1)} %collective-permute-done.6.refs_5_) | copy-start | bytes 3538948
  72.1 25.4 %collective-permute-start.8 = (bf16[96,6144]{1,0:T(8,128)(2,1)S(1)}, bf16[96,6144]{1,0:T(8,128)(2,1)}, u32[]{:S(2)}, u32[]{:S(2)}) collective-permute-start(bf16[96,6144]{1,0:T(8,128)(2,1)S(1)} %collective-permute-done.6.refs_5_), channel_id=1, source_target_pairs={{0,384},{1,97},{2,386},{3,99},{4,388},{5,101},{6,390},{7,103},{8,3... | collective-permute-start | bytes 3538952 | tf_op jit(solution)/shard_map/ppermute | solution.py:367
  84.7 8.0 %copy-start.11 = (bf16[96,6144]{1,0:T(8,128)(2,1)}, bf16[96,6144]{1,0:T(8,128)(2,1)S(1)}, u32[]{:S(2)}) copy-start(bf16[96,6144]{1,0:T(8,128)(2,1)S(1)} %collective-permute-done.4.refs_3_) | copy-start | bytes 3538948
  84.7 8.0 %copy-start.12 = (bf16[96,6144]{1,0:T(8,128)(2,1)}, bf16[96,6144]{1,0:T(8,128)(2,1)S(1)}, u32[]{:S(2)}) copy-start(bf16[96,6144]{1,0:T(8,128)(2,1)S(1)} %collective-permute-done.5.refs_4_) | copy-start | bytes 3538948
  92.7 1.0 copy-start.13
  106.5 14.0 %copy-start.7 = (bf16[1,128,256]{2,1,0:T(8,128)(2,1)S(1)}, bf16[1,128,256]{2,1,0:T(8,128)(2,1)}, u32[]{:S(2)}) copy-start(bf16[1,128,256]{2,1,0:T(8,128)(2,1)} %param.12) | copy-start | bytes 196612
  106.5 14.0 %copy-start.8 = (bf16[1,128,256]{2,1,0:T(8,128)(2,1)S(1)}, bf16[1,128,256]{2,1,0:T(8,128)(2,1)}, u32[]{:S(2)}) copy-start(bf16[1,128,256]{2,1,0:T(8,128)(2,1)} %param.11) | copy-start | bytes 196612
  106.6 91.8 %all-to-all-start.1 = ((bf16[32,8,3072]{2,1,0:T(8,128)(2,1)}), bf16[32,8,3072]{2,1,0:T(8,128)(2,1)S(1)}, u32[]{:S(2)}, u32[]{:S(2)}) async-start(bf16[32,8,3072]{2,1,0:T(8,128)(2,1)} %bitcast.14), calls=%async_computation.1 | async-start | bytes 3145728 | tf_op jit(solution)/shard_map/all_to_all | solution.py:386
  120.6 8.3 %collective-permute-start.11 = (bf16[128,512]{1,0:T(8,128)(2,1)S(1)}, bf16[128,512]{1,0:T(8,128)(2,1)S(1)}, u32[]{:S(2)}, u32[]{:S(2)}) collective-permute-start(bf16[128,512]{1,0:T(8,128)(2,1)S(1)} %pad_maximum_fusion.3), channel_id=1, source_target_pairs={{0,64},{32,96},{64,0},{96,32},{128,192},{160,224},{192,128},{224,1... | collective-permute-start | bytes 393224 | tf_op jit(solution)/shard_map/ppermute | solution.py:344
  123.0 6.4 %collective-permute-start.10 = (bf16[128,512]{1,0:T(8,128)(2,1)S(1)}, bf16[128,512]{1,0:T(8,128)(2,1)S(1)}, u32[]{:S(2)}, u32[]{:S(2)}) collective-permute-start(bf16[128,512]{1,0:T(8,128)(2,1)S(1)} %pad_maximum_fusion.3), channel_id=1, source_target_pairs={{0,96},{32,0},{64,32},{96,64},{128,224},{160,128},{192,160},{224,1... | collective-permute-start | bytes 393224 | tf_op jit(solution)/shard_map/ppermute | solution.py:344
  125.7 7.3 %collective-permute-start.9 = (bf16[128,512]{1,0:T(8,128)(2,1)S(1)}, bf16[128,512]{1,0:T(8,128)(2,1)S(1)}, u32[]{:S(2)}, u32[]{:S(2)}) collective-permute-start(bf16[128,512]{1,0:T(8,128)(2,1)S(1)} %pad_maximum_fusion.3), channel_id=1, source_target_pairs={{0,32},{32,64},{64,96},{96,0},{128,160},{160,192},{192,224},{224,1... | collective-permute-start | bytes 393224 | tf_op jit(solution)/shard_map/ppermute | solution.py:344
  133.1 14.1 %collective-permute-start.13 = (bf16[512,512]{1,0:T(8,128)(2,1)S(1)}, bf16[512,512]{1,0:T(8,128)(2,1)S(1)}, u32[]{:S(2)}, u32[]{:S(2)}) collective-permute-start(bf16[512,512]{1,0:T(8,128)(2,1)S(1)} %pad_maximum_fusion.2.refs_0_.refs_5_), channel_id=1, source_target_pairs={{0,384},{32,416},{64,448},{96,480},{128,0},{160,32},{192,64},{224,... | collective-permute-start | bytes 1572872 | tf_op jit(solution)/shard_map/ppermute | solution.py:337
  137.6 15.5 %collective-permute-start.12 = (bf16[512,512]{1,0:T(8,128)(2,1)S(1)}, bf16[512,512]{1,0:T(8,128)(2,1)S(1)}, u32[]{:S(2)}, u32[]{:S(2)}) collective-permute-start(bf16[512,512]{1,0:T(8,128)(2,1)S(1)} %pad_maximum_fusion.2.refs_0_.refs_5_), channel_id=1, source_target_pairs={{0,128},{32,160},{64,192},{96,224},{128,256},{160,288},{192,320},{... | collective-permute-start | bytes 1572872 | tf_op jit(solution)/shard_map/ppermute | solution.py:337
  147.9 8.9 %collective-permute-start.15 = (bf16[256,512]{1,0:T(8,128)(2,1)}, bf16[256,512]{1,0:T(8,128)(2,1)S(1)}, u32[]{:S(2)}, u32[]{:S(2)}) collective-permute-start(bf16[256,512]{1,0:T(8,128)(2,1)} %slice.9), channel_id=1, source_target_pairs={{0,384},{32,416},{64,448},{96,480},{128,0},{160,32},{192,64},{224,... | collective-permute-start | bytes 786440 | tf_op jit(solution)/shard_map/ppermute | solution.py:337
  153.9 8.8 %collective-permute-start.14 = (bf16[256,512]{1,0:T(8,128)(2,1)}, bf16[256,512]{1,0:T(8,128)(2,1)}, u32[]{:S(2)}, u32[]{:S(2)}) collective-permute-start(bf16[256,512]{1,0:T(8,128)(2,1)} %slice.8), channel_id=1, source_target_pairs={{0,128},{32,160},{64,192},{96,224},{128,256},{160,288},{192,320},{... | collective-permute-start | bytes 786440 | tf_op jit(solution)/shard_map/ppermute | solution.py:337
  162.7 1.2 copy-start.1
  164.0 34.4 %copy-start = (f32[1,128,2]{1,2,0:T(2,128)S(1)}, f32[1,128,2]{1,2,0:T(2,128)}, u32[]{:S(2)}) copy-start(f32[1,128,2]{1,2,0:T(2,128)} %param.15) | copy-start | bytes 3076

commit v4 on v3

--- a/solution.py
+++ b/solution.py
@@ -367,14 +367,34 @@
     return lax.ppermute(rows, ("ctx", "ep"), pairs)
 
 
-def gather_split(rows):
-    before, after = shift_split(rows, 0, 1), shift_split(rows, 0, -1)
-    top = jnp.concatenate([rows, before], axis=0)
-    bottom = jnp.concatenate([after, shift_split(before, 0, 1)], axis=0)
-    top_before, bottom_after = shift_split(top, 1, 1), shift_split(bottom, 1, -1)
-    top_after, bottom_before = shift_split(top, 1, -1), shift_split(bottom, 1, 1)
-    top_far, bottom_far = shift_split(top_before, 1, 1), shift_split(bottom_after, 1, -1)
-    return [top, bottom, top_before, top_after, bottom_before, bottom_after, top_far, bottom_far]
+def gather_blocks(own):
+    def along(direction, rows, step):
+        return shift_split(rows, direction, step)
+
+    near = {
+        (-1, 0): along(0, own, 1),
+        (1, 0): along(0, own, -1),
+        (0, -1): along(1, own, 1),
+        (0, 1): along(1, own, -1),
+    }
+    corner = {
+        (-1, -1): along(0, near[0, -1], 1),
+        (1, 1): along(0, near[0, 1], -1),
+        (1, -1): along(1, near[1, 0], 1),
+        (-1, 1): along(1, near[-1, 0], -1),
+    }
+    far = {
+        (2, 0): along(0, near[-1, 0], 1),
+        (2, 1): along(0, corner[1, 1], -1),
+        (0, 2): along(1, near[0, -1], 1),
+        (1, 2): along(1, corner[1, 1], -1),
+    }
+    last = {
+        (2, -1): along(0, corner[-1, -1], 1),
+        (2, 2): along(0, far[1, 2], -1),
+        (-1, 2): along(1, corner[-1, 1], -1),
+    }
+    return [own, *near.values(), *corner.values(), *far.values(), *last.values()]
 
 
 def per_device(
@@ -392,7 +412,7 @@
     outgoing, *shards = lax.optimization_barrier((outgoing, w_gate, w_up, w_down))
     received = exchange(outgoing)
     shards = jnp.concatenate([shard[0] for shard in shards], axis=1)
-    produced = expert(received, gather_split(shards))
+    produced = expert(received, gather_blocks(shards))
 
     produced, keys, values = lax.optimization_barrier((produced, keys, values))
     returned = exchange(produced)

time: 201 us -> 192 us (0.955)
  waiting for transfers between devices: 87.1 us -> 65.4 us
  starting transfers between devices: 79.2 us -> 91.5 us
    ppermute x9 -> x15, waiting for transfers between devices: 48.5 us -> 14.8 us  [shift_split(): return lax.ppermute(rows, ('ctx', 'ep'), pairs)]
    ppermute x9 -> x15, starting transfers between devices: 26.7 us -> 46.4 us  [shift_split(): return lax.ppermute(rows, ('ctx', 'ep'), pairs)]
    all_to_all x2, waiting for transfers between devices: 19.5 us -> 31.9 us  [exchange(): lax.all_to_all(rows.reshape(experts, WHOLE, rows.shape[1]), 'ep', split_a...]
    all_to_all x2, starting transfers between devices: 30.9 us -> 21.2 us  [exchange(): lax.all_to_all(rows.reshape(experts, WHOLE, rows.shape[1]), 'ep', split_a...]
    ppermute x3, starting transfers between devices: 7.68 us -> 10.1 us  [shift_y(): return lax.ppermute(rows, 'ctx', pairs)]
  transfers between devices with their start and end apart: 18 -> 24, of which waited for: 14 -> 13; matrix products, arithmetic and copies ran while one was open for 1% -> 1% of each run, Pallas kernels for 8% -> 8%
where the time goes in v4:
time: 192 us; the launch traced here: 191 us
  starting transfers between devices  91.5 us (48%)
  waiting for transfers between devices  65.4 us (34%)
  Pallas kernels  29.2 us (15%)
  local copies, waits for them, and re-layouts  3.59 us (2%)
    ppermute x15, starting transfers between devices, shift_split(): return lax.ppermute(rows, ('ctx', 'ep'), pairs)  46.4 us
    all_to_all x2, waiting for transfers between devices, exchange(): lax.all_to_all(rows.reshape(experts, WHOLE, rows.shape[1]), 'ep', split_a...  31.9 us
    all_to_all x2, starting transfers between devices, exchange(): lax.all_to_all(rows.reshape(experts, WHOLE, rows.shape[1]), 'ep', split_a...  21.2 us
    pallas_call x1, Pallas kernels, attention(): pl.pallas_call(attention_kernel, out_shape=jax.ShapeDtypeStruct(queries.s...  16 us
    ppermute x15, waiting for transfers between devices, shift_split(): return lax.ppermute(rows, ('ctx', 'ep'), pairs)  14.8 us
    ppermute x4, waiting for transfers between devices, shift_x(): return lax.ppermute(rows, 'ctx', pairs)  14.2 us
    ppermute x4, starting transfers between devices, shift_x(): return lax.ppermute(rows, 'ctx', pairs)  13.7 us
    ppermute x3, starting transfers between devices, shift_y(): return lax.ppermute(rows, 'ctx', pairs)  10.1 us
  transfers between devices with their start and end apart: 24, of which 13 were waited for; matrix products, arithmetic and copies ran while one was open for 1% of the time, Pallas kernels for 8%

profile of v4, /device:TPU:1, one launch (start us, length us, event | category | flops | bytes accessed | tf_op | source)
XLA Modules:
  0.0 190.9 jit_solution(13561778682318065351)
XLA Ops:
  0.6 3.1 %dispatch.1 = (bf16[256,3072]{1,0:T(8,128)(2,1)}, s32[8,128]{1,0:T(8,128)S(1)}) custom-call(bf16[128,2048]{1,0:T(8,128)(2,1)} %bitcast.25, s32[2,128]{1,0:T(2,128)} %bitcast.35, f32[1,2048]{1,0:T(1,128)} %bitcast.34), custom_call_target="tpu_custom_call" | custom-call | tf_op jit(solution)/shard_map/dispatch/pallas_call | solution.py:89
  3.8 16.9 %all-to-all-start = ((bf16[32,8,3072]{2,1,0:T(8,128)(2,1)}), bf16[32,8,3072]{2,1,0:T(8,128)(2,1)S(1)}, u32[]{:S(2)}, u32[]{:S(2)}) async-start(bf16[32,8,3072]{2,1,0:T(8,128)(2,1)} %bitcast.6), calls=%async_computation | async-start | bytes 3145728 | tf_op jit(solution)/shard_map/all_to_all | solution.py:406
  20.8 4.7 %collective-permute-start.3 = (bf16[48,6144]{1,0:T(8,128)(2,1)S(1)}, bf16[48,6144]{1,0:T(8,128)(2,1)S(1)}, u32[]{:S(2)}, u32[]{:S(2)}) collective-permute-start(bf16[48,6144]{1,0:T(8,128)(2,1)S(1)} %pad_maximum_fusion.refs_0_), channel_id=1, source_target_pairs={{0,384},{1,97},{2,386},{3,99},{4,388},{5,101},{6,390},{7,103},{8,3... | collective-permute-start | bytes 1769480 | tf_op jit(solution)/shard_map/ppermute | solution.py:367
  27.4 4.4 %collective-permute-start.1 = (bf16[48,6144]{1,0:T(8,128)(2,1)S(1)}, bf16[48,6144]{1,0:T(8,128)(2,1)S(1)}, u32[]{:S(2)}, u32[]{:S(2)}) collective-permute-start(bf16[48,6144]{1,0:T(8,128)(2,1)S(1)} %pad_maximum_fusion.refs_0_), channel_id=1, source_target_pairs={{0,96},{1,385},{2,98},{3,387},{4,100},{5,389},{6,102},{7,391},{8,1... | collective-permute-start | bytes 1769480 | tf_op jit(solution)/shard_map/ppermute | solution.py:367
  33.7 4.6 %collective-permute-start.5 = (bf16[48,6144]{1,0:T(8,128)(2,1)S(1)}, bf16[48,6144]{1,0:T(8,128)(2,1)S(1)}, u32[]{:S(2)}, u32[]{:S(2)}) collective-permute-start(bf16[48,6144]{1,0:T(8,128)(2,1)S(1)} %collective-permute-done.3.refs_4_), channel_id=1, source_target_pairs={{0,96},{1,385},{2,98},{3,387},{4,100},{5,389},{6,102},{7,391},{8,1... | collective-permute-start | bytes 1769480 | tf_op jit(solution)/shard_map/ppermute | solution.py:367
  38.3 1.9 %collective-permute-start.10 = (bf16[48,6144]{1,0:T(8,128)(2,1)S(1)}, bf16[48,6144]{1,0:T(8,128)(2,1)S(1)}, u32[]{:S(2)}, u32[]{:S(2)}) collective-permute-start(bf16[48,6144]{1,0:T(8,128)(2,1)S(1)} %collective-permute-done.2.refs_3_), channel_id=1, source_target_pairs={{0,128},{1,33},{2,130},{3,35},{4,132},{5,37},{6,134},{7,39},{8,136... | collective-permute-start | bytes 1769480 | tf_op jit(solution)/shard_map/ppermute | solution.py:367
  40.3 2.2 %collective-permute-start.4 = (bf16[48,6144]{1,0:T(8,128)(2,1)S(1)}, bf16[48,6144]{1,0:T(8,128)(2,1)S(1)}, u32[]{:S(2)}, u32[]{:S(2)}) collective-permute-start(bf16[48,6144]{1,0:T(8,128)(2,1)S(1)} %collective-permute-done.2.refs_3_), channel_id=1, source_target_pairs={{0,32},{1,129},{2,34},{3,131},{4,36},{5,133},{6,38},{7,135},{8,40}... | collective-permute-start | bytes 1769480 | tf_op jit(solution)/shard_map/ppermute | solution.py:367
  42.5 2.9 %collective-permute-start.6 = (bf16[48,6144]{1,0:T(8,128)(2,1)S(1)}, bf16[48,6144]{1,0:T(8,128)(2,1)S(1)}, u32[]{:S(2)}, u32[]{:S(2)}) collective-permute-start(bf16[48,6144]{1,0:T(8,128)(2,1)S(1)} %collective-permute-done.1.refs_2_), channel_id=1, source_target_pairs={{0,128},{1,33},{2,130},{3,35},{4,132},{5,37},{6,134},{7,39},{8,136... | collective-permute-start | bytes 1769480 | tf_op jit(solution)/shard_map/ppermute | solution.py:367
  45.5 3.8 %collective-permute-start.7 = (bf16[48,6144]{1,0:T(8,128)(2,1)S(1)}, bf16[48,6144]{1,0:T(8,128)(2,1)S(1)}, u32[]{:S(2)}, u32[]{:S(2)}) collective-permute-start(bf16[48,6144]{1,0:T(8,128)(2,1)S(1)} %collective-permute-done.refs_1_), channel_id=1, source_target_pairs={{0,384},{1,97},{2,386},{3,99},{4,388},{5,101},{6,390},{7,103},{8,3... | collective-permute-start | bytes 1769480 | tf_op jit(solution)/shard_map/ppermute | solution.py:367
  49.3 3.1 %collective-permute-start.11 = (bf16[48,6144]{1,0:T(8,128)(2,1)S(1)}, bf16[48,6144]{1,0:T(8,128)(2,1)S(1)}, u32[]{:S(2)}, u32[]{:S(2)}) collective-permute-start(bf16[48,6144]{1,0:T(8,128)(2,1)S(1)} %collective-permute-done.5.refs_6_), channel_id=1, source_target_pairs={{0,384},{1,97},{2,386},{3,99},{4,388},{5,101},{6,390},{7,103},{8,3... | collective-permute-start | bytes 1769480 | tf_op jit(solution)/shard_map/ppermute | solution.py:367
  56.2 2.5 %collective-permute-done.4.refs_5_ = bf16[48,6144]{1,0:T(8,128)(2,1)S(1)} collective-permute-done((bf16[48,6144]{1,0:T(8,128)(2,1)S(1)}, bf16[48,6144]{1,0:T(8,128)(2,1)S(1)}, u32[]{:S(2)}, u32[]{:S(2)}) %collective-permute-start.4) | collective-permute-done | bytes 589856 | tf_op jit(solution)/shard_map/ppermute | solution.py:367
  58.7 3.1 %collective-permute-start.9 = (bf16[48,6144]{1,0:T(8,128)(2,1)S(1)}, bf16[48,6144]{1,0:T(8,128)(2,1)S(1)}, u32[]{:S(2)}, u32[]{:S(2)}) collective-permute-start(bf16[48,6144]{1,0:T(8,128)(2,1)S(1)} %collective-permute-done.5.refs_6_), channel_id=1, source_target_pairs={{0,96},{1,385},{2,98},{3,387},{4,100},{5,389},{6,102},{7,391},{8,1... | collective-permute-start | bytes 1769480 | tf_op jit(solution)/shard_map/ppermute | solution.py:367
  61.8 2.3 %collective-permute-done.6.refs_7_ = bf16[48,6144]{1,0:T(8,128)(2,1)S(1)} collective-permute-done((bf16[48,6144]{1,0:T(8,128)(2,1)S(1)}, bf16[48,6144]{1,0:T(8,128)(2,1)S(1)}, u32[]{:S(2)}, u32[]{:S(2)}) %collective-permute-start.6) | collective-permute-done | bytes 589856 | tf_op jit(solution)/shard_map/ppermute | solution.py:367
  64.1 2.4 %collective-permute-start.12 = (bf16[48,6144]{1,0:T(8,128)(2,1)S(1)}, bf16[48,6144]{1,0:T(8,128)(2,1)S(1)}, u32[]{:S(2)}, u32[]{:S(2)}) collective-permute-start(bf16[48,6144]{1,0:T(8,128)(2,1)S(1)} %collective-permute-done.4.refs_5_), channel_id=1, source_target_pairs={{0,32},{1,129},{2,34},{3,131},{4,36},{5,133},{6,38},{7,135},{8,40}... | collective-permute-start | bytes 1769480 | tf_op jit(solution)/shard_map/ppermute | solution.py:367
  66.6 2.0 %collective-permute-start.14 = (bf16[48,6144]{1,0:T(8,128)(2,1)S(1)}, bf16[48,6144]{1,0:T(8,128)(2,1)S(1)}, u32[]{:S(2)}, u32[]{:S(2)}) collective-permute-start(bf16[48,6144]{1,0:T(8,128)(2,1)S(1)} %collective-permute-done.7.refs_8_), channel_id=1, source_target_pairs={{0,384},{1,97},{2,386},{3,99},{4,388},{5,101},{6,390},{7,103},{8,3... | collective-permute-start | bytes 1769480 | tf_op jit(solution)/shard_map/ppermute | solution.py:367
  68.6 5.5 %collective-permute-start.13 = (bf16[48,6144]{1,0:T(8,128)(2,1)S(1)}, bf16[48,6144]{1,0:T(8,128)(2,1)}, u32[]{:S(2)}, u32[]{:S(2)}) collective-permute-start(bf16[48,6144]{1,0:T(8,128)(2,1)S(1)} %collective-permute-done.11.refs_12_), channel_id=1, source_target_pairs={{0,96},{1,385},{2,98},{3,387},{4,100},{5,389},{6,102},{7,391},{8,1... | collective-permute-start | bytes 1769480 | tf_op jit(solution)/shard_map/ppermute | solution.py:367
  74.2 3.6 %collective-permute-done.12.refs_13_ = bf16[48,6144]{1,0:T(8,128)(2,1)S(1)} collective-permute-done((bf16[48,6144]{1,0:T(8,128)(2,1)S(1)}, bf16[48,6144]{1,0:T(8,128)(2,1)S(1)}, u32[]{:S(2)}, u32[]{:S(2)}) %collective-permute-start.12) | collective-permute-done | bytes 589856 | tf_op jit(solution)/shard_map/ppermute | solution.py:367
  77.8 3.3 %collective-permute-done.14.refs_15_ = bf16[48,6144]{1,0:T(8,128)(2,1)S(1)} collective-permute-done((bf16[48,6144]{1,0:T(8,128)(2,1)S(1)}, bf16[48,6144]{1,0:T(8,128)(2,1)S(1)}, u32[]{:S(2)}, u32[]{:S(2)}) %collective-permute-start.14) | collective-permute-done | bytes 589856 | tf_op jit(solution)/shard_map/ppermute | solution.py:367
  83.2 15.3 %all-to-all-done = bf16[32,8,3072]{2,1,0:T(8,128)(2,1)S(1)} async-done(((bf16[32,8,3072]{2,1,0:T(8,128)(2,1)}), bf16[32,8,3072]{2,1,0:T(8,128)(2,1)S(1)}, u32[]{:S(2)}, u32[]{:S(2)}) %all-to-all-start) | async-done | bytes 1572896 | tf_op jit(solution)/shard_map/all_to_all | solution.py:406
  98.5 8.3 %expert.1 = bf16[256,3072]{1,0:T(8,128)(2,1)} custom-call(bf16[256,3072]{1,0:T(8,128)(2,1)S(1)} %bitcast.22, bf16[48,6144]{1,0:T(8,128)(2,1)} %copy-done.2, bf16[48,6144]{1,0:T(8,128)(2,1)} %copy-done.11, bf16[48,6144]{1,0:T(8,128)(2,1)} %copy-done.10, bf16[48,6144]{1,0:T(8,128)(2,1)} %copy-done.9, bf16[48,6144]{1,0:T(8,128)(2,1)} %copy-done.8, ...), custom_call_target="tpu_custom_call" | custom-call | flops 3623878656 | bytes 12582912 | tf_op jit(solution)/shard_map/expert/pallas_call | solution.py:178
  106.8 4.4 %all-to-all-start.1 = ((bf16[32,8,3072]{2,1,0:T(8,128)(2,1)}), bf16[32,8,3072]{2,1,0:T(8,128)(2,1)S(1)}, u32[]{:S(2)}, u32[]{:S(2)}) async-start(bf16[32,8,3072]{2,1,0:T(8,128)(2,1)} %bitcast.14), calls=%async_computation.1 | async-start | bytes 3145728 | tf_op jit(solution)/shard_map/all_to_all | solution.py:406
  111.3 4.8 %collective-permute-start.17 = (bf16[128,512]{1,0:T(8,128)(2,1)S(1)}, bf16[128,512]{1,0:T(8,128)(2,1)S(1)}, u32[]{:S(2)}, u32[]{:S(2)}) collective-permute-start(bf16[128,512]{1,0:T(8,128)(2,1)S(1)} %pad_maximum_fusion.2), channel_id=1, source_target_pairs={{0,64},{32,96},{64,0},{96,32},{128,192},{160,224},{192,128},{224,1... | collective-permute-start | bytes 393224 | tf_op jit(solution)/shard_map/ppermute | solution.py:344
  116.1 2.7 %collective-permute-start.16 = (bf16[128,512]{1,0:T(8,128)(2,1)S(1)}, bf16[128,512]{1,0:T(8,128)(2,1)S(1)}, u32[]{:S(2)}, u32[]{:S(2)}) collective-permute-start(bf16[128,512]{1,0:T(8,128)(2,1)S(1)} %pad_maximum_fusion.2), channel_id=1, source_target_pairs={{0,96},{32,0},{64,32},{96,64},{128,224},{160,128},{192,160},{224,1... | collective-permute-start | bytes 393224 | tf_op jit(solution)/shard_map/ppermute | solution.py:344
  118.8 2.6 %collective-permute-start.15 = (bf16[128,512]{1,0:T(8,128)(2,1)S(1)}, bf16[128,512]{1,0:T(8,128)(2,1)S(1)}, u32[]{:S(2)}, u32[]{:S(2)}) collective-permute-start(bf16[128,512]{1,0:T(8,128)(2,1)S(1)} %pad_maximum_fusion.2), channel_id=1, source_target_pairs={{0,32},{32,64},{64,96},{96,0},{128,160},{160,192},{192,224},{224,1... | collective-permute-start | bytes 393224 | tf_op jit(solution)/shard_map/ppermute | solution.py:344
  122.4 3.6 %collective-permute-done.15 = bf16[128,512]{1,0:T(8,128)(2,1)S(1)} collective-permute-done((bf16[128,512]{1,0:T(8,128)(2,1)S(1)}, bf16[128,512]{1,0:T(8,128)(2,1)S(1)}, u32[]{:S(2)}, u32[]{:S(2)}) %collective-permute-start.15) | collective-permute-done | bytes 131104 | tf_op jit(solution)/shard_map/ppermute | solution.py:344
  126.0 4.4 %collective-permute-start.19 = (bf16[512,512]{1,0:T(8,128)(2,1)S(1)}, bf16[512,512]{1,0:T(8,128)(2,1)S(1)}, u32[]{:S(2)}, u32[]{:S(2)}) collective-permute-start(bf16[512,512]{1,0:T(8,128)(2,1)S(1)} %pad_maximum_fusion.1.refs_0_.refs_5_), channel_id=1, source_target_pairs={{0,384},{32,416},{64,448},{96,480},{128,0},{160,32},{192,64},{224,... | collective-permute-start | bytes 1572872 | tf_op jit(solution)/shard_map/ppermute | solution.py:337
  132.4 7.5 %collective-permute-done.19.refs_2_.refs_7_ = bf16[512,512]{1,0:T(8,128)(2,1)S(1)} collective-permute-done((bf16[512,512]{1,0:T(8,128)(2,1)S(1)}, bf16[512,512]{1,0:T(8,128)(2,1)S(1)}, u32[]{:S(2)}, u32[]{:S(2)}) %collective-permute-start.19) | collective-permute-done | bytes 524320 | tf_op jit(solution)/shard_map/ppermute | solution.py:337
  140.6 5.3 %collective-permute-start.21 = (bf16[256,512]{1,0:T(8,128)(2,1)}, bf16[256,512]{1,0:T(8,128)(2,1)S(1)}, u32[]{:S(2)}, u32[]{:S(2)}) collective-permute-start(bf16[256,512]{1,0:T(8,128)(2,1)} %slice.9), channel_id=1, source_target_pairs={{0,384},{32,416},{64,448},{96,480},{128,0},{160,32},{192,64},{224,... | collective-permute-start | bytes 786440 | tf_op jit(solution)/shard_map/ppermute | solution.py:337
  146.6 2.1 %collective-permute-start.20 = (bf16[256,512]{1,0:T(8,128)(2,1)}, bf16[256,512]{1,0:T(8,128)(2,1)}, u32[]{:S(2)}, u32[]{:S(2)}) collective-permute-start(bf16[256,512]{1,0:T(8,128)(2,1)} %slice.8), channel_id=1, source_target_pairs={{0,128},{32,160},{64,192},{96,224},{128,256},{160,288},{192,320},{... | collective-permute-start | bytes 786440 | tf_op jit(solution)/shard_map/ppermute | solution.py:337
  149.5 5.9 %collective-permute-done.20.refs_3_.refs_8_ = bf16[256,512]{1,0:T(8,128)(2,1)} collective-permute-done((bf16[256,512]{1,0:T(8,128)(2,1)}, bf16[256,512]{1,0:T(8,128)(2,1)}, u32[]{:S(2)}, u32[]{:S(2)}) %collective-permute-start.20) | collective-permute-done | bytes 262176 | tf_op jit(solution)/shard_map/ppermute | solution.py:337
  156.6 16.0 %attention.1 = bf16[128,4096]{1,0:T(8,128)(2,1)} custom-call(s32[1]{0:T(128)} %bitcast.block_ref, bf16[128,4096]{1,0:T(8,128)(2,1)S(1)} %bitcast.24, bf16[512,512]{1,0:T(8,128)(2,1)S(1)} %pad_maximum_fusion.1.refs_0_.refs_5_, bf16[512,512]{1,0:T(8,128)(2,1)S(1)} %collective-permute-done.18.refs_1_.refs_6_, ...), custom_call_target="tpu_custom_call" | custom-call | flops 4294967296 | bytes 4194304 | tf_op jit(solution)/shard_map/attention/pallas_call | solution.py:308
  172.7 16.5 %all-to-all-done.1 = bf16[32,8,3072]{2,1,0:T(8,128)(2,1)S(1)} async-done(((bf16[32,8,3072]{2,1,0:T(8,128)(2,1)}), bf16[32,8,3072]{2,1,0:T(8,128)(2,1)S(1)}, u32[]{:S(2)}, u32[]{:S(2)}) %all-to-all-start.1) | async-done | bytes 1572896 | tf_op jit(solution)/shard_map/all_to_all | solution.py:406
  (69 shorter events, 17.9 us)
Async XLA Ops:
  3.8 94.7 %all-to-all-start = ((bf16[32,8,3072]{2,1,0:T(8,128)(2,1)}), bf16[32,8,3072]{2,1,0:T(8,128)(2,1)S(1)}, u32[]{:S(2)}, u32[]{:S(2)}) async-start(bf16[32,8,3072]{2,1,0:T(8,128)(2,1)} %bitcast.6), calls=%async_computation | async-start | bytes 3145728 | tf_op jit(solution)/shard_map/all_to_all | solution.py:406
  20.8 77.7 %copy-start.2 = (bf16[48,6144]{1,0:T(8,128)(2,1)}, bf16[48,6144]{1,0:T(8,128)(2,1)S(1)}, u32[]{:S(2)}) copy-start(bf16[48,6144]{1,0:T(8,128)(2,1)S(1)} %pad_maximum_fusion.refs_0_) | copy-start | bytes 1769476
  20.8 12.9 %collective-permute-start.3 = (bf16[48,6144]{1,0:T(8,128)(2,1)S(1)}, bf16[48,6144]{1,0:T(8,128)(2,1)S(1)}, u32[]{:S(2)}, u32[]{:S(2)}) collective-permute-start(bf16[48,6144]{1,0:T(8,128)(2,1)S(1)} %pad_maximum_fusion.refs_0_), channel_id=1, source_target_pairs={{0,384},{1,97},{2,386},{3,99},{4,388},{5,101},{6,390},{7,103},{8,3... | collective-permute-start | bytes 1769480 | tf_op jit(solution)/shard_map/ppermute | solution.py:367
  25.5 12.9 %collective-permute-start.2 = (bf16[48,6144]{1,0:T(8,128)(2,1)S(1)}, bf16[48,6144]{1,0:T(8,128)(2,1)S(1)}, u32[]{:S(2)}, u32[]{:S(2)}) collective-permute-start(bf16[48,6144]{1,0:T(8,128)(2,1)S(1)} %pad_maximum_fusion.refs_0_), channel_id=1, source_target_pairs={{0,128},{1,33},{2,130},{3,35},{4,132},{5,37},{6,134},{7,39},{8,136... | collective-permute-start | bytes 1769480 | tf_op jit(solution)/shard_map/ppermute | solution.py:367
  27.4 15.1 %collective-permute-start.1 = (bf16[48,6144]{1,0:T(8,128)(2,1)S(1)}, bf16[48,6144]{1,0:T(8,128)(2,1)S(1)}, u32[]{:S(2)}, u32[]{:S(2)}) collective-permute-start(bf16[48,6144]{1,0:T(8,128)(2,1)S(1)} %pad_maximum_fusion.refs_0_), channel_id=1, source_target_pairs={{0,96},{1,385},{2,98},{3,387},{4,100},{5,389},{6,102},{7,391},{8,1... | collective-permute-start | bytes 1769480 | tf_op jit(solution)/shard_map/ppermute | solution.py:367
  31.8 13.6 %collective-permute-start = (bf16[48,6144]{1,0:T(8,128)(2,1)S(1)}, bf16[48,6144]{1,0:T(8,128)(2,1)S(1)}, u32[]{:S(2)}, u32[]{:S(2)}) collective-permute-start(bf16[48,6144]{1,0:T(8,128)(2,1)S(1)} %pad_maximum_fusion.refs_0_), channel_id=1, source_target_pairs={{0,32},{1,129},{2,34},{3,131},{4,36},{5,133},{6,38},{7,135},{8,40}... | collective-permute-start | bytes 1769480 | tf_op jit(solution)/shard_map/ppermute | solution.py:367
  33.7 64.8 %copy-start.8 = (bf16[48,6144]{1,0:T(8,128)(2,1)}, bf16[48,6144]{1,0:T(8,128)(2,1)S(1)}, u32[]{:S(2)}) copy-start(bf16[48,6144]{1,0:T(8,128)(2,1)S(1)} %collective-permute-done.3.refs_4_) | copy-start | bytes 1769476
  33.7 15.5 %collective-permute-start.5 = (bf16[48,6144]{1,0:T(8,128)(2,1)S(1)}, bf16[48,6144]{1,0:T(8,128)(2,1)S(1)}, u32[]{:S(2)}, u32[]{:S(2)}) collective-permute-start(bf16[48,6144]{1,0:T(8,128)(2,1)S(1)} %collective-permute-done.3.refs_4_), channel_id=1, source_target_pairs={{0,96},{1,385},{2,98},{3,387},{4,100},{5,389},{6,102},{7,391},{8,1... | collective-permute-start | bytes 1769480 | tf_op jit(solution)/shard_map/ppermute | solution.py:367
  38.3 42.8 %copy-start.9 = (bf16[48,6144]{1,0:T(8,128)(2,1)}, bf16[48,6144]{1,0:T(8,128)(2,1)S(1)}, u32[]{:S(2)}) copy-start(bf16[48,6144]{1,0:T(8,128)(2,1)S(1)} %collective-permute-done.2.refs_3_) | copy-start | bytes 1769476
  38.3 16.0 %collective-permute-start.10 = (bf16[48,6144]{1,0:T(8,128)(2,1)S(1)}, bf16[48,6144]{1,0:T(8,128)(2,1)S(1)}, u32[]{:S(2)}, u32[]{:S(2)}) collective-permute-start(bf16[48,6144]{1,0:T(8,128)(2,1)S(1)} %collective-permute-done.2.refs_3_), channel_id=1, source_target_pairs={{0,128},{1,33},{2,130},{3,35},{4,132},{5,37},{6,134},{7,39},{8,136... | collective-permute-start | bytes 1769480 | tf_op jit(solution)/shard_map/ppermute | solution.py:367
  40.3 18.5 %collective-permute-start.4 = (bf16[48,6144]{1,0:T(8,128)(2,1)S(1)}, bf16[48,6144]{1,0:T(8,128)(2,1)S(1)}, u32[]{:S(2)}, u32[]{:S(2)}) collective-permute-start(bf16[48,6144]{1,0:T(8,128)(2,1)S(1)} %collective-permute-done.2.refs_3_), channel_id=1, source_target_pairs={{0,32},{1,129},{2,34},{3,131},{4,36},{5,133},{6,38},{7,135},{8,40}... | collective-permute-start | bytes 1769480 | tf_op jit(solution)/shard_map/ppermute | solution.py:367
  42.5 38.6 %copy-start.10 = (bf16[48,6144]{1,0:T(8,128)(2,1)}, bf16[48,6144]{1,0:T(8,128)(2,1)S(1)}, u32[]{:S(2)}) copy-start(bf16[48,6144]{1,0:T(8,128)(2,1)S(1)} %collective-permute-done.1.refs_2_) | copy-start | bytes 1769476
  42.5 21.6 %collective-permute-start.6 = (bf16[48,6144]{1,0:T(8,128)(2,1)S(1)}, bf16[48,6144]{1,0:T(8,128)(2,1)S(1)}, u32[]{:S(2)}, u32[]{:S(2)}) collective-permute-start(bf16[48,6144]{1,0:T(8,128)(2,1)S(1)} %collective-permute-done.1.refs_2_), channel_id=1, source_target_pairs={{0,128},{1,33},{2,130},{3,35},{4,132},{5,37},{6,134},{7,39},{8,136... | collective-permute-start | bytes 1769480 | tf_op jit(solution)/shard_map/ppermute | solution.py:367
  45.4 35.7 %copy-start.11 = (bf16[48,6144]{1,0:T(8,128)(2,1)}, bf16[48,6144]{1,0:T(8,128)(2,1)S(1)}, u32[]{:S(2)}) copy-start(bf16[48,6144]{1,0:T(8,128)(2,1)S(1)} %collective-permute-done.refs_1_) | copy-start | bytes 1769476
  45.5 21.1 %collective-permute-start.7 = (bf16[48,6144]{1,0:T(8,128)(2,1)S(1)}, bf16[48,6144]{1,0:T(8,128)(2,1)S(1)}, u32[]{:S(2)}, u32[]{:S(2)}) collective-permute-start(bf16[48,6144]{1,0:T(8,128)(2,1)S(1)} %collective-permute-done.refs_1_), channel_id=1, source_target_pairs={{0,384},{1,97},{2,386},{3,99},{4,388},{5,101},{6,390},{7,103},{8,3... | collective-permute-start | bytes 1769480 | tf_op jit(solution)/shard_map/ppermute | solution.py:367
  49.3 31.8 %copy-start.12 = (bf16[48,6144]{1,0:T(8,128)(2,1)}, bf16[48,6144]{1,0:T(8,128)(2,1)S(1)}, u32[]{:S(2)}) copy-start(bf16[48,6144]{1,0:T(8,128)(2,1)S(1)} %collective-permute-done.5.refs_6_) | copy-start | bytes 1769476
  49.3 19.3 %collective-permute-start.11 = (bf16[48,6144]{1,0:T(8,128)(2,1)S(1)}, bf16[48,6144]{1,0:T(8,128)(2,1)S(1)}, u32[]{:S(2)}, u32[]{:S(2)}) collective-permute-start(bf16[48,6144]{1,0:T(8,128)(2,1)S(1)} %collective-permute-done.5.refs_6_), channel_id=1, source_target_pairs={{0,384},{1,97},{2,386},{3,99},{4,388},{5,101},{6,390},{7,103},{8,3... | collective-permute-start | bytes 1769480 | tf_op jit(solution)/shard_map/ppermute | solution.py:367
  54.3 26.8 %copy-start.13 = (bf16[48,6144]{1,0:T(8,128)(2,1)}, bf16[48,6144]{1,0:T(8,128)(2,1)S(1)}, u32[]{:S(2)}) copy-start(bf16[48,6144]{1,0:T(8,128)(2,1)S(1)} %collective-permute-done.10.refs_11_) | copy-start | bytes 1769476
  54.3 19.9 %collective-permute-start.8 = (bf16[48,6144]{1,0:T(8,128)(2,1)S(1)}, bf16[48,6144]{1,0:T(8,128)(2,1)S(1)}, u32[]{:S(2)}, u32[]{:S(2)}) collective-permute-start(bf16[48,6144]{1,0:T(8,128)(2,1)S(1)} %collective-permute-done.refs_1_), channel_id=1, source_target_pairs={{0,32},{1,129},{2,34},{3,131},{4,36},{5,133},{6,38},{7,135},{8,40}... | collective-permute-start | bytes 1769480 | tf_op jit(solution)/shard_map/ppermute | solution.py:367
  58.7 15.5 %collective-permute-start.9 = (bf16[48,6144]{1,0:T(8,128)(2,1)S(1)}, bf16[48,6144]{1,0:T(8,128)(2,1)S(1)}, u32[]{:S(2)}, u32[]{:S(2)}) collective-permute-start(bf16[48,6144]{1,0:T(8,128)(2,1)S(1)} %collective-permute-done.5.refs_6_), channel_id=1, source_target_pairs={{0,96},{1,385},{2,98},{3,387},{4,100},{5,389},{6,102},{7,391},{8,1... | collective-permute-start | bytes 1769480 | tf_op jit(solution)/shard_map/ppermute | solution.py:367
  64.1 13.7 %collective-permute-start.12 = (bf16[48,6144]{1,0:T(8,128)(2,1)S(1)}, bf16[48,6144]{1,0:T(8,128)(2,1)S(1)}, u32[]{:S(2)}, u32[]{:S(2)}) collective-permute-start(bf16[48,6144]{1,0:T(8,128)(2,1)S(1)} %collective-permute-done.4.refs_5_), channel_id=1, source_target_pairs={{0,32},{1,129},{2,34},{3,131},{4,36},{5,133},{6,38},{7,135},{8,40}... | collective-permute-start | bytes 1769480 | tf_op jit(solution)/shard_map/ppermute | solution.py:367
  66.6 14.5 %collective-permute-start.14 = (bf16[48,6144]{1,0:T(8,128)(2,1)S(1)}, bf16[48,6144]{1,0:T(8,128)(2,1)S(1)}, u32[]{:S(2)}, u32[]{:S(2)}) collective-permute-start(bf16[48,6144]{1,0:T(8,128)(2,1)S(1)} %collective-permute-done.7.refs_8_), channel_id=1, source_target_pairs={{0,384},{1,97},{2,386},{3,99},{4,388},{5,101},{6,390},{7,103},{8,3... | collective-permute-start | bytes 1769480 | tf_op jit(solution)/shard_map/ppermute | solution.py:367
  68.6 14.6 %collective-permute-start.13 = (bf16[48,6144]{1,0:T(8,128)(2,1)S(1)}, bf16[48,6144]{1,0:T(8,128)(2,1)}, u32[]{:S(2)}, u32[]{:S(2)}) collective-permute-start(bf16[48,6144]{1,0:T(8,128)(2,1)S(1)} %collective-permute-done.11.refs_12_), channel_id=1, source_target_pairs={{0,96},{1,385},{2,98},{3,387},{4,100},{5,389},{6,102},{7,391},{8,1... | collective-permute-start | bytes 1769480 | tf_op jit(solution)/shard_map/ppermute | solution.py:367
  106.8 82.4 %all-to-all-start.1 = ((bf16[32,8,3072]{2,1,0:T(8,128)(2,1)}), bf16[32,8,3072]{2,1,0:T(8,128)(2,1)S(1)}, u32[]{:S(2)}, u32[]{:S(2)}) async-start(bf16[32,8,3072]{2,1,0:T(8,128)(2,1)} %bitcast.14), calls=%async_computation.1 | async-start | bytes 3145728 | tf_op jit(solution)/shard_map/all_to_all | solution.py:406
  111.3 10.1 %collective-permute-start.17 = (bf16[128,512]{1,0:T(8,128)(2,1)S(1)}, bf16[128,512]{1,0:T(8,128)(2,1)S(1)}, u32[]{:S(2)}, u32[]{:S(2)}) collective-permute-start(bf16[128,512]{1,0:T(8,128)(2,1)S(1)} %pad_maximum_fusion.2), channel_id=1, source_target_pairs={{0,64},{32,96},{64,0},{96,32},{128,192},{160,224},{192,128},{224,1... | collective-permute-start | bytes 393224 | tf_op jit(solution)/shard_map/ppermute | solution.py:344
  116.1 6.3 %collective-permute-start.16 = (bf16[128,512]{1,0:T(8,128)(2,1)S(1)}, bf16[128,512]{1,0:T(8,128)(2,1)S(1)}, u32[]{:S(2)}, u32[]{:S(2)}) collective-permute-start(bf16[128,512]{1,0:T(8,128)(2,1)S(1)} %pad_maximum_fusion.2), channel_id=1, source_target_pairs={{0,96},{32,0},{64,32},{96,64},{128,224},{160,128},{192,160},{224,1... | collective-permute-start | bytes 393224 | tf_op jit(solution)/shard_map/ppermute | solution.py:344
  118.8 7.2 %collective-permute-start.15 = (bf16[128,512]{1,0:T(8,128)(2,1)S(1)}, bf16[128,512]{1,0:T(8,128)(2,1)S(1)}, u32[]{:S(2)}, u32[]{:S(2)}) collective-permute-start(bf16[128,512]{1,0:T(8,128)(2,1)S(1)} %pad_maximum_fusion.2), channel_id=1, source_target_pairs={{0,32},{32,64},{64,96},{96,0},{128,160},{160,192},{192,224},{224,1... | collective-permute-start | bytes 393224 | tf_op jit(solution)/shard_map/ppermute | solution.py:344
  126.0 13.8 %collective-permute-start.19 = (bf16[512,512]{1,0:T(8,128)(2,1)S(1)}, bf16[512,512]{1,0:T(8,128)(2,1)S(1)}, u32[]{:S(2)}, u32[]{:S(2)}) collective-permute-start(bf16[512,512]{1,0:T(8,128)(2,1)S(1)} %pad_maximum_fusion.1.refs_0_.refs_5_), channel_id=1, source_target_pairs={{0,384},{32,416},{64,448},{96,480},{128,0},{160,32},{192,64},{224,... | collective-permute-start | bytes 1572872 | tf_op jit(solution)/shard_map/ppermute | solution.py:337
  130.4 15.4 %collective-permute-start.18 = (bf16[512,512]{1,0:T(8,128)(2,1)S(1)}, bf16[512,512]{1,0:T(8,128)(2,1)S(1)}, u32[]{:S(2)}, u32[]{:S(2)}) collective-permute-start(bf16[512,512]{1,0:T(8,128)(2,1)S(1)} %pad_maximum_fusion.1.refs_0_.refs_5_), channel_id=1, source_target_pairs={{0,128},{32,160},{64,192},{96,224},{128,256},{160,288},{192,320},{... | collective-permute-start | bytes 1572872 | tf_op jit(solution)/shard_map/ppermute | solution.py:337
  140.6 8.9 %collective-permute-start.21 = (bf16[256,512]{1,0:T(8,128)(2,1)}, bf16[256,512]{1,0:T(8,128)(2,1)S(1)}, u32[]{:S(2)}, u32[]{:S(2)}) collective-permute-start(bf16[256,512]{1,0:T(8,128)(2,1)} %slice.9), channel_id=1, source_target_pairs={{0,384},{32,416},{64,448},{96,480},{128,0},{160,32},{192,64},{224,... | collective-permute-start | bytes 786440 | tf_op jit(solution)/shard_map/ppermute | solution.py:337
  146.6 8.8 %collective-permute-start.20 = (bf16[256,512]{1,0:T(8,128)(2,1)}, bf16[256,512]{1,0:T(8,128)(2,1)}, u32[]{:S(2)}, u32[]{:S(2)}) collective-permute-start(bf16[256,512]{1,0:T(8,128)(2,1)} %slice.8), channel_id=1, source_target_pairs={{0,128},{32,160},{64,192},{96,224},{128,256},{160,288},{192,320},{... | collective-permute-start | bytes 786440 | tf_op jit(solution)/shard_map/ppermute | solution.py:337
  156.6 32.6 %copy-start = (f32[1,128,2]{1,2,0:T(2,128)S(1)}, f32[1,128,2]{1,2,0:T(2,128)}, u32[]{:S(2)}) copy-start(f32[1,128,2]{1,2,0:T(2,128)} %param.15) | copy-start | bytes 3076
  (14 other events, 145.7 us)

commit v5 on v4

--- a/solution.py
+++ b/solution.py
@@ -354,22 +354,9 @@
     return jnp.concatenate([rows, shift(rows, 1), shift(rows, -1), shift(rows, 2)], axis=0)
 
 
-def shift_split(rows, phase, step):
-    cores = lax.axis_size("ep")
-    pairs = []
-    for x in range(RING):
-        for y in range(RING):
-            for ep in range(cores):
-                along_y = (phase + ep) % 2 == 0
-                to_x = x if along_y else (x + step) % RING
-                to_y = (y + step) % RING if along_y else y
-                pairs.append(((x * RING + y) * cores + ep, (to_x * RING + to_y) * cores + ep))
-    return lax.ppermute(rows, ("ctx", "ep"), pairs)
-
-
 def gather_blocks(own):
     def along(direction, rows, step):
-        return shift_split(rows, direction, step)
+        return (shift_x, shift_y)[direction](rows, step)
 
     near = {
         (-1, 0): along(0, own, 1),

time: 192 us -> 197 us (1.026)
  starting transfers between devices: 91.5 us -> 101 us
  waiting for transfers between devices: 65.4 us -> 61.3 us
    ppermute x15 -> x0, starting transfers between devices: 46.4 us -> none  [shift_split(): return lax.ppermute(rows, ('ctx', 'ep'), pairs)]
    ppermute x4 -> x12, starting transfers between devices: 13.7 us -> 42.7 us  [shift_x(): return lax.ppermute(rows, 'ctx', pairs)]
    ppermute x3 -> x10, starting transfers between devices: 10.1 us -> 31.4 us  [shift_y(): return lax.ppermute(rows, 'ctx', pairs)]
    ppermute x15 -> x0, waiting for transfers between devices: 14.8 us -> none  [shift_split(): return lax.ppermute(rows, ('ctx', 'ep'), pairs)]
    ppermute x3 -> x10, waiting for transfers between devices: 4.6 us -> 16 us  [shift_y(): return lax.ppermute(rows, 'ctx', pairs)]
    all_to_all x2, waiting for transfers between devices: 31.9 us -> 21 us  [exchange(): lax.all_to_all(rows.reshape(experts, WHOLE, rows.shape[1]), 'ep', split_a...]
    ppermute x4 -> x12, waiting for transfers between devices: 14.2 us -> 24.3 us  [shift_x(): return lax.ppermute(rows, 'ctx', pairs)]
    all_to_all x2, starting transfers between devices: 21.2 us -> 26.5 us  [exchange(): lax.all_to_all(rows.reshape(experts, WHOLE, rows.shape[1]), 'ep', split_a...]
  transfers between devices with their start and end apart: 24 -> 24, of which waited for: 13 -> 14; matrix products, arithmetic and copies ran while one was open for 1% -> 1% of each run, Pallas kernels for 8% -> 8%
where the time goes in v5:
time: 197 us; the launch traced here: 196 us
  starting transfers between devices  101 us (51%)
  waiting for transfers between devices  61.3 us (31%)
  Pallas kernels  29.2 us (15%)
  local copies, waits for them, and re-layouts  3.79 us (2%)
    ppermute x12, starting transfers between devices, shift_x(): return lax.ppermute(rows, 'ctx', pairs)  42.7 us
    ppermute x10, starting transfers between devices, shift_y(): return lax.ppermute(rows, 'ctx', pairs)  31.4 us
    all_to_all x2, starting transfers between devices, exchange(): lax.all_to_all(rows.reshape(experts, WHOLE, rows.shape[1]), 'ep', split_a...  26.5 us
    ppermute x12, waiting for transfers between devices, shift_x(): return lax.ppermute(rows, 'ctx', pairs)  24.3 us
    all_to_all x2, waiting for transfers between devices, exchange(): lax.all_to_all(rows.reshape(experts, WHOLE, rows.shape[1]), 'ep', split_a...  21 us
    ppermute x10, waiting for transfers between devices, shift_y(): return lax.ppermute(rows, 'ctx', pairs)  16 us
    pallas_call x1, Pallas kernels, attention(): pl.pallas_call(attention_kernel, out_shape=jax.ShapeDtypeStruct(queries.s...  16 us
    pallas_call x1, Pallas kernels, expert(): pl.pallas_call(expert_kernel, out_shape=jax.ShapeDtypeStruct(rows.shape,...  8.27 us
  transfers between devices with their start and end apart: 24, of which 14 were waited for; matrix products, arithmetic and copies ran while one was open for 1% of the time, Pallas kernels for 8%

profile of v5, /device:TPU:1, one launch (start us, length us, event | category | flops | bytes accessed | tf_op | source)
XLA Modules:
  0.0 196.1 jit_solution(10901697803108689790)
XLA Ops:
  0.6 3.1 %dispatch.1 = (bf16[256,3072]{1,0:T(8,128)(2,1)}, s32[8,128]{1,0:T(8,128)S(1)}) custom-call(bf16[128,2048]{1,0:T(8,128)(2,1)} %bitcast.25, s32[2,128]{1,0:T(2,128)} %bitcast.35, f32[1,2048]{1,0:T(1,128)} %bitcast.34), custom_call_target="tpu_custom_call" | custom-call | tf_op jit(solution)/shard_map/dispatch/pallas_call | solution.py:89
  3.8 16.9 %all-to-all-start = ((bf16[32,8,3072]{2,1,0:T(8,128)(2,1)}), bf16[32,8,3072]{2,1,0:T(8,128)(2,1)S(1)}, u32[]{:S(2)}, u32[]{:S(2)}) async-start(bf16[32,8,3072]{2,1,0:T(8,128)(2,1)} %bitcast.6), calls=%async_computation | async-start | bytes 3145728 | tf_op jit(solution)/shard_map/all_to_all | solution.py:393
  20.8 4.7 %collective-permute-start.3 = (bf16[48,6144]{1,0:T(8,128)(2,1)S(1)}, bf16[48,6144]{1,0:T(8,128)(2,1)S(1)}, u32[]{:S(2)}, u32[]{:S(2)}) collective-permute-start(bf16[48,6144]{1,0:T(8,128)(2,1)S(1)} %pad_maximum_fusion.refs_0_), channel_id=1, source_target_pairs={{0,96},{32,0},{64,32},{96,64},{128,224},{160,128},{192,160},{224,1... | collective-permute-start | bytes 1769480 | tf_op jit(solution)/shard_map/ppermute | solution.py:344
  27.4 4.4 %collective-permute-start.1 = (bf16[48,6144]{1,0:T(8,128)(2,1)S(1)}, bf16[48,6144]{1,0:T(8,128)(2,1)S(1)}, u32[]{:S(2)}, u32[]{:S(2)}) collective-permute-start(bf16[48,6144]{1,0:T(8,128)(2,1)S(1)} %pad_maximum_fusion.refs_0_), channel_id=1, source_target_pairs={{0,384},{32,416},{64,448},{96,480},{128,0},{160,32},{192,64},{224,... | collective-permute-start | bytes 1769480 | tf_op jit(solution)/shard_map/ppermute | solution.py:337
  33.7 4.2 %collective-permute-done.3.refs_4_ = bf16[48,6144]{1,0:T(8,128)(2,1)S(1)} collective-permute-done((bf16[48,6144]{1,0:T(8,128)(2,1)S(1)}, bf16[48,6144]{1,0:T(8,128)(2,1)S(1)}, u32[]{:S(2)}, u32[]{:S(2)}) %collective-permute-start.3) | collective-permute-done | bytes 589856 | tf_op jit(solution)/shard_map/ppermute | solution.py:344
  37.9 4.4 %collective-permute-start.5 = (bf16[48,6144]{1,0:T(8,128)(2,1)S(1)}, bf16[48,6144]{1,0:T(8,128)(2,1)S(1)}, u32[]{:S(2)}, u32[]{:S(2)}) collective-permute-start(bf16[48,6144]{1,0:T(8,128)(2,1)S(1)} %collective-permute-done.3.refs_4_), channel_id=1, source_target_pairs={{0,384},{32,416},{64,448},{96,480},{128,0},{160,32},{192,64},{224,... | collective-permute-start | bytes 1769480 | tf_op jit(solution)/shard_map/ppermute | solution.py:337
  42.9 2.1 %collective-permute-start.10 = (bf16[48,6144]{1,0:T(8,128)(2,1)S(1)}, bf16[48,6144]{1,0:T(8,128)(2,1)S(1)}, u32[]{:S(2)}, u32[]{:S(2)}) collective-permute-start(bf16[48,6144]{1,0:T(8,128)(2,1)S(1)} %collective-permute-done.2.refs_3_), channel_id=1, source_target_pairs={{0,32},{32,64},{64,96},{96,0},{128,160},{160,192},{192,224},{224,1... | collective-permute-start | bytes 1769480 | tf_op jit(solution)/shard_map/ppermute | solution.py:344
  45.0 3.0 %collective-permute-start.4 = (bf16[48,6144]{1,0:T(8,128)(2,1)S(1)}, bf16[48,6144]{1,0:T(8,128)(2,1)S(1)}, u32[]{:S(2)}, u32[]{:S(2)}) collective-permute-start(bf16[48,6144]{1,0:T(8,128)(2,1)S(1)} %collective-permute-done.2.refs_3_), channel_id=1, source_target_pairs={{0,128},{32,160},{64,192},{96,224},{128,256},{160,288},{192,320},{... | collective-permute-start | bytes 1769480 | tf_op jit(solution)/shard_map/ppermute | solution.py:337
  48.0 2.2 %collective-permute-start.6 = (bf16[48,6144]{1,0:T(8,128)(2,1)S(1)}, bf16[48,6144]{1,0:T(8,128)(2,1)S(1)}, u32[]{:S(2)}, u32[]{:S(2)}) collective-permute-start(bf16[48,6144]{1,0:T(8,128)(2,1)S(1)} %collective-permute-done.1.refs_2_), channel_id=1, source_target_pairs={{0,32},{32,64},{64,96},{96,0},{128,160},{160,192},{192,224},{224,1... | collective-permute-start | bytes 1769480 | tf_op jit(solution)/shard_map/ppermute | solution.py:344
  50.2 4.3 %collective-permute-start.7 = (bf16[48,6144]{1,0:T(8,128)(2,1)S(1)}, bf16[48,6144]{1,0:T(8,128)(2,1)S(1)}, u32[]{:S(2)}, u32[]{:S(2)}) collective-permute-start(bf16[48,6144]{1,0:T(8,128)(2,1)S(1)} %collective-permute-done.refs_1_), channel_id=1, source_target_pairs={{0,96},{32,0},{64,32},{96,64},{128,224},{160,128},{192,160},{224,1... | collective-permute-start | bytes 1769480 | tf_op jit(solution)/shard_map/ppermute | solution.py:344
  54.5 2.0 %collective-permute-done.5.refs_6_ = bf16[48,6144]{1,0:T(8,128)(2,1)S(1)} collective-permute-done((bf16[48,6144]{1,0:T(8,128)(2,1)S(1)}, bf16[48,6144]{1,0:T(8,128)(2,1)S(1)}, u32[]{:S(2)}, u32[]{:S(2)}) %collective-permute-start.5) | collective-permute-done | bytes 589856 | tf_op jit(solution)/shard_map/ppermute | solution.py:337
  56.6 4.2 %collective-permute-start.11 = (bf16[48,6144]{1,0:T(8,128)(2,1)S(1)}, bf16[48,6144]{1,0:T(8,128)(2,1)S(1)}, u32[]{:S(2)}, u32[]{:S(2)}) collective-permute-start(bf16[48,6144]{1,0:T(8,128)(2,1)S(1)} %collective-permute-done.5.refs_6_), channel_id=1, source_target_pairs={{0,96},{32,0},{64,32},{96,64},{128,224},{160,128},{192,160},{224,1... | collective-permute-start | bytes 1769480 | tf_op jit(solution)/shard_map/ppermute | solution.py:344
  60.9 2.8 %collective-permute-start.8 = (bf16[48,6144]{1,0:T(8,128)(2,1)S(1)}, bf16[48,6144]{1,0:T(8,128)(2,1)S(1)}, u32[]{:S(2)}, u32[]{:S(2)}) collective-permute-start(bf16[48,6144]{1,0:T(8,128)(2,1)S(1)} %collective-permute-done.refs_1_), channel_id=1, source_target_pairs={{0,128},{32,160},{64,192},{96,224},{128,256},{160,288},{192,320},{... | collective-permute-start | bytes 1769480 | tf_op jit(solution)/shard_map/ppermute | solution.py:337
  63.7 4.4 %collective-permute-start.9 = (bf16[48,6144]{1,0:T(8,128)(2,1)S(1)}, bf16[48,6144]{1,0:T(8,128)(2,1)S(1)}, u32[]{:S(2)}, u32[]{:S(2)}) collective-permute-start(bf16[48,6144]{1,0:T(8,128)(2,1)S(1)} %collective-permute-done.5.refs_6_), channel_id=1, source_target_pairs={{0,384},{32,416},{64,448},{96,480},{128,0},{160,32},{192,64},{224,... | collective-permute-start | bytes 1769480 | tf_op jit(solution)/shard_map/ppermute | solution.py:337
  68.1 4.3 %collective-permute-done.6.refs_7_ = bf16[48,6144]{1,0:T(8,128)(2,1)S(1)} collective-permute-done((bf16[48,6144]{1,0:T(8,128)(2,1)S(1)}, bf16[48,6144]{1,0:T(8,128)(2,1)S(1)}, u32[]{:S(2)}, u32[]{:S(2)}) %collective-permute-start.6) | collective-permute-done | bytes 589856 | tf_op jit(solution)/shard_map/ppermute | solution.py:344
  72.4 2.8 %collective-permute-start.12 = (bf16[48,6144]{1,0:T(8,128)(2,1)S(1)}, bf16[48,6144]{1,0:T(8,128)(2,1)S(1)}, u32[]{:S(2)}, u32[]{:S(2)}) collective-permute-start(bf16[48,6144]{1,0:T(8,128)(2,1)S(1)} %collective-permute-done.4.refs_5_), channel_id=1, source_target_pairs={{0,128},{32,160},{64,192},{96,224},{128,256},{160,288},{192,320},{... | collective-permute-start | bytes 1769480 | tf_op jit(solution)/shard_map/ppermute | solution.py:337
  75.3 2.4 %collective-permute-start.14 = (bf16[48,6144]{1,0:T(8,128)(2,1)S(1)}, bf16[48,6144]{1,0:T(8,128)(2,1)S(1)}, u32[]{:S(2)}, u32[]{:S(2)}) collective-permute-start(bf16[48,6144]{1,0:T(8,128)(2,1)S(1)} %collective-permute-done.7.refs_8_), channel_id=1, source_target_pairs={{0,96},{32,0},{64,32},{96,64},{128,224},{160,128},{192,160},{224,1... | collective-permute-start | bytes 1769480 | tf_op jit(solution)/shard_map/ppermute | solution.py:344
  78.7 4.3 %collective-permute-start.13 = (bf16[48,6144]{1,0:T(8,128)(2,1)S(1)}, bf16[48,6144]{1,0:T(8,128)(2,1)}, u32[]{:S(2)}, u32[]{:S(2)}) collective-permute-start(bf16[48,6144]{1,0:T(8,128)(2,1)S(1)} %collective-permute-done.11.refs_12_), channel_id=1, source_target_pairs={{0,384},{32,416},{64,448},{96,480},{128,0},{160,32},{192,64},{224,... | collective-permute-start | bytes 1769480 | tf_op jit(solution)/shard_map/ppermute | solution.py:337
  83.0 7.9 %collective-permute-done.12.refs_13_ = bf16[48,6144]{1,0:T(8,128)(2,1)S(1)} collective-permute-done((bf16[48,6144]{1,0:T(8,128)(2,1)S(1)}, bf16[48,6144]{1,0:T(8,128)(2,1)S(1)}, u32[]{:S(2)}, u32[]{:S(2)}) %collective-permute-start.12) | collective-permute-done | bytes 589856 | tf_op jit(solution)/shard_map/ppermute | solution.py:337
  92.6 5.9 %all-to-all-done = bf16[32,8,3072]{2,1,0:T(8,128)(2,1)S(1)} async-done(((bf16[32,8,3072]{2,1,0:T(8,128)(2,1)}), bf16[32,8,3072]{2,1,0:T(8,128)(2,1)S(1)}, u32[]{:S(2)}, u32[]{:S(2)}) %all-to-all-start) | async-done | bytes 1572896 | tf_op jit(solution)/shard_map/all_to_all | solution.py:393
  98.5 8.3 %expert.1 = bf16[256,3072]{1,0:T(8,128)(2,1)} custom-call(bf16[256,3072]{1,0:T(8,128)(2,1)S(1)} %bitcast.22, bf16[48,6144]{1,0:T(8,128)(2,1)} %copy-done.2, bf16[48,6144]{1,0:T(8,128)(2,1)} %copy-done.11, bf16[48,6144]{1,0:T(8,128)(2,1)} %copy-done.10, bf16[48,6144]{1,0:T(8,128)(2,1)} %copy-done.9, bf16[48,6144]{1,0:T(8,128)(2,1)} %copy-done.8, ...), custom_call_target="tpu_custom_call" | custom-call | flops 3623878656 | bytes 12582912 | tf_op jit(solution)/shard_map/expert/pallas_call | solution.py:178
  106.8 9.7 %all-to-all-start.1 = ((bf16[32,8,3072]{2,1,0:T(8,128)(2,1)}), bf16[32,8,3072]{2,1,0:T(8,128)(2,1)S(1)}, u32[]{:S(2)}, u32[]{:S(2)}) async-start(bf16[32,8,3072]{2,1,0:T(8,128)(2,1)} %bitcast.14), calls=%async_computation.1 | async-start | bytes 3145728 | tf_op jit(solution)/shard_map/all_to_all | solution.py:393
  116.6 4.3 %collective-permute-start.17 = (bf16[128,512]{1,0:T(8,128)(2,1)S(1)}, bf16[128,512]{1,0:T(8,128)(2,1)S(1)}, u32[]{:S(2)}, u32[]{:S(2)}) collective-permute-start(bf16[128,512]{1,0:T(8,128)(2,1)S(1)} %pad_maximum_fusion.2), channel_id=1, source_target_pairs={{0,64},{32,96},{64,0},{96,32},{128,192},{160,224},{192,128},{224,1... | collective-permute-start | bytes 393224 | tf_op jit(solution)/shard_map/ppermute | solution.py:344
  120.9 3.2 %collective-permute-start.16 = (bf16[128,512]{1,0:T(8,128)(2,1)S(1)}, bf16[128,512]{1,0:T(8,128)(2,1)S(1)}, u32[]{:S(2)}, u32[]{:S(2)}) collective-permute-start(bf16[128,512]{1,0:T(8,128)(2,1)S(1)} %pad_maximum_fusion.2), channel_id=1, source_target_pairs={{0,96},{32,0},{64,32},{96,64},{128,224},{160,128},{192,160},{224,1... | collective-permute-start | bytes 393224 | tf_op jit(solution)/shard_map/ppermute | solution.py:344
  127.4 4.1 %collective-permute-done.15 = bf16[128,512]{1,0:T(8,128)(2,1)S(1)} collective-permute-done((bf16[128,512]{1,0:T(8,128)(2,1)S(1)}, bf16[128,512]{1,0:T(8,128)(2,1)S(1)}, u32[]{:S(2)}, u32[]{:S(2)}) %collective-permute-start.15) | collective-permute-done | bytes 131104 | tf_op jit(solution)/shard_map/ppermute | solution.py:344
  131.5 5.4 %collective-permute-start.19 = (bf16[512,512]{1,0:T(8,128)(2,1)S(1)}, bf16[512,512]{1,0:T(8,128)(2,1)S(1)}, u32[]{:S(2)}, u32[]{:S(2)}) collective-permute-start(bf16[512,512]{1,0:T(8,128)(2,1)S(1)} %pad_maximum_fusion.1.refs_0_.refs_5_), channel_id=1, source_target_pairs={{0,384},{32,416},{64,448},{96,480},{128,0},{160,32},{192,64},{224,... | collective-permute-start | bytes 1572872 | tf_op jit(solution)/shard_map/ppermute | solution.py:337
  138.9 7.6 %collective-permute-done.19.refs_2_.refs_7_ = bf16[512,512]{1,0:T(8,128)(2,1)S(1)} collective-permute-done((bf16[512,512]{1,0:T(8,128)(2,1)S(1)}, bf16[512,512]{1,0:T(8,128)(2,1)S(1)}, u32[]{:S(2)}, u32[]{:S(2)}) %collective-permute-start.19) | collective-permute-done | bytes 524320 | tf_op jit(solution)/shard_map/ppermute | solution.py:337
  147.2 5.3 %collective-permute-start.21 = (bf16[256,512]{1,0:T(8,128)(2,1)}, bf16[256,512]{1,0:T(8,128)(2,1)S(1)}, u32[]{:S(2)}, u32[]{:S(2)}) collective-permute-start(bf16[256,512]{1,0:T(8,128)(2,1)} %slice.9), channel_id=1, source_target_pairs={{0,384},{32,416},{64,448},{96,480},{128,0},{160,32},{192,64},{224,... | collective-permute-start | bytes 786440 | tf_op jit(solution)/shard_map/ppermute | solution.py:337
  153.2 2.1 %collective-permute-start.20 = (bf16[256,512]{1,0:T(8,128)(2,1)}, bf16[256,512]{1,0:T(8,128)(2,1)}, u32[]{:S(2)}, u32[]{:S(2)}) collective-permute-start(bf16[256,512]{1,0:T(8,128)(2,1)} %slice.8), channel_id=1, source_target_pairs={{0,128},{32,160},{64,192},{96,224},{128,256},{160,288},{192,320},{... | collective-permute-start | bytes 786440 | tf_op jit(solution)/shard_map/ppermute | solution.py:337
  156.1 5.9 %collective-permute-done.20.refs_3_.refs_8_ = bf16[256,512]{1,0:T(8,128)(2,1)} collective-permute-done((bf16[256,512]{1,0:T(8,128)(2,1)}, bf16[256,512]{1,0:T(8,128)(2,1)}, u32[]{:S(2)}, u32[]{:S(2)}) %collective-permute-start.20) | collective-permute-done | bytes 262176 | tf_op jit(solution)/shard_map/ppermute | solution.py:337
  163.3 16.0 %attention.1 = bf16[128,4096]{1,0:T(8,128)(2,1)} custom-call(s32[1]{0:T(128)} %bitcast.block_ref, bf16[128,4096]{1,0:T(8,128)(2,1)S(1)} %bitcast.24, bf16[512,512]{1,0:T(8,128)(2,1)S(1)} %pad_maximum_fusion.1.refs_0_.refs_5_, bf16[512,512]{1,0:T(8,128)(2,1)S(1)} %collective-permute-done.18.refs_1_.refs_6_, ...), custom_call_target="tpu_custom_call" | custom-call | flops 4294967296 | bytes 4194304 | tf_op jit(solution)/shard_map/attention/pallas_call | solution.py:308
  179.3 15.0 %all-to-all-done.1 = bf16[32,8,3072]{2,1,0:T(8,128)(2,1)S(1)} async-done(((bf16[32,8,3072]{2,1,0:T(8,128)(2,1)}), bf16[32,8,3072]{2,1,0:T(8,128)(2,1)S(1)}, u32[]{:S(2)}, u32[]{:S(2)}) %all-to-all-start.1) | async-done | bytes 1572896 | tf_op jit(solution)/shard_map/all_to_all | solution.py:393
  (69 shorter events, 17.6 us)
Async XLA Ops:
  3.8 94.7 %all-to-all-start = ((bf16[32,8,3072]{2,1,0:T(8,128)(2,1)}), bf16[32,8,3072]{2,1,0:T(8,128)(2,1)S(1)}, u32[]{:S(2)}, u32[]{:S(2)}) async-start(bf16[32,8,3072]{2,1,0:T(8,128)(2,1)} %bitcast.6), calls=%async_computation | async-start | bytes 3145728 | tf_op jit(solution)/shard_map/all_to_all | solution.py:393
  20.8 77.7 %copy-start.2 = (bf16[48,6144]{1,0:T(8,128)(2,1)}, bf16[48,6144]{1,0:T(8,128)(2,1)S(1)}, u32[]{:S(2)}) copy-start(bf16[48,6144]{1,0:T(8,128)(2,1)S(1)} %pad_maximum_fusion.refs_0_) | copy-start | bytes 1769476
  20.8 17.1 %collective-permute-start.3 = (bf16[48,6144]{1,0:T(8,128)(2,1)S(1)}, bf16[48,6144]{1,0:T(8,128)(2,1)S(1)}, u32[]{:S(2)}, u32[]{:S(2)}) collective-permute-start(bf16[48,6144]{1,0:T(8,128)(2,1)S(1)} %pad_maximum_fusion.refs_0_), channel_id=1, source_target_pairs={{0,96},{32,0},{64,32},{96,64},{128,224},{160,128},{192,160},{224,1... | collective-permute-start | bytes 1769480 | tf_op jit(solution)/shard_map/ppermute | solution.py:344
  25.5 17.5 %collective-permute-start.2 = (bf16[48,6144]{1,0:T(8,128)(2,1)S(1)}, bf16[48,6144]{1,0:T(8,128)(2,1)S(1)}, u32[]{:S(2)}, u32[]{:S(2)}) collective-permute-start(bf16[48,6144]{1,0:T(8,128)(2,1)S(1)} %pad_maximum_fusion.refs_0_), channel_id=1, source_target_pairs={{0,32},{32,64},{64,96},{96,0},{128,160},{160,192},{192,224},{224,1... | collective-permute-start | bytes 1769480 | tf_op jit(solution)/shard_map/ppermute | solution.py:344
  27.4 20.6 %collective-permute-start.1 = (bf16[48,6144]{1,0:T(8,128)(2,1)S(1)}, bf16[48,6144]{1,0:T(8,128)(2,1)S(1)}, u32[]{:S(2)}, u32[]{:S(2)}) collective-permute-start(bf16[48,6144]{1,0:T(8,128)(2,1)S(1)} %pad_maximum_fusion.refs_0_), channel_id=1, source_target_pairs={{0,384},{32,416},{64,448},{96,480},{128,0},{160,32},{192,64},{224,... | collective-permute-start | bytes 1769480 | tf_op jit(solution)/shard_map/ppermute | solution.py:337
  31.8 18.4 %collective-permute-start = (bf16[48,6144]{1,0:T(8,128)(2,1)S(1)}, bf16[48,6144]{1,0:T(8,128)(2,1)S(1)}, u32[]{:S(2)}, u32[]{:S(2)}) collective-permute-start(bf16[48,6144]{1,0:T(8,128)(2,1)S(1)} %pad_maximum_fusion.refs_0_), channel_id=1, source_target_pairs={{0,128},{32,160},{64,192},{96,224},{128,256},{160,288},{192,320},{... | collective-permute-start | bytes 1769480 | tf_op jit(solution)/shard_map/ppermute | solution.py:337
  37.9 60.6 %copy-start.8 = (bf16[48,6144]{1,0:T(8,128)(2,1)}, bf16[48,6144]{1,0:T(8,128)(2,1)S(1)}, u32[]{:S(2)}) copy-start(bf16[48,6144]{1,0:T(8,128)(2,1)S(1)} %collective-permute-done.3.refs_4_) | copy-start | bytes 1769476
  37.9 18.6 %collective-permute-start.5 = (bf16[48,6144]{1,0:T(8,128)(2,1)S(1)}, bf16[48,6144]{1,0:T(8,128)(2,1)S(1)}, u32[]{:S(2)}, u32[]{:S(2)}) collective-permute-start(bf16[48,6144]{1,0:T(8,128)(2,1)S(1)} %collective-permute-done.3.refs_4_), channel_id=1, source_target_pairs={{0,384},{32,416},{64,448},{96,480},{128,0},{160,32},{192,64},{224,... | collective-permute-start | bytes 1769480 | tf_op jit(solution)/shard_map/ppermute | solution.py:337
  42.9 48.5 %copy-start.9 = (bf16[48,6144]{1,0:T(8,128)(2,1)}, bf16[48,6144]{1,0:T(8,128)(2,1)S(1)}, u32[]{:S(2)}) copy-start(bf16[48,6144]{1,0:T(8,128)(2,1)S(1)} %collective-permute-done.2.refs_3_) | copy-start | bytes 1769476
  42.9 17.9 %collective-permute-start.10 = (bf16[48,6144]{1,0:T(8,128)(2,1)S(1)}, bf16[48,6144]{1,0:T(8,128)(2,1)S(1)}, u32[]{:S(2)}, u32[]{:S(2)}) collective-permute-start(bf16[48,6144]{1,0:T(8,128)(2,1)S(1)} %collective-permute-done.2.refs_3_), channel_id=1, source_target_pairs={{0,32},{32,64},{64,96},{96,0},{128,160},{160,192},{192,224},{224,1... | collective-permute-start | bytes 1769480 | tf_op jit(solution)/shard_map/ppermute | solution.py:344
  45.0 18.7 %collective-permute-start.4 = (bf16[48,6144]{1,0:T(8,128)(2,1)S(1)}, bf16[48,6144]{1,0:T(8,128)(2,1)S(1)}, u32[]{:S(2)}, u32[]{:S(2)}) collective-permute-start(bf16[48,6144]{1,0:T(8,128)(2,1)S(1)} %collective-permute-done.2.refs_3_), channel_id=1, source_target_pairs={{0,128},{32,160},{64,192},{96,224},{128,256},{160,288},{192,320},{... | collective-permute-start | bytes 1769480 | tf_op jit(solution)/shard_map/ppermute | solution.py:337
  48.0 43.5 %copy-start.10 = (bf16[48,6144]{1,0:T(8,128)(2,1)}, bf16[48,6144]{1,0:T(8,128)(2,1)S(1)}, u32[]{:S(2)}) copy-start(bf16[48,6144]{1,0:T(8,128)(2,1)S(1)} %collective-permute-done.1.refs_2_) | copy-start | bytes 1769476
  48.0 24.4 %collective-permute-start.6 = (bf16[48,6144]{1,0:T(8,128)(2,1)S(1)}, bf16[48,6144]{1,0:T(8,128)(2,1)S(1)}, u32[]{:S(2)}, u32[]{:S(2)}) collective-permute-start(bf16[48,6144]{1,0:T(8,128)(2,1)S(1)} %collective-permute-done.1.refs_2_), channel_id=1, source_target_pairs={{0,32},{32,64},{64,96},{96,0},{128,160},{160,192},{192,224},{224,1... | collective-permute-start | bytes 1769480 | tf_op jit(solution)/shard_map/ppermute | solution.py:344
  50.2 41.3 %copy-start.11 = (bf16[48,6144]{1,0:T(8,128)(2,1)}, bf16[48,6144]{1,0:T(8,128)(2,1)S(1)}, u32[]{:S(2)}) copy-start(bf16[48,6144]{1,0:T(8,128)(2,1)S(1)} %collective-permute-done.refs_1_) | copy-start | bytes 1769476
  50.2 25.0 %collective-permute-start.7 = (bf16[48,6144]{1,0:T(8,128)(2,1)S(1)}, bf16[48,6144]{1,0:T(8,128)(2,1)S(1)}, u32[]{:S(2)}, u32[]{:S(2)}) collective-permute-start(bf16[48,6144]{1,0:T(8,128)(2,1)S(1)} %collective-permute-done.refs_1_), channel_id=1, source_target_pairs={{0,96},{32,0},{64,32},{96,64},{128,224},{160,128},{192,160},{224,1... | collective-permute-start | bytes 1769480 | tf_op jit(solution)/shard_map/ppermute | solution.py:344
  56.6 34.9 %copy-start.12 = (bf16[48,6144]{1,0:T(8,128)(2,1)}, bf16[48,6144]{1,0:T(8,128)(2,1)S(1)}, u32[]{:S(2)}) copy-start(bf16[48,6144]{1,0:T(8,128)(2,1)S(1)} %collective-permute-done.5.refs_6_) | copy-start | bytes 1769476
  56.6 22.1 %collective-permute-start.11 = (bf16[48,6144]{1,0:T(8,128)(2,1)S(1)}, bf16[48,6144]{1,0:T(8,128)(2,1)S(1)}, u32[]{:S(2)}, u32[]{:S(2)}) collective-permute-start(bf16[48,6144]{1,0:T(8,128)(2,1)S(1)} %collective-permute-done.5.refs_6_), channel_id=1, source_target_pairs={{0,96},{32,0},{64,32},{96,64},{128,224},{160,128},{192,160},{224,1... | collective-permute-start | bytes 1769480 | tf_op jit(solution)/shard_map/ppermute | solution.py:344
  60.8 30.7 %copy-start.13 = (bf16[48,6144]{1,0:T(8,128)(2,1)}, bf16[48,6144]{1,0:T(8,128)(2,1)S(1)}, u32[]{:S(2)}) copy-start(bf16[48,6144]{1,0:T(8,128)(2,1)S(1)} %collective-permute-done.10.refs_11_) | copy-start | bytes 1769476
  60.9 22.2 %collective-permute-start.8 = (bf16[48,6144]{1,0:T(8,128)(2,1)S(1)}, bf16[48,6144]{1,0:T(8,128)(2,1)S(1)}, u32[]{:S(2)}, u32[]{:S(2)}) collective-permute-start(bf16[48,6144]{1,0:T(8,128)(2,1)S(1)} %collective-permute-done.refs_1_), channel_id=1, source_target_pairs={{0,128},{32,160},{64,192},{96,224},{128,256},{160,288},{192,320},{... | collective-permute-start | bytes 1769480 | tf_op jit(solution)/shard_map/ppermute | solution.py:337
  63.7 19.3 %collective-permute-start.9 = (bf16[48,6144]{1,0:T(8,128)(2,1)S(1)}, bf16[48,6144]{1,0:T(8,128)(2,1)S(1)}, u32[]{:S(2)}, u32[]{:S(2)}) collective-permute-start(bf16[48,6144]{1,0:T(8,128)(2,1)S(1)} %collective-permute-done.5.refs_6_), channel_id=1, source_target_pairs={{0,384},{32,416},{64,448},{96,480},{128,0},{160,32},{192,64},{224,... | collective-permute-start | bytes 1769480 | tf_op jit(solution)/shard_map/ppermute | solution.py:337
  72.4 18.5 %collective-permute-start.12 = (bf16[48,6144]{1,0:T(8,128)(2,1)S(1)}, bf16[48,6144]{1,0:T(8,128)(2,1)S(1)}, u32[]{:S(2)}, u32[]{:S(2)}) collective-permute-start(bf16[48,6144]{1,0:T(8,128)(2,1)S(1)} %collective-permute-done.4.refs_5_), channel_id=1, source_target_pairs={{0,128},{32,160},{64,192},{96,224},{128,256},{160,288},{192,320},{... | collective-permute-start | bytes 1769480 | tf_op jit(solution)/shard_map/ppermute | solution.py:337
  75.3 16.2 %collective-permute-start.14 = (bf16[48,6144]{1,0:T(8,128)(2,1)S(1)}, bf16[48,6144]{1,0:T(8,128)(2,1)S(1)}, u32[]{:S(2)}, u32[]{:S(2)}) collective-permute-start(bf16[48,6144]{1,0:T(8,128)(2,1)S(1)} %collective-permute-done.7.refs_8_), channel_id=1, source_target_pairs={{0,96},{32,0},{64,32},{96,64},{128,224},{160,128},{192,160},{224,1... | collective-permute-start | bytes 1769480 | tf_op jit(solution)/shard_map/ppermute | solution.py:344
  78.7 13.9 %collective-permute-start.13 = (bf16[48,6144]{1,0:T(8,128)(2,1)S(1)}, bf16[48,6144]{1,0:T(8,128)(2,1)}, u32[]{:S(2)}, u32[]{:S(2)}) collective-permute-start(bf16[48,6144]{1,0:T(8,128)(2,1)S(1)} %collective-permute-done.11.refs_12_), channel_id=1, source_target_pairs={{0,384},{32,416},{64,448},{96,480},{128,0},{160,32},{192,64},{224,... | collective-permute-start | bytes 1769480 | tf_op jit(solution)/shard_map/ppermute | solution.py:337
  106.8 87.5 %all-to-all-start.1 = ((bf16[32,8,3072]{2,1,0:T(8,128)(2,1)}), bf16[32,8,3072]{2,1,0:T(8,128)(2,1)S(1)}, u32[]{:S(2)}, u32[]{:S(2)}) async-start(bf16[32,8,3072]{2,1,0:T(8,128)(2,1)} %bitcast.14), calls=%async_computation.1 | async-start | bytes 3145728 | tf_op jit(solution)/shard_map/all_to_all | solution.py:393
  116.6 9.7 %collective-permute-start.17 = (bf16[128,512]{1,0:T(8,128)(2,1)S(1)}, bf16[128,512]{1,0:T(8,128)(2,1)S(1)}, u32[]{:S(2)}, u32[]{:S(2)}) collective-permute-start(bf16[128,512]{1,0:T(8,128)(2,1)S(1)} %pad_maximum_fusion.2), channel_id=1, source_target_pairs={{0,64},{32,96},{64,0},{96,32},{128,192},{160,224},{192,128},{224,1... | collective-permute-start | bytes 393224 | tf_op jit(solution)/shard_map/ppermute | solution.py:344
  120.9 6.5 %collective-permute-start.16 = (bf16[128,512]{1,0:T(8,128)(2,1)S(1)}, bf16[128,512]{1,0:T(8,128)(2,1)S(1)}, u32[]{:S(2)}, u32[]{:S(2)}) collective-permute-start(bf16[128,512]{1,0:T(8,128)(2,1)S(1)} %pad_maximum_fusion.2), channel_id=1, source_target_pairs={{0,96},{32,0},{64,32},{96,64},{128,224},{160,128},{192,160},{224,1... | collective-permute-start | bytes 393224 | tf_op jit(solution)/shard_map/ppermute | solution.py:344
  124.2 7.3 %collective-permute-start.15 = (bf16[128,512]{1,0:T(8,128)(2,1)S(1)}, bf16[128,512]{1,0:T(8,128)(2,1)S(1)}, u32[]{:S(2)}, u32[]{:S(2)}) collective-permute-start(bf16[128,512]{1,0:T(8,128)(2,1)S(1)} %pad_maximum_fusion.2), channel_id=1, source_target_pairs={{0,32},{32,64},{64,96},{96,0},{128,160},{160,192},{192,224},{224,1... | collective-permute-start | bytes 393224 | tf_op jit(solution)/shard_map/ppermute | solution.py:344
  131.5 14.9 %collective-permute-start.19 = (bf16[512,512]{1,0:T(8,128)(2,1)S(1)}, bf16[512,512]{1,0:T(8,128)(2,1)S(1)}, u32[]{:S(2)}, u32[]{:S(2)}) collective-permute-start(bf16[512,512]{1,0:T(8,128)(2,1)S(1)} %pad_maximum_fusion.1.refs_0_.refs_5_), channel_id=1, source_target_pairs={{0,384},{32,416},{64,448},{96,480},{128,0},{160,32},{192,64},{224,... | collective-permute-start | bytes 1572872 | tf_op jit(solution)/shard_map/ppermute | solution.py:337
  137.0 15.5 %collective-permute-start.18 = (bf16[512,512]{1,0:T(8,128)(2,1)S(1)}, bf16[512,512]{1,0:T(8,128)(2,1)S(1)}, u32[]{:S(2)}, u32[]{:S(2)}) collective-permute-start(bf16[512,512]{1,0:T(8,128)(2,1)S(1)} %pad_maximum_fusion.1.refs_0_.refs_5_), channel_id=1, source_target_pairs={{0,128},{32,160},{64,192},{96,224},{128,256},{160,288},{192,320},{... | collective-permute-start | bytes 1572872 | tf_op jit(solution)/shard_map/ppermute | solution.py:337
  147.2 8.9 %collective-permute-start.21 = (bf16[256,512]{1,0:T(8,128)(2,1)}, bf16[256,512]{1,0:T(8,128)(2,1)S(1)}, u32[]{:S(2)}, u32[]{:S(2)}) collective-permute-start(bf16[256,512]{1,0:T(8,128)(2,1)} %slice.9), channel_id=1, source_target_pairs={{0,384},{32,416},{64,448},{96,480},{128,0},{160,32},{192,64},{224,... | collective-permute-start | bytes 786440 | tf_op jit(solution)/shard_map/ppermute | solution.py:337
  153.2 8.8 %collective-permute-start.20 = (bf16[256,512]{1,0:T(8,128)(2,1)}, bf16[256,512]{1,0:T(8,128)(2,1)}, u32[]{:S(2)}, u32[]{:S(2)}) collective-permute-start(bf16[256,512]{1,0:T(8,128)(2,1)} %slice.8), channel_id=1, source_target_pairs={{0,128},{32,160},{64,192},{96,224},{128,256},{160,288},{192,320},{... | collective-permute-start | bytes 786440 | tf_op jit(solution)/shard_map/ppermute | solution.py:337
  163.3 31.1 %copy-start = (f32[1,128,2]{1,2,0:T(2,128)S(1)}, f32[1,128,2]{1,2,0:T(2,128)}, u32[]{:S(2)}) copy-start(f32[1,128,2]{1,2,0:T(2,128)} %param.15) | copy-start | bytes 3076
  (14 other events, 166.1 us)
